TPU v7x, 32 devices: a whole 2x2x4 slice. The times are simulated.
32 devices in a mesh: batch: 8 (over y, x, core), ctx: 4 (over z).
Axes of the slice: x: 2, y: 2, z: 4, core: 2. Of those that a mesh axis runs over, the one named last changes fastest.
Arguments:
- tokens: bfloat16 [2, 8, 1024, 2048], P(None, 'batch', 'ctx'), may hold values from -6 to 6
- lengths: int32 [2, 8], P(None, 'batch'), may hold values from 256 to 1024, as said below
- expert_ids: int32 [2, 8, 1024, 8], P(None, 'batch', 'ctx'), may hold values from 0 to 15, all different within a row; in each aligned block of 256 rows (0 to 255, 256 to 511, ..., all dimensions but the last counted through in order) at most 160 rows name the same one
- route_levels: int32 [2, 8, 1024, 8], P(None, 'batch', 'ctx'), may hold values from 1 to 16
- w_query: bfloat16 [2048, 2048], P(('batch', 'ctx')), may hold values from -0.125 to 0.125
- w_key: bfloat16 [2048, 2048], P(('batch', 'ctx')), may hold values from -0.125 to 0.125
- w_value: bfloat16 [2048, 2048], P(('batch', 'ctx')), may hold values from -0.125 to 0.125
- w_out: bfloat16 [2048, 2048], P(('batch', 'ctx')), may hold values from -0.5 to 0.5
- attn_gain: bfloat16 [2048], P(('batch', 'ctx')), may hold values from 0.25 to 1.75
- query_gain: bfloat16 [2048], P(('batch', 'ctx')), may hold values from 0.25 to 1.75
- key_gain: bfloat16 [2048], P(('batch', 'ctx')), may hold values from 0.25 to 1.75
- ffn_gain: bfloat16 [2048], P(('batch', 'ctx')), may hold values from 0.25 to 1.75
- w_gate: bfloat16 [16, 2048, 1024], P('ctx', 'batch'), may hold values from -0.125 to 0.125
- w_up: bfloat16 [16, 2048, 1024], P('ctx', 'batch'), may hold values from -0.125 to 0.125
- w_down: bfloat16 [16, 1024, 2048], P('ctx', None, 'batch'), may hold values from -0.75 to 0.75
- cotangent: bfloat16 [2, 8, 1024, 2048], P(None, 'batch', 'ctx'), may hold values from -6 to 6
Outputs:
- out: bfloat16 [2, 8, 1024, 2048], P(None, 'batch', 'ctx')
- grad_tokens: float32 [2, 8, 1024, 2048], P(None, 'batch', 'ctx')
- grad_w_query: float32 [2048, 2048], P(('batch', 'ctx'))
- grad_w_key: float32 [2048, 2048], P(('batch', 'ctx'))
- grad_w_value: float32 [2048, 2048], P(('batch', 'ctx'))
- grad_w_out: float32 [2048, 2048], P(('batch', 'ctx'))
- grad_attn_gain: float32 [2048], P(('batch', 'ctx'))
- grad_query_gain: float32 [2048], P(('batch', 'ctx'))
- grad_key_gain: float32 [2048], P(('batch', 'ctx'))
- grad_ffn_gain: float32 [2048], P(('batch', 'ctx'))
- grad_w_gate: float32 [16, 2048, 1024], P('ctx', 'batch')
- grad_w_up: float32 [16, 2048, 1024], P('ctx', 'batch')
- grad_w_down: float32 [16, 1024, 2048], P('ctx', None, 'batch')
Inputs may be any that keep to these rules, and one draw needn't show every extreme that they name: The first lengths[m, s] slots of sequence s of micro-batch m are live, the others padding. `expert_ids`: each row names 8 different experts; in each aligned block of 256 rows (one sequence's slots on one index of ctx) no expert is named by more than 160 rows.
All inputs are finite; a program needn't handle non-finite values.
Results may differ from a plain program's by a relative error of at most 0.019.
Values may be sent and summed in bfloat16 or wider, within the bound.
No kernel may reach another device: no remote copies, remote signals or barrier semaphores. Data moves between devices by JAX's collectives and lax.ppermute only.
A program may use at most 512 MiB of HBM per device.

v0:
```python
import jax
import jax.numpy as jnp
from jax import lax
from jax.sharding import PartitionSpec as P

HEAD_DIM = 128


EPS = 1e-05
THETA = 10000.0
MASKED = -1e30


def norm_rows(values, gain):
    return values * lax.rsqrt(jnp.mean(values * values, axis=-1, keepdims=True) + EPS) * gain


def tables(positions, head_dim):
    half = head_dim // 2
    inverse = THETA ** (-(jnp.arange(half, dtype=jnp.float32) * 2.0) / head_dim)
    angle = positions.astype(jnp.float32)[:, None] * inverse[None, :]
    cosines = jnp.cos(angle)
    sines = jnp.sin(angle)
    return (jnp.concatenate([cosines, cosines], axis=-1), jnp.concatenate([sines, sines], axis=-1))


def rotate(projected, gain, cosines, sines):
    normed = norm_rows(projected, gain)
    count = normed.shape[0]
    head_dim = cosines.shape[-1]
    heads = normed.reshape(count, -1, head_dim)
    half = head_dim // 2
    turned = jnp.concatenate([-heads[..., half:], heads[..., :half]], axis=-1)
    return (heads * cosines[:, None, :] + turned * sines[:, None, :]).reshape(count, -1)


def swiglu(gate, upper):
    return gate * jax.nn.sigmoid(gate) * upper


def scores_of(query_heads, key_heads, allowed, scale):
    raw = (
        jnp.einsum("sqhd,skhd->shqk", query_heads, key_heads, preferred_element_type=jnp.float32)
        * scale
    )
    return jnp.where(allowed[:, None, :, :], raw, MASKED)


def unpack(fetched):
    attention, expert = fetched
    gains = tuple((gain.astype(jnp.float32) for gain in attention[4:]))
    return attention[:4] + gains + tuple(expert)


def add_trees(total, extra):
    return extra if total is None else jax.tree.map(jnp.add, total, extra)


def body(
    tokens,
    lengths,
    expert_ids,
    route_levels,
    w_query,
    w_key,
    w_value,
    w_out,
    attn_gain,
    query_gain,
    key_gain,
    ffn_gain,
    w_gate,
    w_up,
    w_down,
    cotangent,
):
    batches, sequences, block_rows, width = tokens.shape
    top_count = expert_ids.shape[-1]
    local_experts = w_gate.shape[0]
    ctx_size = lax.axis_size("ctx")
    experts = local_experts * ctx_size
    capacity = block_rows * top_count * 5 // (4 * experts)
    slots = sequences * capacity
    rows = sequences * block_rows
    span = block_rows * ctx_size
    heads = width // HEAD_DIM
    scale = HEAD_DIM ** (-0.5)
    local_pos = lax.axis_index("ctx") * block_rows + jnp.arange(block_rows, dtype=jnp.int32)
    key_pos = jnp.arange(span, dtype=jnp.int32)
    cosines, sines = tables(jnp.tile(local_pos, sequences), HEAD_DIM)
    causal = key_pos[None, :] <= local_pos[:, None]
    assign_ids = jnp.arange(rows * top_count, dtype=jnp.int32)
    seq_base = jnp.arange(sequences, dtype=jnp.int32)[:, None] * capacity
    expert_iota = jnp.arange(experts, dtype=jnp.int32)

    def fetch():
        attention = (
            lax.all_gather(w_query, ("batch", "ctx"), axis=0, tiled=True),
            lax.all_gather(w_key, ("batch", "ctx"), axis=0, tiled=True),
            lax.all_gather(w_value, ("batch", "ctx"), axis=0, tiled=True),
            lax.all_gather(w_out, ("batch", "ctx"), axis=0, tiled=True),
            lax.all_gather(attn_gain, ("batch", "ctx"), axis=0, tiled=True),
            lax.all_gather(query_gain, ("batch", "ctx"), axis=0, tiled=True),
            lax.all_gather(key_gain, ("batch", "ctx"), axis=0, tiled=True),
            lax.all_gather(ffn_gain, ("batch", "ctx"), axis=0, tiled=True),
        )
        expert = (
            lax.all_gather(w_gate, "batch", axis=1, tiled=True),
            lax.all_gather(w_up, "batch", axis=1, tiled=True),
            lax.all_gather(w_down, "batch", axis=2, tiled=True),
        )
        return (attention, expert)

    outputs = []
    input_grads = []
    attention_total = None
    expert_total = None
    for step in range(batches):
        forward_weights = fetch()
        (
            query_w,
            key_w,
            value_w,
            out_w,
            gain_attn,
            gain_query,
            gain_key,
            gain_ffn,
            gate_w,
            up_w,
            down_w,
        ) = unpack(forward_weights)
        length_now = lengths[step]
        live = (local_pos[None, :] < length_now[:, None]).reshape(rows)
        allowed = causal[None, :, :] & (key_pos[None, None, :] < length_now[:, None, None])
        inputs = tokens[step].reshape(rows, width).astype(jnp.float32)
        normed_in = norm_rows(inputs, gain_attn).astype(jnp.bfloat16)
        query_proj = jnp.dot(normed_in, query_w, preferred_element_type=jnp.float32)
        key_proj = jnp.dot(normed_in, key_w, preferred_element_type=jnp.float32)
        value_low = jnp.dot(normed_in, value_w, preferred_element_type=jnp.float32).astype(
            jnp.bfloat16
        )
        query_low = rotate(query_proj, gain_query, cosines, sines).astype(jnp.bfloat16)
        key_low = rotate(key_proj, gain_key, cosines, sines).astype(jnp.bfloat16)
        keys_all, values_all = (
            lax.all_gather(
                key_low.reshape(sequences, block_rows, width), "ctx", axis=1, tiled=True
            ),
            lax.all_gather(
                value_low.reshape(sequences, block_rows, width), "ctx", axis=1, tiled=True
            ),
        )
        query_heads = query_low.reshape(sequences, block_rows, heads, HEAD_DIM)
        key_heads = keys_all.reshape(sequences, span, heads, HEAD_DIM)
        value_heads = values_all.reshape(sequences, span, heads, HEAD_DIM)
        scores = scores_of(query_heads, key_heads, allowed, scale)
        peak = jnp.max(scores, axis=-1, keepdims=True)
        log_total = peak + jnp.log(jnp.sum(jnp.exp(scores - peak), axis=-1, keepdims=True))
        probs_low = jnp.exp(scores - log_total).astype(jnp.bfloat16)
        attended = (
            jnp.einsum(
                "shqk,skhd->sqhd", probs_low, value_heads, preferred_element_type=jnp.float32
            )
            .astype(jnp.bfloat16)
            .reshape(rows, width)
        )
        hidden = inputs + jnp.dot(attended, out_w, preferred_element_type=jnp.float32)
        normed_mid = norm_rows(hidden, gain_ffn).astype(jnp.bfloat16)
        chosen = expert_ids[step].reshape(sequences, block_rows * top_count)
        onehot = (chosen[:, :, None] == expert_iota[None, None, :]).astype(jnp.int32)
        rank = jnp.sum(jnp.cumsum(onehot, axis=1) * onehot, axis=-1) - 1
        place = (chosen * slots + seq_base + rank).reshape(-1)
        filled = jnp.full((experts * slots,), rows * top_count, jnp.int32).at[place].set(assign_ids)
        levels = route_levels[step].reshape(rows, top_count).astype(jnp.float32)
        mixing = levels / jnp.sum(levels, axis=-1, keepdims=True)
        padded = jnp.concatenate([normed_mid, jnp.zeros((1, width), jnp.bfloat16)], axis=0)
        outgoing = padded[filled // top_count].reshape(ctx_size, local_experts, slots, width)
        arrived = lax.all_to_all(outgoing, "ctx", split_axis=0, concat_axis=0, tiled=True)
        gate = jnp.einsum("cesd,edf->cesf", arrived, gate_w, preferred_element_type=jnp.float32)
        upper = jnp.einsum("cesd,edf->cesf", arrived, up_w, preferred_element_type=jnp.float32)
        active = swiglu(gate, upper).astype(jnp.bfloat16)
        produced = jnp.einsum(
            "cesf,efd->cesd", active, down_w, preferred_element_type=jnp.float32
        ).astype(jnp.bfloat16)
        returned = lax.all_to_all(produced, "ctx", split_axis=0, concat_axis=0, tiled=True).reshape(
            experts * slots, width
        )
        picked = returned[place].reshape(rows, top_count, width)
        mixture = jnp.sum(picked.astype(jnp.float32) * mixing[:, :, None], axis=1)
        final = hidden + mixture
        outputs.append(
            jnp.where(live[:, None], final, 0.0)
            .astype(jnp.bfloat16)
            .reshape(sequences, block_rows, width)
        )
        backward_weights = fetch()
        (
            query_w,
            key_w,
            value_w,
            out_w,
            gain_attn,
            gain_query,
            gain_key,
            gain_ffn,
            gate_w,
            up_w,
            down_w,
        ) = unpack(backward_weights)
        grad_final = jnp.where(
            live[:, None], cotangent[step].reshape(rows, width).astype(jnp.float32), 0.0
        )
        route_grad = (
            (mixing[:, :, None] * grad_final[:, None, :])
            .astype(jnp.bfloat16)
            .reshape(rows * top_count, width)
        )
        route_pad = jnp.concatenate([route_grad, jnp.zeros((1, width), jnp.bfloat16)], axis=0)
        grad_outgoing = route_pad[filled].reshape(ctx_size, local_experts, slots, width)
        grad_arrived = lax.all_to_all(grad_outgoing, "ctx", split_axis=0, concat_axis=0, tiled=True)
        grad_down_w = jnp.einsum(
            "cesf,cesd->efd", active, grad_arrived, preferred_element_type=jnp.float32
        )
        grad_active = jnp.einsum(
            "cesd,efd->cesf", grad_arrived, down_w, preferred_element_type=jnp.float32
        )
        unused, swiglu_back = jax.vjp(swiglu, gate, upper)
        grad_gate, grad_upper = swiglu_back(grad_active)
        grad_gate = grad_gate.astype(jnp.bfloat16)
        grad_upper = grad_upper.astype(jnp.bfloat16)
        grad_gate_w = jnp.einsum(
            "cesd,cesf->edf", arrived, grad_gate, preferred_element_type=jnp.float32
        )
        grad_up_w = jnp.einsum(
            "cesd,cesf->edf", arrived, grad_upper, preferred_element_type=jnp.float32
        )
        grad_sent = jnp.einsum(
            "cesf,edf->cesd", grad_gate, gate_w, preferred_element_type=jnp.float32
        )
        grad_sent = (
            grad_sent
            + jnp.einsum("cesf,edf->cesd", grad_upper, up_w, preferred_element_type=jnp.float32)
        ).astype(jnp.bfloat16)
        grad_returned = lax.all_to_all(
            grad_sent, "ctx", split_axis=0, concat_axis=0, tiled=True
        ).reshape(experts * slots, width)
        grad_mid = jnp.sum(
            grad_returned[place].reshape(rows, top_count, width).astype(jnp.float32), axis=1
        )
        unused, mid_back = jax.vjp(norm_rows, hidden, gain_ffn)
        grad_hidden_norm, grad_gain_ffn = mid_back(grad_mid)
        grad_hidden = grad_final + grad_hidden_norm
        grad_att_low = grad_hidden.astype(jnp.bfloat16)
        grad_out_w = jnp.einsum(
            "rd,re->de", attended, grad_att_low, preferred_element_type=jnp.float32
        )
        grad_attended = jnp.einsum(
            "re,de->rd", grad_att_low, out_w, preferred_element_type=jnp.float32
        ).astype(jnp.bfloat16)
        grad_heads = grad_attended.reshape(sequences, block_rows, heads, HEAD_DIM)
        scores = scores_of(query_heads, key_heads, allowed, scale)
        probs = jnp.exp(scores - log_total)
        probs_low = probs.astype(jnp.bfloat16)
        grad_probs = jnp.einsum(
            "sqhd,skhd->shqk", grad_heads, value_heads, preferred_element_type=jnp.float32
        )
        grad_scores = (
            probs * (grad_probs - jnp.sum(probs * grad_probs, axis=-1, keepdims=True))
        ).astype(jnp.bfloat16)
        grad_query = (
            jnp.einsum(
                "shqk,skhd->sqhd", grad_scores, key_heads, preferred_element_type=jnp.float32
            )
            * scale
        ).reshape(rows, width)
        count = block_rows * lax.axis_size("ctx")
        grad_key = (
            jnp.einsum(
                "shqk,sqhd->kshd", grad_scores, query_heads, preferred_element_type=jnp.float32
            )
            * scale
        )
        grad_value = jnp.einsum(
            "shqk,sqhd->kshd", probs_low, grad_heads, preferred_element_type=jnp.float32
        )
        key_sums = lax.psum_scatter(
            jnp.stack(
                [
                    grad_key.reshape(count, sequences, width),
                    grad_value.reshape(count, sequences, width),
                ],
                axis=2,
            ).astype(jnp.bfloat16),
            "ctx",
            scatter_dimension=0,
            tiled=True,
        ).astype(jnp.float32)
        grad_key_local = jnp.swapaxes(key_sums[:, :, 0], 0, 1).reshape(rows, width)
        grad_value_low = (
            jnp.swapaxes(key_sums[:, :, 1], 0, 1).reshape(rows, width).astype(jnp.bfloat16)
        )

        def turn(projected, gain):
            return rotate(projected, gain, cosines, sines)

        unused, query_back = jax.vjp(turn, query_proj, gain_query)
        grad_query_proj, grad_gain_query = query_back(grad_query)
        unused, key_back = jax.vjp(turn, key_proj, gain_key)
        grad_key_proj, grad_gain_key = key_back(grad_key_local)
        grad_query_low = grad_query_proj.astype(jnp.bfloat16)
        grad_key_low = grad_key_proj.astype(jnp.bfloat16)
        grad_query_w = jnp.einsum(
            "rd,re->de", normed_in, grad_query_low, preferred_element_type=jnp.float32
        )
        grad_key_w = jnp.einsum(
            "rd,re->de", normed_in, grad_key_low, preferred_element_type=jnp.float32
        )
        grad_value_w = jnp.einsum(
            "rd,re->de", normed_in, grad_value_low, preferred_element_type=jnp.float32
        )
        grad_normed = jnp.einsum(
            "re,de->rd", grad_query_low, query_w, preferred_element_type=jnp.float32
        )
        grad_normed = grad_normed + jnp.einsum(
            "re,de->rd", grad_key_low, key_w, preferred_element_type=jnp.float32
        )
        grad_normed = grad_normed + jnp.einsum(
            "re,de->rd", grad_value_low, value_w, preferred_element_type=jnp.float32
        )
        unused, in_back = jax.vjp(norm_rows, inputs, gain_attn)
        grad_inputs_norm, grad_gain_attn = in_back(grad_normed)
        input_grads.append((grad_hidden + grad_inputs_norm).reshape(sequences, block_rows, width))
        attention_grads = (
            grad_query_w,
            grad_key_w,
            grad_value_w,
            grad_out_w,
            grad_gain_attn,
            grad_gain_query,
            grad_gain_key,
            grad_gain_ffn,
        )
        expert_grads = (grad_gate_w, grad_up_w, grad_down_w)
        attention_part = (
            lax.psum_scatter(attention_grads[0], ("batch", "ctx"), scatter_dimension=0, tiled=True),
            lax.psum_scatter(attention_grads[1], ("batch", "ctx"), scatter_dimension=0, tiled=True),
            lax.psum_scatter(attention_grads[2], ("batch", "ctx"), scatter_dimension=0, tiled=True),
            lax.psum_scatter(attention_grads[3], ("batch", "ctx"), scatter_dimension=0, tiled=True),
            lax.psum_scatter(attention_grads[4], ("batch", "ctx"), scatter_dimension=0, tiled=True),
            lax.psum_scatter(attention_grads[5], ("batch", "ctx"), scatter_dimension=0, tiled=True),
            lax.psum_scatter(attention_grads[6], ("batch", "ctx"), scatter_dimension=0, tiled=True),
            lax.psum_scatter(attention_grads[7], ("batch", "ctx"), scatter_dimension=0, tiled=True),
        )
        expert_part = (
            lax.psum_scatter(
                expert_grads[0].astype(jnp.bfloat16), "batch", scatter_dimension=1, tiled=True
            ).astype(jnp.float32),
            lax.psum_scatter(
                expert_grads[1].astype(jnp.bfloat16), "batch", scatter_dimension=1, tiled=True
            ).astype(jnp.float32),
            lax.psum_scatter(
                expert_grads[2].astype(jnp.bfloat16), "batch", scatter_dimension=2, tiled=True
            ).astype(jnp.float32),
        )
        attention_part, expert_part = (attention_part, expert_part)
        attention_total = add_trees(attention_total, attention_part)
        expert_total = add_trees(expert_total, expert_part)
    return (
        jnp.stack(outputs),
        jnp.stack(input_grads),
        attention_total[0],
        attention_total[1],
        attention_total[2],
        attention_total[3],
        attention_total[4],
        attention_total[5],
        attention_total[6],
        attention_total[7],
        expert_total[0],
        expert_total[1],
        expert_total[2],
    )


def solution(mesh):
    in_specs = (
        P(None, "batch", "ctx", None),
        P(None, "batch"),
        P(None, "batch", "ctx", None),
        P(None, "batch", "ctx", None),
        P(("batch", "ctx"), None),
        P(("batch", "ctx"), None),
        P(("batch", "ctx"), None),
        P(("batch", "ctx"), None),
        P(("batch", "ctx")),
        P(("batch", "ctx")),
        P(("batch", "ctx")),
        P(("batch", "ctx")),
        P("ctx", "batch", None),
        P("ctx", "batch", None),
        P("ctx", None, "batch"),
        P(None, "batch", "ctx", None),
    )
    out_specs = (
        P(None, "batch", "ctx", None),
        P(None, "batch", "ctx", None),
        P(("batch", "ctx"), None),
        P(("batch", "ctx"), None),
        P(("batch", "ctx"), None),
        P(("batch", "ctx"), None),
        P(("batch", "ctx")),
        P(("batch", "ctx")),
        P(("batch", "ctx")),
        P(("batch", "ctx")),
        P("ctx", "batch", None),
        P("ctx", "batch", None),
        P("ctx", None, "batch"),
    )
    return jax.shard_map(body, mesh=mesh, in_specs=in_specs, out_specs=out_specs, check_vma=False)
```

profile of v0, /device:TPU:0, one launch (start us, length us, event | category | flops | bytes accessed | tf_op | source)
XLA Modules:
  0.0 5164.6 jit_solution(10643547647718028710)
XLA Ops:
  12.9 42.6 all-reduce.21
  62.1 29.4 all-gather.18.cloned.1.call-done
  108.7 61.8 %all-gather.20.cloned.1.call-done = bf16[2048,2048]{1,0:T(8,128)(2,1)} async-done(((bf16[64,2048]{1,0:T(8,128)(2,1)}), bf16[2048,2048]{1,0:T(8,128)(2,1)}) %all-gather.20.cloned.1.call-update) | async-done | bytes 8388624 | tf_op jit(solution)/shard_map/all_gather | solution.py:99
  217.8 31.6 all-gather.16.cloned.1.call-done
  293.0 24.8 gather_fusion.4
  328.4 60.3 %all-gather.32.cloned.1.call-done = bf16[1024,2048]{1,0:T(8,128)(2,1)} async-done(((bf16[256,2048]{1,0:T(8,128)(2,1)}), bf16[1024,2048]{1,0:T(8,128)(2,1)}) %all-gather.32.cloned.1.call-update) | async-done | bytes 4194320 | tf_op jit(solution)/shard_map/all_gather | solution.py:146
  406.4 151.9 %all-gather.30.cloned.1.call-done = bf16[1024,2048]{1,0:T(8,128)(2,1)} async-done(((bf16[256,2048]{1,0:T(8,128)(2,1)}), bf16[1024,2048]{1,0:T(8,128)(2,1)}) %all-gather.30.cloned.1.call-update) | async-done | bytes 4194320 | tf_op jit(solution)/shard_map/all_gather | solution.py:149
  568.6 114.4 %all-gather.22.cloned.1.call-done = bf16[2048,2048]{1,0:T(8,128)(2,1)} async-done(((bf16[64,2048]{1,0:T(8,128)(2,1)}), bf16[2048,2048]{1,0:T(8,128)(2,1)}) %all-gather.22.cloned.1.call-update) | async-done | bytes 8388624 | tf_op jit(solution)/shard_map/all_gather | solution.py:101
  707.6 69.0 %all-gather.28.cloned.1.call-done = bf16[4,1024,2048]{2,1,0:T(8,128)(2,1)} async-done(((bf16[4,1024,256]{2,1,0:T(8,128)(2,1)}), bf16[4,1024,2048]{2,1,0:T(8,128)(2,1)}) %all-gather.28.cloned.1.call-update) | async-done | bytes 16777232 | tf_op jit(solution)/shard_map/all_gather | solution.py:110
  795.0 73.3 %all-gather.26.cloned.1.call-done = bf16[4,2048,1024]{2,1,0:T(8,128)(2,1)} async-done(((bf16[4,256,1024]{2,1,0:T(8,128)(2,1)}), bf16[4,2048,1024]{2,1,0:T(8,128)(2,1)}) %all-gather.26.cloned.1.call-update) | async-done | bytes 16777232 | tf_op jit(solution)/shard_map/all_gather | solution.py:109
  868.4 67.9 %all-to-all-done = bf16[4,4,160,2048]{3,2,1,0:T(8,128)(2,1)} async-done(((bf16[4,4,160,2048]{3,2,1,0:T(8,128)(2,1)}), bf16[4,4,160,2048]{3,2,1,0:T(8,128)(2,1)}, u32[]{:S(2)}, u32[]{:S(2)}) %all-to-all-start) | async-done | bytes 10485792 | tf_op jit(solution)/shard_map/all_to_all | solution.py:178
  960.2 28.6 fusion.32
  1073.0 25.1 gather_fusion.6
  1098.1 243.7 %all-to-all-done.5 = bf16[4,4,160,2048]{3,2,1,0:T(8,128)(2,1)} async-done(((bf16[4,4,160,2048]{3,2,1,0:T(8,128)(2,1)}), bf16[4,4,160,2048]{3,2,1,0:T(8,128)(2,1)}, u32[]{:S(2)}, u32[]{:S(2)}) %all-to-all-start.5) | async-done | bytes 10485792 | tf_op jit(solution)/shard_map/all_to_all | solution.py:244
  1374.6 135.2 %all-gather.34.cloned.1.call-done = bf16[1024,2048]{1,0:T(8,128)(2,1)} async-done(((bf16[256,2048]{1,0:T(8,128)(2,1)}), bf16[1024,2048]{1,0:T(8,128)(2,1)}) %all-gather.34.cloned.1.call-update) | async-done | bytes 4194320 | tf_op jit(solution)/shard_map/all_gather | solution.py:149
  1576.0 67.2 %all-to-all-done.6 = bf16[4,4,160,2048]{3,2,1,0:T(8,128)(2,1)} async-done(((bf16[4,4,160,2048]{3,2,1,0:T(8,128)(2,1)}), bf16[4,4,160,2048]{3,2,1,0:T(8,128)(2,1)}, u32[]{:S(2)}, u32[]{:S(2)}) %all-to-all-start.6) | async-done | bytes 10485792 | tf_op jit(solution)/shard_map/all_to_all | solution.py:220
  1679.7 197.2 %all-to-all-done.2 = bf16[4,4,160,2048]{3,2,1,0:T(8,128)(2,1)} async-done(((bf16[4,4,160,2048]{3,2,1,0:T(8,128)(2,1)}), bf16[4,4,160,2048]{3,2,1,0:T(8,128)(2,1)}, u32[]{:S(2)}, u32[]{:S(2)}) %all-to-all-start.2) | async-done | bytes 10485792 | tf_op jit(solution)/shard_map/all_to_all | solution.py:178
  1921.3 28.5 fusion.35
  1980.1 130.5 %all-to-all-done.1 = bf16[4,4,160,2048]{3,2,1,0:T(8,128)(2,1)} async-done(((bf16[4,4,160,2048]{3,2,1,0:T(8,128)(2,1)}), bf16[4,4,160,2048]{3,2,1,0:T(8,128)(2,1)}, u32[]{:S(2)}, u32[]{:S(2)}) %all-to-all-start.1) | async-done | bytes 10485792 | tf_op jit(solution)/shard_map/all_to_all | solution.py:185
  2167.6 176.9 %all-to-all-done.3 = bf16[4,4,160,2048]{3,2,1,0:T(8,128)(2,1)} async-done(((bf16[4,4,160,2048]{3,2,1,0:T(8,128)(2,1)}), bf16[4,4,160,2048]{3,2,1,0:T(8,128)(2,1)}, u32[]{:S(2)}, u32[]{:S(2)}) %all-to-all-start.3) | async-done | bytes 10485792 | tf_op jit(solution)/shard_map/all_to_all | solution.py:185
  2406.9 171.1 %all-to-all-done.7 = bf16[4,4,160,2048]{3,2,1,0:T(8,128)(2,1)} async-done(((bf16[4,4,160,2048]{3,2,1,0:T(8,128)(2,1)}), bf16[4,4,160,2048]{3,2,1,0:T(8,128)(2,1)}, u32[]{:S(2)}, u32[]{:S(2)}) %all-to-all-start.7) | async-done | bytes 10485792 | tf_op jit(solution)/shard_map/all_to_all | solution.py:244
  2893.1 84.5 %reduce-scatter.15.cloned.1.call-done = bf16[256,1,2,2048]{0,3,2,1:T(8,128)(2,1)} async-done(((bf16[1024,1,2,2048]{0,3,2,1:T(8,128)(2,1)}), bf16[256,1,2,2048]{0,3,2,1:T(8,128)(2,1)}) %reduce-scatter.15.cloned.1.call-update) | async-done | bytes 2097168 | tf_op jit(solution)/shard_map/reduce_scatter | solution.py:286
  3097.7 119.4 %reduce-scatter.27.cloned.1.call-done = bf16[4,1024,256]{2,1,0:T(8,128)(2,1)} async-done(((bf16[4,1024,2048]{2,1,0:T(8,128)(2,1)}), bf16[4,1024,256]{2,1,0:T(8,128)(2,1)}) %reduce-scatter.27.cloned.1.call-update) | async-done | bytes 2097168 | tf_op jit(solution)/shard_map/reduce_scatter | solution.py:361
  3221.8 114.7 %reduce-scatter.17.cloned.1.call-done = bf16[4,256,1024]{2,1,0:T(8,128)(2,1)} async-done(((bf16[4,2048,1024]{2,1,0:T(8,128)(2,1)}), bf16[4,256,1024]{2,1,0:T(8,128)(2,1)}) %reduce-scatter.17.cloned.1.call-update) | async-done | bytes 2097168 | tf_op jit(solution)/shard_map/reduce_scatter | solution.py:355
  3336.4 119.4 %reduce-scatter.19.cloned.1.call-done = bf16[4,256,1024]{2,1,0:T(8,128)(2,1)} async-done(((bf16[4,2048,1024]{2,1,0:T(8,128)(2,1)}), bf16[4,256,1024]{2,1,0:T(8,128)(2,1)}) %reduce-scatter.19.cloned.1.call-update) | async-done | bytes 2097168 | tf_op jit(solution)/shard_map/reduce_scatter | solution.py:355
  3461.0 114.3 %reduce-scatter.21.cloned.1.call-done = bf16[4,256,1024]{2,1,0:T(8,128)(2,1)} async-done(((bf16[4,2048,1024]{2,1,0:T(8,128)(2,1)}), bf16[4,256,1024]{2,1,0:T(8,128)(2,1)}) %reduce-scatter.21.cloned.1.call-update) | async-done | bytes 2097168 | tf_op jit(solution)/shard_map/reduce_scatter | solution.py:358
  3575.2 119.6 %reduce-scatter.23.cloned.1.call-done = bf16[4,256,1024]{2,1,0:T(8,128)(2,1)} async-done(((bf16[4,2048,1024]{2,1,0:T(8,128)(2,1)}), bf16[4,256,1024]{2,1,0:T(8,128)(2,1)}) %reduce-scatter.23.cloned.1.call-update) | async-done | bytes 2097168 | tf_op jit(solution)/shard_map/reduce_scatter | solution.py:358
  3730.2 44.0 all-reduce.20
  3783.7 278.9 %reduce-scatter.35.cloned.1.call-done = f32[64,2048]{1,0:T(8,128)} async-done(((f32[2048,2048]{1,0:T(8,128)}), f32[64,2048]{1,0:T(8,128)}) %reduce-scatter.35.cloned.1.call-update) | async-done | bytes 524304 | tf_op jit(solution)/shard_map/reduce_scatter | solution.py:348
  4062.6 365.1 %reduce-scatter.33.cloned.1.call-done = f32[64,2048]{1,0:T(8,128)} async-done(((f32[2048,2048]{1,0:T(8,128)}), f32[64,2048]{1,0:T(8,128)}) %reduce-scatter.33.cloned.1.call-update) | async-done | bytes 524304 | tf_op jit(solution)/shard_map/reduce_scatter | solution.py:347
  4427.7 365.1 %reduce-scatter.31.cloned.1.call-done = f32[64,2048]{1,0:T(8,128)} async-done(((f32[2048,2048]{1,0:T(8,128)}), f32[64,2048]{1,0:T(8,128)}) %reduce-scatter.31.cloned.1.call-update) | async-done | bytes 524304 | tf_op jit(solution)/shard_map/reduce_scatter | solution.py:346
  4792.8 365.1 %reduce-scatter.29.cloned.1.call-done = f32[64,2048]{1,0:T(8,128)} async-done(((f32[2048,2048]{1,0:T(8,128)}), f32[64,2048]{1,0:T(8,128)}) %reduce-scatter.29.cloned.1.call-update) | async-done | bytes 524304 | tf_op jit(solution)/shard_map/reduce_scatter | solution.py:345
  (584 shorter events, 1126.9 us)
Async XLA Ops:
  7.2 84.4 %all-gather.18.cloned.1.call-start = ((), (), s32[]{:S(2)}) async-start(), calls=%async_computation.21 | async-start | bytes 8650752 | tf_op jit(solution)/shard_map/all_gather | solution.py:98
  7.9 162.6 %all-gather.20.cloned.1.call-start = ((), (), s32[]{:S(2)}) async-start(), calls=%async_computation.22 | async-start | bytes 8650752 | tf_op jit(solution)/shard_map/all_gather | solution.py:99
  8.7 240.8 %all-gather.16.cloned.1.call-start = ((), (), s32[]{:S(2)}) async-start(), calls=%async_computation.20 | async-start | bytes 8650752 | tf_op jit(solution)/shard_map/all_gather | solution.py:100
  9.4 379.3 %all-gather.32.cloned.1.call-start = ((), (), s32[]{:S(2)}) async-start(), calls=%async_computation.36 | async-start | bytes 5242880 | tf_op jit(solution)/shard_map/all_gather | solution.py:146
  217.8 340.5 %all-gather.30.cloned.1.call-start = ((), (), s32[]{:S(2)}) async-start(), calls=%async_computation.35 | async-start | bytes 5242880 | tf_op jit(solution)/shard_map/all_gather | solution.py:149
  256.2 426.7 %all-gather.22.cloned.1.call-start = ((), (), s32[]{:S(2)}) async-start(), calls=%async_computation.23 | async-start | bytes 8650752 | tf_op jit(solution)/shard_map/all_gather | solution.py:101
  256.8 519.8 %all-gather.28.cloned.1.call-start = ((), (), s32[]{:S(2)}) async-start(), calls=%async_computation.26 | async-start | bytes 18874368 | tf_op jit(solution)/shard_map/all_gather | solution.py:110
  257.5 610.8 %all-gather.26.cloned.1.call-start = ((), (), s32[]{:S(2)}) async-start(), calls=%async_computation.25 | async-start | bytes 18874368 | tf_op jit(solution)/shard_map/all_gather | solution.py:109
  317.8 383.6 %all-to-all-start.4 = ((bf16[4,4,160,2048]{3,2,1,0:T(8,128)(2,1)}), bf16[4,4,160,2048]{3,2,1,0:T(8,128)(2,1)}, u32[]{:S(2)}, u32[]{:S(2)}) async-start(bf16[4,4,160,2048]{3,2,1,0:T(8,128)(2,1)} %bitcast.491), calls=%async_computation.4 | async-start | bytes 20971520 | tf_op jit(solution)/shard_map/all_to_all | solution.py:220
  323.7 636.5 %all-gather.24.cloned.1.call-start = ((), (), s32[]{:S(2)}) async-start(), calls=%async_computation.24 | async-start | bytes 18874368 | tf_op jit(solution)/shard_map/all_gather | solution.py:108
  324.4 364.4 %copy-start.63 = (f32[2048]{0:T(1024)}, f32[2048]{0:T(1024)S(1)}, u32[]{:S(2)}) copy-start(f32[2048]{0:T(1024)S(1)} %convert_element_type.383) | copy-start | bytes 24580
  701.3 235.0 %all-to-all-start = ((bf16[4,4,160,2048]{3,2,1,0:T(8,128)(2,1)}), bf16[4,4,160,2048]{3,2,1,0:T(8,128)(2,1)}, u32[]{:S(2)}, u32[]{:S(2)}) async-start(bf16[4,4,160,2048]{3,2,1,0:T(8,128)(2,1)} %bitcast.492), calls=%async_computation | async-start | bytes 20971520 | tf_op jit(solution)/shard_map/all_to_all | solution.py:178
  1039.5 302.2 %all-to-all-start.5 = ((bf16[4,4,160,2048]{3,2,1,0:T(8,128)(2,1)}), bf16[4,4,160,2048]{3,2,1,0:T(8,128)(2,1)}, u32[]{:S(2)}, u32[]{:S(2)}) async-start(bf16[4,4,160,2048]{3,2,1,0:T(8,128)(2,1)} %copy.149), calls=%async_computation.5 | async-start | bytes 20971520 | tf_op jit(solution)/shard_map/all_to_all | solution.py:244
  1045.7 310.9 %all-gather.36.cloned.1.call-start = ((), (), s32[]{:S(2)}) async-start(), calls=%async_computation.38 | async-start | bytes 5242880 | tf_op jit(solution)/shard_map/all_gather | solution.py:146
  1341.8 301.4 %all-to-all-start.6 = ((bf16[4,4,160,2048]{3,2,1,0:T(8,128)(2,1)}), bf16[4,4,160,2048]{3,2,1,0:T(8,128)(2,1)}, u32[]{:S(2)}, u32[]{:S(2)}) async-start(bf16[4,4,160,2048]{3,2,1,0:T(8,128)(2,1)} %bitcast.490), calls=%async_computation.7 | async-start | bytes 20971520 | tf_op jit(solution)/shard_map/all_to_all | solution.py:220
  1347.9 161.8 %all-gather.34.cloned.1.call-start = ((), (), s32[]{:S(2)}) async-start(), calls=%async_computation.37 | async-start | bytes 5242880 | tf_op jit(solution)/shard_map/all_gather | solution.py:149
  1643.2 233.7 %all-to-all-start.2 = ((bf16[4,4,160,2048]{3,2,1,0:T(8,128)(2,1)}), bf16[4,4,160,2048]{3,2,1,0:T(8,128)(2,1)}, u32[]{:S(2)}, u32[]{:S(2)}) async-start(bf16[4,4,160,2048]{3,2,1,0:T(8,128)(2,1)} %bitcast.493), calls=%async_computation.2 | async-start | bytes 20971520 | tf_op jit(solution)/shard_map/all_to_all | solution.py:178
  1876.9 233.7 %all-to-all-start.1 = ((bf16[4,4,160,2048]{3,2,1,0:T(8,128)(2,1)}), bf16[4,4,160,2048]{3,2,1,0:T(8,128)(2,1)}, u32[]{:S(2)}, u32[]{:S(2)}) async-start(bf16[4,4,160,2048]{3,2,1,0:T(8,128)(2,1)} %copy.129), calls=%async_computation.1 | async-start | bytes 20971520 | tf_op jit(solution)/shard_map/all_to_all | solution.py:185
  2110.6 234.0 %all-to-all-start.3 = ((bf16[4,4,160,2048]{3,2,1,0:T(8,128)(2,1)}), bf16[4,4,160,2048]{3,2,1,0:T(8,128)(2,1)}, u32[]{:S(2)}, u32[]{:S(2)}) async-start(bf16[4,4,160,2048]{3,2,1,0:T(8,128)(2,1)} %copy.144), calls=%async_computation.3 | async-start | bytes 20971520 | tf_op jit(solution)/shard_map/all_to_all | solution.py:185
  2344.5 233.5 %all-to-all-start.7 = ((bf16[4,4,160,2048]{3,2,1,0:T(8,128)(2,1)}), bf16[4,4,160,2048]{3,2,1,0:T(8,128)(2,1)}, u32[]{:S(2)}, u32[]{:S(2)}) async-start(bf16[4,4,160,2048]{3,2,1,0:T(8,128)(2,1)} %copy.160), calls=%async_computation.8 | async-start | bytes 20971520 | tf_op jit(solution)/shard_map/all_to_all | solution.py:244
  2350.5 531.8 %reduce-scatter.13.cloned.1.call-start = ((), (), s32[]{:S(2)}) async-start(), calls=%async_computation.27 | async-start | bytes 10485760 | tf_op jit(solution)/shard_map/reduce_scatter | solution.py:286
  2687.2 290.4 %reduce-scatter.15.cloned.1.call-start = ((), (), s32[]{:S(2)}) async-start(), calls=%async_computation.28 | async-start | bytes 10485760 | tf_op jit(solution)/shard_map/reduce_scatter | solution.py:286
  2743.3 354.4 %reduce-scatter.25.cloned.1.call-start = ((), (), s32[]{:S(2)}) async-start(), calls=%async_computation.33 | async-start | bytes 18874368 | tf_op jit(solution)/shard_map/reduce_scatter | solution.py:361
  2763.9 453.2 %reduce-scatter.27.cloned.1.call-start = ((), (), s32[]{:S(2)}) async-start(), calls=%async_computation.34 | async-start | bytes 18874368 | tf_op jit(solution)/shard_map/reduce_scatter | solution.py:361
  2784.5 552.0 %reduce-scatter.17.cloned.1.call-start = ((), (), s32[]{:S(2)}) async-start(), calls=%async_computation.29 | async-start | bytes 18874368 | tf_op jit(solution)/shard_map/reduce_scatter | solution.py:355
  2804.7 651.1 %reduce-scatter.19.cloned.1.call-start = ((), (), s32[]{:S(2)}) async-start(), calls=%async_computation.30 | async-start | bytes 18874368 | tf_op jit(solution)/shard_map/reduce_scatter | solution.py:355
  2825.2 750.0 %reduce-scatter.21.cloned.1.call-start = ((), (), s32[]{:S(2)}) async-start(), calls=%async_computation.31 | async-start | bytes 18874368 | tf_op jit(solution)/shard_map/reduce_scatter | solution.py:358
  2845.7 849.1 %reduce-scatter.23.cloned.1.call-start = ((), (), s32[]{:S(2)}) async-start(), calls=%async_computation.32 | async-start | bytes 18874368 | tf_op jit(solution)/shard_map/reduce_scatter | solution.py:358
  2866.3 1196.3 %reduce-scatter.35.cloned.1.call-start = ((), (), s32[]{:S(2)}) async-start(), calls=%async_computation.42 | async-start | bytes 17301504 | tf_op jit(solution)/shard_map/reduce_scatter | solution.py:348
  2882.0 1545.7 %reduce-scatter.33.cloned.1.call-start = ((), (), s32[]{:S(2)}) async-start(), calls=%async_computation.41 | async-start | bytes 17301504 | tf_op jit(solution)/shard_map/reduce_scatter | solution.py:347
  2995.0 1797.8 %reduce-scatter.31.cloned.1.call-start = ((), (), s32[]{:S(2)}) async-start(), calls=%async_computation.40 | async-start | bytes 17301504 | tf_op jit(solution)/shard_map/reduce_scatter | solution.py:346
  3058.9 2098.9 %reduce-scatter.29.cloned.1.call-start = ((), (), s32[]{:S(2)}) async-start(), calls=%async_computation.39 | async-start | bytes 17301504 | tf_op jit(solution)/shard_map/reduce_scatter | solution.py:345
  (141 other events, 3635.5 us)
Sparse Core Ops, SparseCore 0:
  11.0 80.5 all-gather.17
  94.5 75.9 all-gather.19
  173.4 75.9 all-gather.15
  250.9 137.8 all-gather.31
  390.7 167.5 all-gather.29
  561.1 121.8 all-gather.21
  684.8 91.6 all-gather.27
  778.5 89.8 all-gather.25
  870.3 89.8 all-gather.23
  1064.6 144.2 all-gather.35
  1355.1 154.6 all-gather.33
  2687.3 142.6 reduce-scatter.12
  2832.3 145.1 reduce-scatter.14
  2980.9 116.6 reduce-scatter.24
  3101.1 115.9 reduce-scatter.26
  3220.5 115.9 reduce-scatter.16
  3339.9 115.9 reduce-scatter.18
  3459.2 115.9 reduce-scatter.20
  3578.8 115.9 reduce-scatter.22
  3697.5 365.0 reduce-scatter.34
  4065.5 362.1 reduce-scatter.32
  4430.6 362.1 reduce-scatter.30
  4795.6 362.1 reduce-scatter.28
where the time goes:
time: 5180 us; the launch traced here: 5160 us
  waiting for transfers between devices  3840 us (74%)
  matrix products  635 us (12%)
  local copies, waits for them, and re-layouts  330 us (6%)
  other arithmetic  202 us (4%)
  blocking collectives  86.7 us (2%)
    all_to_all x2, waiting for transfers between devices, body(): lax.all_to_all(grad_sent, 'ctx', split_axis=0, concat_axis=0, tiled=True)  415 us
    reduce_scatter x1, waiting for transfers between devices, body(): lax.psum_scatter(attention_grads[2], ('batch', 'ctx'), scatter_dimension=...  365 us
    reduce_scatter x1, waiting for transfers between devices, body(): lax.psum_scatter(attention_grads[0], ('batch', 'ctx'), scatter_dimension=...  365 us
    reduce_scatter x1, waiting for transfers between devices, body(): lax.psum_scatter(attention_grads[1], ('batch', 'ctx'), scatter_dimension=...  365 us
    all_to_all x2, waiting for transfers between devices, body(): lax.all_to_all(produced, 'ctx', split_axis=0, concat_axis=0, tiled=True)  307 us
    all_gather x2, waiting for transfers between devices, body(): lax.all_gather(value_low.reshape(sequences, block_rows, width), 'ctx', ax...  287 us
    reduce_scatter x1, waiting for transfers between devices, body(): lax.psum_scatter(attention_grads[3], ('batch', 'ctx'), scatter_dimension=...  279 us
    all_to_all x2, waiting for transfers between devices, body(): lax.all_to_all(outgoing, 'ctx', split_axis=0, concat_axis=0, tiled=True)  265 us
  transfers between devices with their start and end apart: 31, of which 28 were waited for; matrix products, arithmetic and copies ran while one was open for 18% of the time, Pallas kernels for 0%

commit v1 on v0

v1 whole, which is shorter than its diff:
```python
import jax
import jax.numpy as jnp
from jax import lax
from jax.experimental import pallas as pl
from jax.experimental.pallas import tpu as pltpu
from jax.sharding import PartitionSpec as P

HEAD_DIM = 128
EPS = 1e-05
THETA = 10000.0
MASKED = -1e30
LANES = 128
ROOM = 58 << 20

f32 = jnp.float32
bf16 = jnp.bfloat16


def dot(left, right, contract=((1,), (0,))):
    return lax.dot_general(left, right, (contract, ((), ())), preferred_element_type=f32)


def dot_nt(left, right):
    return dot(left, right, ((1,), (1,)))


def dot_tn(left, right):
    return dot(left, right, ((0,), (0,)))


def struct(shape, dtype):
    return jax.ShapeDtypeStruct(shape, dtype)


def cost(flops, *arrays):
    moved = sum(a.size * a.dtype.itemsize for a in arrays)
    return pl.CostEstimate(flops=int(flops), bytes_accessed=int(moved), transcendentals=0)


def whole(array):
    zeros = (0,) * len(array.shape)
    return pl.BlockSpec(array.shape, lambda *_: zeros, pipeline_mode=pl.Buffered(1))


def params(axes):
    return pltpu.CompilerParams(
        dimension_semantics=("arbitrary",) * axes, vmem_limit_bytes=ROOM
    )


def chunks_of(blocks, cap):
    parts = max(1, (blocks * cap) // 640)
    while blocks % parts:
        parts -= 1
    return parts


def project(pieces, gain, weight):
    count, (rows, width) = len(pieces), pieces[0].shape
    third = weight.shape[1] // 3
    total = count * rows
    step = 32
    part = min(total, 512)

    def kernel(*refs):
        xs, (gain_ref, w_ref), (n_ref, out_ref, ss_ref) = (
            refs[:count],
            refs[count : count + 2],
            refs[count + 2 :],
        )

        @pl.when(pl.program_id(0) == 0)
        def _():
            for i in range(count):

                @pl.loop(0, rows // step)
                def _(k):
                    v = xs[i][pl.ds(k * step, step), :].astype(f32)
                    r = lax.rsqrt(jnp.mean(v * v, axis=-1, keepdims=True) + EPS)
                    n_ref[pl.ds(i * rows + k * step, step), :] = (v * r * gain_ref[...]).astype(
                        bf16
                    )

        @pl.loop(0, total // part)
        def _(k):
            at = pl.ds(pl.multiple_of(k * part, part), part)
            p = dot(n_ref[at, :], w_ref[...])
            out_ref[at, :] = p
            ss_ref[0, at, :] = jnp.sum(p * p, axis=-1, keepdims=True)

    outs = (
        struct((total, width), bf16),
        struct((total, 3 * third), f32),
        struct((3, total, 1), f32),
    )
    return pl.pallas_call(
        kernel,
        grid=(3,),
        in_specs=[whole(x) for x in pieces]
        + [whole(gain), pl.BlockSpec((width, third), lambda t: (0, t))],
        out_specs=(
            pl.BlockSpec((total, width), lambda t: (0, 0)),
            pl.BlockSpec((total, third), lambda t: (0, t)),
            pl.BlockSpec((1, total, 1), lambda t: (t, 0, 0)),
        ),
        out_shape=outs,
        compiler_params=params(1),
        cost_estimate=cost(2 * total * width * 3 * third, *pieces, weight, *outs[:2]),
        name="project",
    )(*pieces, gain, weight)


def turn(v, cosines, sines):
    return v * cosines + pltpu.roll(v, HEAD_DIM // 2, 1) * sines


def turn_back(v, cosines, sines):
    return v * cosines + pltpu.roll(v * sines, HEAD_DIM // 2, 1)


def allowed_of(start, rows, count, length):
    row = start + lax.broadcasted_iota(jnp.int32, (rows, count), 0)
    col = lax.broadcasted_iota(jnp.int32, (rows, count), 1)
    return (col <= row) & (col < length)


def attention_forward(place, lengths, qkv, inverse, gains, cosines, sines):
    n, seqs, rows, wide = qkv.shape
    cols = wide // 3
    heads = cols // HEAD_DIM
    span = n * rows
    scale = HEAD_DIM ** (-0.5)

    def kernel(place_ref, len_ref, qi, ki, vi, inv, gain_ref, cos_ref, sin_ref, q_o, k_o, v_o, att, lse):
        here = place_ref[0]
        length = len_ref[pl.program_id(0)]
        for p in range(n):
            j = lax.rem(here + (n - p), n)
            at = slice(p * rows, (p + 1) * rows)
            for which, (src, dst) in enumerate(((qi, q_o), (ki, k_o))):
                z = src[j, 0] * inv[which, j, 0] * gain_ref[which]
                dst[0, at, :] = turn(z, cos_ref[p], sin_ref[p]).astype(bf16)
            v_o[0, at, :] = vi[j, 0].astype(bf16)
        for p in range(n):
            at = slice(p * rows, (p + 1) * rows)
            kv = (p + 1) * rows
            s = dot_nt(q_o[0, at, :], k_o[0, :kv, :]) * scale
            s = jnp.where(allowed_of(p * rows, rows, kv, length), s, MASKED)
            peak = jnp.max(s, axis=-1, keepdims=True)
            e = jnp.exp(s - peak)
            z = jnp.sum(e, axis=-1, keepdims=True)
            att[p, 0] = dot((e / z).astype(bf16), v_o[0, :kv, :]).astype(bf16)
            lse[0, 0, at, :] = peak + jnp.log(z)

    def part(k):
        return pl.BlockSpec((n, 1, rows, HEAD_DIM), lambda g, h, *_: (0, g, 0, k * heads + h))

    line = pl.BlockSpec((1, span, HEAD_DIM), lambda g, h, *_: (g, 0, h))
    outs = (struct((seqs, span, cols), bf16),) * 3 + (
        struct((n, seqs, rows, cols), bf16),
        struct((seqs, heads, span, 1), f32),
    )
    return pl.pallas_call(
        kernel,
        grid_spec=pltpu.PrefetchScalarGridSpec(
            num_scalar_prefetch=2,
            grid=(seqs, heads),
            in_specs=[
                part(0),
                part(1),
                part(2),
                pl.BlockSpec((2, n, 1, rows, 1), lambda g, h, *_: (0, 0, g, 0, 0)),
                pl.BlockSpec((2, 1, HEAD_DIM), lambda g, h, *_: (0, 0, h)),
                whole(cosines),
                whole(sines),
            ],
            out_specs=(
                line,
                line,
                line,
                pl.BlockSpec((n, 1, rows, HEAD_DIM), lambda g, h, *_: (0, g, 0, h)),
                pl.BlockSpec((1, 1, span, 1), lambda g, h, *_: (g, h, 0, 0)),
            ),
        ),
        out_shape=outs,
        compiler_params=params(2),
        cost_estimate=cost(3 * seqs * heads * span * span * HEAD_DIM, qkv, *outs[:4]),
        name="attention",
    )(place, lengths, qkv, qkv, qkv, inverse, gains, cosines, sines)


def attention_backward(place, lengths, q, k, v, grad, lse, qkv, inverse, gains, cosines, sines):
    n, seqs, rows, wide = qkv.shape
    cols = wide // 3
    heads = cols // HEAD_DIM
    span = n * rows
    scale = HEAD_DIM ** (-0.5)

    def kernel(
        place_ref, len_ref, q_i, k_i, v_i, do_i, lse_i, qp_i, kp_i, inv, gain_ref, cos_ref, sin_ref,
        dq_o, dk_o, dv_o, st_o, dg_o, dq_s, dk_s, dv_s,
    ):
        here = place_ref[0]
        length = len_ref[pl.program_id(0)]
        dk_s[...] = jnp.zeros_like(dk_s)
        dv_s[...] = jnp.zeros_like(dv_s)
        for p in range(n):
            at = slice(p * rows, (p + 1) * rows)
            kv = (p + 1) * rows
            query, keys, values, do = q_i[0, at, :], k_i[0, :kv, :], v_i[0, :kv, :], do_i[p, 0]
            s = dot_nt(query, keys) * scale
            probs = jnp.where(
                allowed_of(p * rows, rows, kv, length), jnp.exp(s - lse_i[0, 0, at, :]), 0.0
            )
            dp = dot_nt(do, values)
            ds = (probs * (dp - jnp.sum(probs * dp, axis=-1, keepdims=True))).astype(bf16)
            dq_s[at, :] = dot(ds, keys) * scale
            dk_s[:kv, :] += dot_tn(ds, query)
            dv_s[:kv, :] += dot_tn(probs.astype(bf16), do)
        dk_s[...] = dk_s[...] * scale
        sums = [jnp.zeros((1, HEAD_DIM), f32)] * 2
        for p in range(n):
            j = lax.rem(here + (n - p), n)
            at = slice(p * rows, (p + 1) * rows)
            for which, (src, raw, dst) in enumerate(((dq_s, qp_i, dq_o), (dk_s, kp_i, dk_o))):
                dz = turn_back(src[at, :], cos_ref[p], sin_ref[p])
                moved = raw[j, 0] * dz
                dst[j, 0] = dz
                st_o[which, 0, 0, j] = jnp.sum(moved * gain_ref[which], axis=-1, keepdims=True)
                sums[which] += jnp.sum(moved * inv[which, j, 0], axis=0, keepdims=True)
            dv_o[j, 0] = dv_s[at, :].astype(bf16)
        for which in range(2):
            dg_o[which, 0] = sums[which]

    def part(i):
        return pl.BlockSpec((n, 1, rows, HEAD_DIM), lambda g, h, *_: (0, g, 0, i * heads + h))

    line = pl.BlockSpec((1, span, HEAD_DIM), lambda g, h, *_: (g, 0, h))
    block = part(0)
    outs = (
        struct((n, seqs, rows, cols), f32),
        struct((n, seqs, rows, cols), f32),
        struct((n, seqs, rows, cols), bf16),
        struct((2, seqs, heads, n, rows, 1), f32),
        struct((2, seqs, 1, cols), f32),
    )
    return pl.pallas_call(
        kernel,
        grid_spec=pltpu.PrefetchScalarGridSpec(
            num_scalar_prefetch=2,
            grid=(seqs, heads),
            in_specs=[
                line,
                line,
                line,
                block,
                pl.BlockSpec((1, 1, span, 1), lambda g, h, *_: (g, h, 0, 0)),
                part(0),
                part(1),
                pl.BlockSpec((2, n, 1, rows, 1), lambda g, h, *_: (0, 0, g, 0, 0)),
                pl.BlockSpec((2, 1, HEAD_DIM), lambda g, h, *_: (0, 0, h)),
                whole(cosines),
                whole(sines),
            ],
            out_specs=(
                block,
                block,
                block,
                pl.BlockSpec((2, 1, 1, n, rows, 1), lambda g, h, *_: (0, g, h, 0, 0, 0)),
                pl.BlockSpec((2, 1, 1, HEAD_DIM), lambda g, h, *_: (0, g, 0, h)),
            ),
            scratch_shapes=[pltpu.VMEM((span, HEAD_DIM), f32)] * 3,
        ),
        out_shape=outs,
        compiler_params=params(2),
        cost_estimate=cost(7 * seqs * heads * span * span * HEAD_DIM, qkv, *outs[:3]),
        name="attention_back",
    )(place, lengths, q, k, v, grad, lse, qkv, qkv, inverse, gains, cosines, sines)


def picks(rank_ref, nb, cap):
    row = rank_ref[0, nb : nb + 1, :]
    return lax.broadcasted_iota(jnp.int32, (cap, row.shape[1]), 0) == row


def slot_weight(hot, coef_ref, nb):
    return jnp.sum(jnp.where(hot, coef_ref[0, nb : nb + 1, :], 0.0), axis=-1, keepdims=True)


def expert_forward(pieces, rank, gate_up, cap):
    experts, blocks, rows = rank.shape
    width, hidden = gate_up.shape[1:]
    slots = blocks * cap
    tile = min(256, hidden)
    parts = chunks_of(blocks, cap)
    part = slots // parts

    def kernel(*refs):
        xs, (rank_ref, wg, wu), (x_o, g_o, u_o, a_o) = (
            refs[:blocks],
            refs[blocks : blocks + 3],
            refs[blocks + 3 :],
        )

        @pl.when(pl.program_id(1) == 0)
        def _():
            for nb in range(blocks):
                hot = picks(rank_ref, nb, cap).astype(bf16)
                x_o[0, nb * cap : (nb + 1) * cap, :] = dot(hot, xs[nb][...]).astype(bf16)

        @pl.loop(0, parts)
        def _(i):
            at = pl.ds(pl.multiple_of(i * part, part), part)
            x = x_o[0, at, :]
            gate = dot(x, wg[0])
            upper = dot(x, wu[0])
            g_o[0, at, :] = gate.astype(bf16)
            u_o[0, at, :] = upper.astype(bf16)
            a_o[0, at, :] = (gate * jax.nn.sigmoid(gate) * upper).astype(bf16)

    tiled = pl.BlockSpec((1, slots, tile), lambda e, f: (e, 0, f))
    outs = (struct((experts, slots, width), bf16),) + (struct((experts, slots, hidden), bf16),) * 3
    return pl.pallas_call(
        kernel,
        grid=(experts, hidden // tile),
        in_specs=[whole(x) for x in pieces]
        + [
            pl.BlockSpec((1, blocks, rows), lambda e, f: (e, 0, 0)),
            pl.BlockSpec((1, width, tile), lambda e, f: (e, 0, f)),
            pl.BlockSpec((1, width, tile), lambda e, f: (experts + e, 0, f)),
        ],
        out_specs=(pl.BlockSpec((1, slots, width), lambda e, f: (e, 0, 0)), tiled, tiled, tiled),
        out_shape=outs,
        compiler_params=params(2),
        cost_estimate=cost(4 * experts * slots * width * hidden, *pieces, gate_up, *outs),
        name="expert_forward",
    )(*pieces, rank, gate_up, gate_up)


def expert_output(active, rank, coef, down, cap):
    experts, blocks, rows = rank.shape
    hidden, width = down.shape[1:]
    slots = blocks * cap
    tile = min(512, width)
    parts = chunks_of(blocks, cap)
    per = blocks // parts

    def kernel(a_i, rank_ref, coef_ref, wd, *rest):
        outs, acc = rest[:blocks], rest[blocks]
        e = pl.program_id(1)

        @pl.when(e == 0)
        def _():
            acc[...] = jnp.zeros_like(acc)

        for i in range(parts):
            y = dot(a_i[0, i * per * cap : (i + 1) * per * cap, :], wd[0])
            for m in range(per):
                nb = i * per + m
                hot = picks(rank_ref, nb, cap)
                weighed = y[m * cap : (m + 1) * cap, :] * slot_weight(hot, coef_ref, nb)
                acc[nb] += dot_tn(hot.astype(bf16), weighed.astype(bf16))

        @pl.when(e == experts - 1)
        def _():
            for nb in range(blocks):
                outs[nb][...] = acc[nb].astype(bf16)

    table = pl.BlockSpec((1, blocks, rows), lambda d, e: (e, 0, 0))
    outs = (struct((rows, width), bf16),) * blocks
    return pl.pallas_call(
        kernel,
        grid=(width // tile, experts),
        in_specs=[
            pl.BlockSpec((1, slots, hidden), lambda d, e: (e, 0, 0)),
            table,
            table,
            pl.BlockSpec((1, hidden, tile), lambda d, e: (e, 0, d)),
        ],
        out_specs=(pl.BlockSpec((rows, tile), lambda d, e: (0, d)),) * blocks,
        out_shape=outs,
        scratch_shapes=[pltpu.VMEM((blocks, rows, tile), f32)],
        compiler_params=params(2),
        cost_estimate=cost(2 * experts * slots * width * hidden, active, down, *outs),
        name="expert_output",
    )(active, rank, coef, down)


def expert_backward(pieces, rank, coef, down, gate, upper, active, cap):
    experts, blocks, rows = rank.shape
    hidden, width = down.shape[1:]
    slots = blocks * cap
    tile = min(256, hidden)
    parts = chunks_of(blocks, cap)
    part = slots // parts

    def kernel(*refs):
        ds, (rank_ref, coef_ref, wd, g_i, u_i, a_i), (dg_o, du_o, dw_o, dy) = (
            refs[:blocks],
            refs[blocks : blocks + 6],
            refs[blocks + 6 :],
        )

        @pl.when(pl.program_id(1) == 0)
        def _():
            for nb in range(blocks):
                hot = picks(rank_ref, nb, cap)
                picked = dot(hot.astype(bf16), ds[nb][...])
                dy[nb * cap : (nb + 1) * cap, :] = (
                    picked * slot_weight(hot, coef_ref, nb)
                ).astype(bf16)

        @pl.loop(0, parts)
        def _(i):
            at = pl.ds(pl.multiple_of(i * part, part), part)
            da = dot_nt(dy[at, :], wd[0])
            g = g_i[0, at, :].astype(f32)
            s = jax.nn.sigmoid(g)
            du_o[0, at, :] = (da * g * s).astype(bf16)
            dg_o[0, at, :] = (
                da * u_i[0, at, :].astype(f32) * s * (1.0 + g * (1.0 - s))
            ).astype(bf16)

        dw_o[0] = dot_tn(a_i[0], dy[...]).astype(bf16)

    table = pl.BlockSpec((1, blocks, rows), lambda e, f: (e, 0, 0))
    tiled = pl.BlockSpec((1, slots, tile), lambda e, f: (e, 0, f))
    line = pl.BlockSpec((1, tile, width), lambda e, f: (e, f, 0))
    outs = (struct((experts, slots, hidden), bf16),) * 2 + (struct((experts, hidden, width), bf16),)
    return pl.pallas_call(
        kernel,
        grid=(experts, hidden // tile),
        in_specs=[whole(x) for x in pieces] + [table, table, line, tiled, tiled, tiled],
        out_specs=(tiled, tiled, line),
        out_shape=outs,
        scratch_shapes=[pltpu.VMEM((slots, width), bf16)],
        compiler_params=params(2),
        cost_estimate=cost(
            4 * experts * slots * width * hidden, *pieces, down, gate, upper, active, *outs
        ),
        name="expert_backward",
    )(*pieces, rank, coef, down, gate, upper, active)


def expert_input_grad(dgate, dupper, rank, gate_up, cap):
    experts, blocks, rows = rank.shape
    width, hidden = gate_up.shape[1:]
    slots = blocks * cap
    tile = min(512, width)
    parts = chunks_of(blocks, cap)
    per = blocks // parts

    def kernel(dg_i, du_i, rank_ref, wg, wu, *rest):
        outs, acc = rest[:blocks], rest[blocks]
        e = pl.program_id(1)

        @pl.when(e == 0)
        def _():
            acc[...] = jnp.zeros_like(acc)

        for i in range(parts):
            at = slice(i * per * cap, (i + 1) * per * cap)
            dx = (dot_nt(dg_i[0, at, :], wg[0]) + dot_nt(du_i[0, at, :], wu[0])).astype(bf16)
            for m in range(per):
                nb = i * per + m
                hot = picks(rank_ref, nb, cap).astype(bf16)
                acc[nb] += dot_tn(hot, dx[m * cap : (m + 1) * cap, :])

        @pl.when(e == experts - 1)
        def _():
            for nb in range(blocks):
                outs[nb][...] = acc[nb].astype(bf16)

    line = pl.BlockSpec((1, slots, hidden), lambda d, e: (e, 0, 0))
    outs = (struct((rows, width), bf16),) * blocks
    return pl.pallas_call(
        kernel,
        grid=(width // tile, experts),
        in_specs=[
            line,
            line,
            pl.BlockSpec((1, blocks, rows), lambda d, e: (e, 0, 0)),
            pl.BlockSpec((1, tile, hidden), lambda d, e: (e, d, 0)),
            pl.BlockSpec((1, tile, hidden), lambda d, e: (experts + e, d, 0)),
        ],
        out_specs=(pl.BlockSpec((rows, tile), lambda d, e: (0, d)),) * blocks,
        out_shape=outs,
        scratch_shapes=[pltpu.VMEM((blocks, rows, tile), f32)],
        compiler_params=params(2),
        cost_estimate=cost(4 * experts * slots * width * hidden, dgate, dupper, gate_up, *outs),
        name="expert_input_grad",
    )(dgate, dupper, rank, gate_up, gate_up)


def expert_weight_grad(x, dgate, dupper):
    experts, slots, width = x.shape
    hidden = dgate.shape[2]
    tile = min(256, width)

    def kernel(x_i, dg_i, du_i, o):
        o[0, 0] = dot_tn(x_i[0], dg_i[0]).astype(bf16)
        o[1, 0] = dot_tn(x_i[0], du_i[0]).astype(bf16)

    line = pl.BlockSpec((1, slots, hidden), lambda e, d: (e, 0, 0))
    out = struct((2, experts, width, hidden), bf16)
    return pl.pallas_call(
        kernel,
        grid=(experts, width // tile),
        in_specs=[pl.BlockSpec((1, slots, tile), lambda e, d: (e, 0, d)), line, line],
        out_specs=pl.BlockSpec((2, 1, tile, hidden), lambda e, d: (0, e, d, 0)),
        out_shape=out,
        compiler_params=params(2),
        cost_estimate=cost(4 * experts * slots * width * hidden, x, dgate, dupper, out),
        name="expert_weight_grad",
    )(x, dgate, dupper).reshape(2 * experts, width, hidden)


def tables(positions):
    half = HEAD_DIM // 2
    inverse = THETA ** (-(jnp.arange(half, dtype=f32) * 2.0) / HEAD_DIM)
    angle = positions.astype(f32)[:, None] * inverse[None, :]
    cosines, sines = jnp.cos(angle), jnp.sin(angle)
    return (
        jnp.concatenate([cosines, cosines], axis=-1),
        jnp.concatenate([-sines, sines], axis=-1),
    )


def norm_back(v, gain, dz):
    r = lax.rsqrt(jnp.mean(v * v, axis=-1, keepdims=True) + EPS)
    moved = dz * gain
    return r * moved - v * (r * r * r) * jnp.mean(v * moved, axis=-1, keepdims=True), dz * v * r


def body(
    tokens, lengths, expert_ids, route_levels, w_query, w_key, w_value, w_out,
    attn_gain, query_gain, key_gain, ffn_gain, w_gate, w_up, w_down, cotangent,
):
    batches, sequences, rows, width = tokens.shape
    top = expert_ids.shape[-1]
    experts = w_gate.shape[0]
    n = lax.axis_size("ctx")
    groups = lax.axis_size("batch")
    here = lax.axis_index("ctx")
    seqs = batches * sequences
    cols = width // n
    own = w_query.shape[0]
    cap = rows * top * 5 // (4 * experts * n)
    cap = -(-cap // 16) * 16
    blocks = n * seqs
    up = [(i, (i + 1) % n) for i in range(n)]
    place = here.reshape(1).astype(jnp.int32)

    def gather_ring(piece):
        held = [piece]
        for _ in range(n - 1):
            held.append(lax.ppermute(held[-1], "ctx", up))
        return held

    def reduce_ring(parts):
        total = parts[1 % n]
        for j in range(2, n + 1):
            moved = lax.ppermute(total, "ctx", up).astype(f32) + parts[j % n].astype(f32)
            total = moved.astype(bf16) if j < n else moved
        return total

    def ctx_sum(x):
        total = x
        for k in range(1, n):
            got = lax.ppermute(x, "ctx", [(i, (i + k) % n) for i in range(n)])
            total = total + jnp.roll(got, k, axis=0)
        return total

    def to_owner(summed):
        pieces = summed.reshape(n, own, summed.shape[-1])
        return lax.all_to_all(pieces, "ctx", split_axis=0, concat_axis=0, tiled=True)

    mine = jnp.concatenate(
        [jnp.swapaxes(w.reshape(own, n, cols), 0, 1) for w in (w_query, w_key, w_value)], axis=2
    )
    mine = lax.all_to_all(mine, "ctx", split_axis=0, concat_axis=0, tiled=True)
    qkv_w = lax.all_gather(mine.reshape(n * own, 3 * cols), "batch", axis=0, tiled=True)
    gain_attn, gain_query, gain_key, gain_ffn = (
        lax.all_gather(g, ("batch", "ctx"), axis=0, tiled=True).astype(f32)
        for g in (attn_gain, query_gain, key_gain, ffn_gain)
    )
    out_w = lax.all_gather(w_out, ("batch", "ctx"), axis=0, tiled=True).reshape(n, cols, width)
    gate_up = lax.all_gather(
        jnp.concatenate([w_gate, w_up], axis=0), "batch", axis=1, tiled=True
    )
    down = lax.all_gather(w_down, "batch", axis=2, tiled=True)
    qk_gains = lax.dynamic_slice_in_dim(
        jnp.stack([gain_query, gain_key]), here * cols, cols, 1
    ).reshape(2, 1, cols)

    xs = tokens.reshape(seqs, rows, width)
    span_len = lengths.reshape(seqs)
    local_pos = here * rows + jnp.arange(rows, dtype=jnp.int32)
    live = (local_pos[None, :] < span_len[:, None])[:, :, None]
    x_rings = [gather_ring(xs[g]) for g in range(seqs)]
    x_pieces = [x_rings[g][j] for j in range(n) for g in range(seqs)]
    grad_low = jnp.where(live, cotangent.reshape(seqs, rows, width), jnp.zeros((), bf16))

    sent = jnp.stack(
        [
            jnp.swapaxes(expert_ids.reshape(seqs, rows, top), 1, 2),
            jnp.swapaxes(route_levels.reshape(seqs, rows, top), 1, 2),
        ]
    )
    routes = lax.all_gather(sent, "ctx", axis=0, tiled=False)
    order = lax.rem(here - jnp.arange(n, dtype=jnp.int32) + n, n)
    routes = jnp.take(routes, order, axis=0)
    chosen = routes[:, 0].reshape(blocks, top, rows)
    levels = routes[:, 1].reshape(blocks, top, rows).astype(f32)
    share = levels / jnp.sum(levels, axis=1, keepdims=True)
    owned = here * experts + jnp.arange(experts, dtype=jnp.int32)
    hit = chosen[None] == owned[:, None, None, None]
    named = jnp.any(hit, axis=2)
    coef = jnp.sum(jnp.where(hit, share[None], 0.0), axis=2)
    upto = (
        jnp.arange(rows, dtype=jnp.int32)[:, None] <= jnp.arange(rows, dtype=jnp.int32)[None, :]
    ).astype(bf16)
    count = jnp.dot(
        named.astype(bf16).reshape(experts * blocks, rows), upto, preferred_element_type=f32
    )
    rank = jnp.where(named, count.reshape(experts, blocks, rows).astype(jnp.int32) - 1, -1)

    cosines, sines = tables(jnp.arange(n * rows, dtype=jnp.int32))
    cosines = cosines.reshape(n, rows, HEAD_DIM)
    sines = sines.reshape(n, rows, HEAD_DIM)
    normed, qkv, squares = project(x_pieces, gain_attn[None, :], qkv_w)
    squares = squares[:2].reshape(2, n, seqs, rows)
    squares = ctx_sum(jnp.swapaxes(squares, 0, 1))
    inverse = lax.rsqrt(squares / width + EPS)
    inverse = jnp.swapaxes(inverse, 0, 1)[..., None]
    qkv = qkv.reshape(n, seqs, rows, 3 * cols)
    q, k, v, att, lse = attention_forward(
        place, span_len, qkv, inverse, qk_gains, cosines, sines
    )
    att = lax.all_to_all(att, "ctx", split_axis=0, concat_axis=0, tiled=True)
    hidden = xs.astype(f32) + jnp.einsum(
        "ngrd,nde->gre", att, out_w, preferred_element_type=f32
    )
    n2 = (
        hidden * lax.rsqrt(jnp.mean(hidden * hidden, axis=-1, keepdims=True) + EPS) * gain_ffn
    ).astype(bf16)

    g_rings = [gather_ring(grad_low[g]) for g in range(seqs)]
    grad_pieces = [g_rings[g][j] for j in range(n) for g in range(seqs)]
    n_rings = [gather_ring(n2[g]) for g in range(seqs)]
    n_pieces = [n_rings[g][j] for j in range(n) for g in range(seqs)]
    slots_x, gate, upper, active = expert_forward(n_pieces, rank, gate_up, cap)
    y_parts = expert_output(active, rank, coef, down, cap)
    mixture = jnp.stack(
        [reduce_ring([y_parts[j * seqs + g] for j in range(n)]) for g in range(seqs)]
    )
    out = jnp.where(live, hidden + mixture, 0.0).astype(bf16)

    dgate, dupper, grad_down = expert_backward(
        grad_pieces, rank, coef, down, gate, upper, active, cap
    )
    grad_down = lax.psum_scatter(grad_down, "batch", scatter_dimension=2, tiled=True)
    dx_parts = expert_input_grad(dgate, dupper, rank, gate_up, cap)
    grad_gu = expert_weight_grad(slots_x, dgate, dupper)
    grad_gu = lax.psum_scatter(grad_gu, "batch", scatter_dimension=1, tiled=True)
    grad_mid = jnp.stack(
        [reduce_ring([dx_parts[j * seqs + g] for j in range(n)]) for g in range(seqs)]
    )
    back, ffn_terms = norm_back(hidden, gain_ffn, grad_mid)
    grad_hidden = grad_low.astype(f32) + back
    ffn_part = jnp.sum(ffn_terms, axis=(0, 1))
    datt = grad_hidden.astype(bf16)

    do = jnp.einsum("gre,nde->ngrd", datt, out_w, preferred_element_type=f32).astype(bf16)
    do = lax.all_to_all(do, "ctx", split_axis=0, concat_axis=0, tiled=True)
    grad_out = jnp.einsum("ngrd,gre->nde", att, datt, preferred_element_type=f32)
    grad_out = grad_out.astype(bf16).reshape(width, width)
    column = jnp.pad(ffn_part.astype(bf16)[:, None], ((0, 0), (0, LANES - 1)))
    grad_out = lax.psum_scatter(
        jnp.concatenate([grad_out, column], axis=1), "batch", scatter_dimension=0, tiled=True
    )
    grad_out = jnp.sum(to_owner(grad_out).astype(f32), axis=0)

    dzq, dzk, dv, stats, qk_part = attention_backward(
        place, span_len, q, k, v, do, lse, qkv, inverse, qk_gains, cosines, sines
    )
    stats = jnp.sum(stats[..., 0], axis=2)
    stats = ctx_sum(jnp.transpose(stats, (2, 0, 1, 3)))
    stats = jnp.swapaxes(stats, 0, 1)[..., None] / width

    def through_norm(which, dz):
        r = inverse[which]
        raw = qkv[..., which * cols : (which + 1) * cols]
        return (r * qk_gains[which] * dz - raw * (r * r * r) * stats[which]).astype(bf16)

    dqkv = jnp.concatenate([through_norm(0, dzq), through_norm(1, dzk), dv], axis=-1)
    dqkv = dqkv.reshape(blocks * rows, 3 * cols)
    dn1 = dot_nt(dqkv, qkv_w).astype(bf16).reshape(n, seqs, rows, width)
    grad_n1 = jnp.stack([reduce_ring([dn1[j, g] for j in range(n)]) for g in range(seqs)])
    back, _ = norm_back(xs.astype(f32), gain_attn, grad_n1)
    grad_tokens = grad_hidden + back

    grad_qkv = dot_tn(normed, dqkv).astype(bf16)
    qk_rows = lax.dynamic_update_slice_in_dim(
        jnp.zeros((2, width), f32), jnp.sum(qk_part, axis=(1, 2)), here * cols, 1
    )
    qk_column = jnp.pad(qk_rows.T.astype(bf16), ((0, 0), (0, LANES - 2)))
    grad_qkv = lax.psum_scatter(
        jnp.concatenate([grad_qkv, qk_column], axis=1), "batch", scatter_dimension=0, tiled=True
    )
    grad_qkv = to_owner(grad_qkv).astype(f32)
    grad_q, grad_k, grad_v = (
        jnp.swapaxes(grad_qkv[:, :, i * cols : (i + 1) * cols], 0, 1).reshape(own, width)
        for i in range(3)
    )
    qk_sums = jnp.sum(grad_qkv[:, :, 3 * cols :], axis=0)
    grad_attn_gain = (
        jnp.sum(
            w_query.astype(f32) * grad_q
            + w_key.astype(f32) * grad_k
            + w_value.astype(f32) * grad_v,
            axis=1,
        )
        / attn_gain.astype(f32)
    )
    shape = (batches, sequences, rows, width)
    return (
        out.reshape(shape),
        grad_tokens.reshape(shape),
        grad_q,
        grad_k,
        grad_v,
        grad_out[:, :width],
        grad_attn_gain,
        qk_sums[:, 0],
        qk_sums[:, 1],
        grad_out[:, width],
        grad_gu[:experts].astype(f32),
        grad_gu[experts:].astype(f32),
        grad_down.astype(f32),
    )


def solution(mesh):
    rows = P(None, "batch", "ctx", None)
    flat = P(("batch", "ctx"), None)
    line = P(("batch", "ctx"))
    wide = P("ctx", "batch", None)
    tall = P("ctx", None, "batch")
    in_specs = (rows, P(None, "batch"), rows, rows) + (flat,) * 4 + (line,) * 4
    in_specs += (wide, wide, tall, rows)
    out_specs = (rows, rows) + (flat,) * 4 + (line,) * 4 + (wide, wide, tall)
    return jax.shard_map(body, mesh=mesh, in_specs=in_specs, out_specs=out_specs, check_vma=False)
```

time: 5180 us -> 1690 us (0.33)
  waiting for transfers between devices: 3840 us -> 870 us
  matrix products: 635 us -> 60.8 us
  Pallas kernels: 0 us -> 415 us
  local copies, waits for them, and re-layouts: 330 us -> 24.1 us
  other arithmetic: 202 us -> 68.2 us
  blocking collectives: 86.7 us -> 184 us
    reduce_scatter x12 -> x4, waiting for transfers between devices: 2050 us -> 175 us  [the longest x1 175 us: body(): lax.psum_scatter(grad_gu, 'batch', scatter_dimension=1, tiled=True)]
    all_to_all x8 -> x4, waiting for transfers between devices: 1050 us -> 115 us  [the longest x1 47.6 us: body(): att = lax.all_to_all(att, 'ctx', split_axis=0, concat_axis=0, tiled=True)]
    all_gather x11 -> x4, waiting for transfers between devices: 731 us -> 0.04 us  [the longest x1 0.02 us: body(): down = lax.all_gather(w_down, 'batch', axis=2, tiled=True)]
    ppermute x0 -> x42, waiting for transfers between devices: none -> 579 us  [the longest x18 340 us: reduce_ring(): lax.ppermute(total, 'ctx', up).astype(f32) + parts[j % n].astype(f32)]
    dot_general x54 -> x6, matrix products: 635 us -> 60.8 us  [the longest x2 34.9 us: dot(): lax.dot_general(left, right, (contract, ((), ())), preferred_element_type...]
    pallas_call x0 -> x8, Pallas kernels: none -> 415 us  [the longest x1 69.7 us: expert_backward(): pl.pallas_call(kernel, grid=(experts, hidden // tile), in_specs=[whole(x)...]
    gather x8 -> x1, local copies, waits for them, and re-layouts: 159 us -> 0.56 us  [body(): routes = jnp.take(routes, order, axis=0)]
    all_gather x0 -> x1, blocking collectives: none -> 95.9 us  [body(): routes = lax.all_gather(sent, 'ctx', axis=0, tiled=False)]
  transfers between devices with their start and end apart: 31 -> 54, of which waited for: 28 -> 33; matrix products, arithmetic and copies ran while one was open for 18% -> 5% of each run, Pallas kernels for 0% -> 14%
where the time goes in v1:
time: 1690 us
  waiting for transfers between devices  870 us (51%)
  Pallas kernels  415 us (25%)
  blocking collectives  184 us (11%)
  other arithmetic  68.2 us (4%)
  matrix products  60.8 us (4%)
  starting transfers between devices  47.8 us (3%)
  local copies, waits for them, and re-layouts  24.1 us (1%)
    ppermute x18, waiting for transfers between devices, reduce_ring(): lax.ppermute(total, 'ctx', up).astype(f32) + parts[j % n].astype(f32)  340 us
    ppermute x18, waiting for transfers between devices, gather_ring(): held.append(lax.ppermute(held[-1], 'ctx', up))  234 us
    reduce_scatter x1, waiting for transfers between devices, body(): lax.psum_scatter(grad_gu, 'batch', scatter_dimension=1, tiled=True)  175 us
    all_gather x1, blocking collectives, body(): routes = lax.all_gather(sent, 'ctx', axis=0, tiled=False)  95.9 us
    pallas_call x1, Pallas kernels, expert_backward(): pl.pallas_call(kernel, grid=(experts, hidden // tile), in_specs=[whole(x)...  69.7 us
    pallas_call x1, Pallas kernels, expert_forward(): pl.pallas_call(kernel, grid=(experts, hidden // tile), in_specs=[whole(x)...  64 us
    pallas_call x1, Pallas kernels, expert_input_grad(): pl.pallas_call(kernel, grid=(width // tile, experts), in_specs=[line, lin...  63 us
    unnamed x1, blocking collectives  62 us
  transfers between devices with their start and end apart: 54, of which 33 were waited for; matrix products, arithmetic and copies ran while one was open for 5% of the time, Pallas kernels for 14%

profile of v1, /device:TPU:0, one launch (start us, length us, event | category | flops | bytes accessed | tf_op | source)
XLA Modules:
  0.0 1685.6 jit_solution(9938095456022006127)
XLA Ops:
  9.5 26.3 %all_to_all.25 = bf16[4,64,1536]{2,1,0:T(8,128)(2,1)} all-to-all(bf16[4,64,1536]{2,1,0:T(8,128)(2,1)S(1)} %pad_maximum_fusion.3), channel_id=1, replica_groups=mesh['batch'=8,'ctx'=4] {'ctx'}, dimensions={0} | all-to-all | bytes 1572864 | tf_op jit(solution)/shard_map/all_to_all | solution.py:581
  43.3 27.3 %collective-permute-done.refs_2_ = bf16[256,2048]{1,0:T(8,128)(2,1)S(1)} collective-permute-done((bf16[256,2048]{1,0:T(8,128)(2,1)S(1)}, bf16[256,2048]{1,0:T(8,128)(2,1)S(1)}, u32[]{:S(2)}, u32[]{:S(2)}) %collective-permute-start) | collective-permute-done | bytes 1048608 | tf_op jit(solution)/shard_map/ppermute | solution.py:557
  70.6 22.5 %collective-permute-done.1.refs_3_ = bf16[256,2048]{1,0:T(8,128)(2,1)S(1)} collective-permute-done((bf16[256,2048]{1,0:T(8,128)(2,1)S(1)}, bf16[256,2048]{1,0:T(8,128)(2,1)S(1)}, u32[]{:S(2)}, u32[]{:S(2)}) %collective-permute-start.1) | collective-permute-done | bytes 1048608 | tf_op jit(solution)/shard_map/ppermute | solution.py:557
  93.0 28.2 %collective-permute-done.2.refs_4_ = bf16[256,2048]{1,0:T(8,128)(2,1)} collective-permute-done((bf16[256,2048]{1,0:T(8,128)(2,1)S(1)}, bf16[256,2048]{1,0:T(8,128)(2,1)}, u32[]{:S(2)}, u32[]{:S(2)}) %collective-permute-start.2) | collective-permute-done | bytes 1048608 | tf_op jit(solution)/shard_map/ppermute | solution.py:557
  121.2 22.5 %collective-permute-done.3.refs_5_ = bf16[256,2048]{1,0:T(8,128)(2,1)} collective-permute-done((bf16[256,2048]{1,0:T(8,128)(2,1)S(1)}, bf16[256,2048]{1,0:T(8,128)(2,1)}, u32[]{:S(2)}, u32[]{:S(2)}) %collective-permute-start.3) | collective-permute-done | bytes 1048608 | tf_op jit(solution)/shard_map/ppermute | solution.py:557
  144.7 62.0 %all-reduce.6 = (bf16[2048]{0:T(1024)(128)(2,1)S(1)}, bf16[2048]{0:T(1024)(128)(2,1)S(1)}, bf16[2048]{0:T(1024)(128)(2,1)S(1)}, bf16[2048]{0:T(1024)(128)(2,1)S(1)}) all-reduce(bf16[2048]{0:T(1024)(128)(2,1)S(1)} %dynamic-update-slice, bf16[2048]{0:T(1024)(128)(2,1)S(1)} %dynamic-update-slice.2, ...), channel_id=1, replica_groups=mesh['batch'=8,'ctx'=4] {'batch','ctx'}, use_global_device_ids=true, to_apply=%add.2 | all-reduce | flops 8192 | bytes 32768
  210.6 34.7 %project.1 = (bf16[2048,2048]{1,0:T(8,128)(2,1)}, f32[2048,1536]{1,0:T(8,128)}, f32[3,2048,1]{2,1,0:T(8,128)}) custom-call(bf16[256,2048]{1,0:T(8,128)(2,1)} %copy-done.39, bf16[256,2048]{1,0:T(8,128)(2,1)} %copy-done.38, bf16[256,2048]{1,0:T(8,128)(2,1)} %copy-done.56, bf16[256,2048]{1,0:T(8,128)(2,1)} %copy-done.57, ...), custom_call_target="tpu_custom_call" | custom-call | flops 12884901888 | bytes 35651584 | tf_op jit(solution)/shard_map/project/pallas_call | solution.py:96
  257.1 29.7 %attention.1 = (bf16[2,1024,512]{2,1,0:T(8,128)(2,1)}, bf16[2,1024,512]{2,1,0:T(8,128)(2,1)}, bf16[2,1024,512]{2,1,0:T(8,128)(2,1)}, bf16[4,2,256,512]{3,2,1,0:T(8,128)(2,1)}, f32[2,4,1024,1]{3,2,1,0:T(8,128)}) custom-call(s32[1]{0:T(128)} %bitcast.3.place_ref, s32[2]{0:T(128)} %bitcast.242, f32[4,2,256,1536]{3,2,1,0:T(8,128)} %bitcast.198, ...), custom_call_target="tpu_custom_call" | custom-call | flops 3221225472 | bytes 20971520 | tf_op jit(solution)/shard_map/attention/pallas_call | solution.py:163
  292.0 47.6 %all-to-all-done.1 = bf16[4,2,256,512]{3,2,1,0:T(8,128)(2,1)} async-done(((bf16[4,2,256,512]{3,2,1,0:T(8,128)(2,1)}), bf16[4,2,256,512]{3,2,1,0:T(8,128)(2,1)}, u32[]{:S(2)}, u32[]{:S(2)}) %all-to-all-start.1) | async-done | bytes 2097184 | tf_op jit(solution)/shard_map/all_to_all | solution.py:640
  354.9 22.5 %collective-permute-done.9.refs_2_ = bf16[256,2048]{1,0:T(8,128)(2,1)} collective-permute-done((bf16[256,2048]{1,0:T(8,128)(2,1)S(1)}, bf16[256,2048]{1,0:T(8,128)(2,1)}, u32[]{:S(2)}, u32[]{:S(2)}) %collective-permute-start.9) | collective-permute-done | bytes 1048608 | tf_op jit(solution)/shard_map/ppermute | solution.py:557
  377.4 22.5 %collective-permute-done.10.refs_3_ = bf16[256,2048]{1,0:T(8,128)(2,1)} collective-permute-done((bf16[256,2048]{1,0:T(8,128)(2,1)S(1)}, bf16[256,2048]{1,0:T(8,128)(2,1)}, u32[]{:S(2)}, u32[]{:S(2)}) %collective-permute-start.10) | collective-permute-done | bytes 1048608 | tf_op jit(solution)/shard_map/ppermute | solution.py:557
  399.9 95.9 %all-gather = s32[8,2,8,256]{3,2,1,0:T(8,128)S(1)} all-gather(s32[2,2,8,256]{3,2,1,0:T(8,128)S(1)} %pad_add_fusion), channel_id=2, replica_groups=mesh['batch'=8,'ctx'=4] {'ctx'}, dimensions={0}, use_global_device_ids=true | all-gather | bytes 163840 | tf_op jit(solution)/shard_map/all_gather | solution.py:610
  524.9 22.5 %collective-permute-done.24.refs_5_ = bf16[256,2048]{1,0:T(8,128)(2,1)} collective-permute-done((bf16[256,2048]{1,0:T(8,128)(2,1)}, bf16[256,2048]{1,0:T(8,128)(2,1)}, u32[]{:S(2)}, u32[]{:S(2)}) %collective-permute-start.24) | collective-permute-done | bytes 1048608 | tf_op jit(solution)/shard_map/ppermute | solution.py:557
  547.3 22.5 %collective-permute-done.13.refs_6_ = bf16[256,2048]{1,0:T(8,128)(2,1)} collective-permute-done((bf16[256,2048]{1,0:T(8,128)(2,1)}, bf16[256,2048]{1,0:T(8,128)(2,1)}, u32[]{:S(2)}, u32[]{:S(2)}) %collective-permute-start.13) | collective-permute-done | bytes 1048608 | tf_op jit(solution)/shard_map/ppermute | solution.py:557
  569.8 22.5 %collective-permute-done.14.refs_7_ = bf16[256,2048]{1,0:T(8,128)(2,1)} collective-permute-done((bf16[256,2048]{1,0:T(8,128)(2,1)S(1)}, bf16[256,2048]{1,0:T(8,128)(2,1)}, u32[]{:S(2)}, u32[]{:S(2)}) %collective-permute-start.14) | collective-permute-done | bytes 1048608 | tf_op jit(solution)/shard_map/ppermute | solution.py:557
  592.3 64.0 %expert_forward.1 = (bf16[4,1280,2048]{2,1,0:T(8,128)(2,1)}, bf16[4,1280,1024]{2,1,0:T(8,128)(2,1)}, bf16[4,1280,1024]{2,1,0:T(8,128)(2,1)}, bf16[4,1280,1024]{2,1,0:T(8,128)(2,1)}) custom-call(bf16[256,2048]{1,0:T(8,128)(2,1)} %copy-done.34, bf16[256,2048]{1,0:T(8,128)(2,1)} %copy-done.33, bf16[256,2048]{1,0:T(8,128)(2,1)} %collective-permute-done.9.refs_2_, ...), custom_call_target="tpu_custom_call" | custom-call | flops 42949672960 | bytes 94371840 | tf_op jit(solution)/shard_map/expert_forward/pallas_call | solution.py:323
  656.4 69.7 %expert_backward.1 = (bf16[4,1280,1024]{2,1,0:T(8,128)(2,1)}, bf16[4,1280,1024]{2,1,0:T(8,128)(2,1)}, bf16[4,1024,2048]{2,1,0:T(8,128)(2,1)}) custom-call(bf16[256,2048]{1,0:T(8,128)(2,1)} %copy-done.31, bf16[256,2048]{1,0:T(8,128)(2,1)} %copy-done.30, bf16[256,2048]{1,0:T(8,128)(2,1)} %collective-permute-done.21.refs_2_, ...), custom_call_target="tpu_custom_call" | custom-call | flops 42949672960 | bytes 94371840 | tf_op jit(solution)/shard_map/expert_backward/pallas_call | solution.py:430
  726.1 63.0 %expert_input_grad.1 = (bf16[256,2048]{1,0:T(8,128)(2,1)}, bf16[256,2048]{1,0:T(8,128)(2,1)}, bf16[256,2048]{1,0:T(8,128)(2,1)}, bf16[256,2048]{1,0:T(8,128)(2,1...) custom-call(bf16[4,1280,1024]{2,1,0:T(8,128)(2,1)} %get-tuple-elemen, ...), custom_call_target="tpu_custom_call" | custom-call | flops 42949672960 | bytes 62914560 | tf_op jit(solution)/shard_map/expert_input_grad/pallas_call | solution.py:476
  789.4 41.0 %expert_output.1 = (bf16[256,2048]{1,0:T(8,128)(2,1)}, bf16[256,2048]{1,0:T(8,128)(2,1)}, bf16[256,2048]{1,0:T(8,128)(2,1)}, bf16[256,2048]{1,0:T(8,128)(2,1)}, ...) custom-call(bf16[4,1280,1024]{2,1,0:T(8,128)(2,1)} %get-tuple-elemen, ...), custom_call_target="tpu_custom_call" | custom-call | flops 21474836480 | bytes 35651584 | tf_op jit(solution)/shard_map/expert_output/pallas_call | solution.py:371
  836.4 22.2 %collective-permute-done.18 = bf16[256,2048]{1,0:T(8,128)(2,1)S(1)} collective-permute-done((bf16[256,2048]{1,0:T(8,128)(2,1)}, bf16[256,2048]{1,0:T(8,128)(2,1)S(1)}, u32[]{:S(2)}, u32[]{:S(2)}) %collective-permute-start.18) | collective-permute-done | bytes 1048608 | tf_op jit(solution)/shard_map/ppermute | solution.py:563
  904.3 21.7 %collective-permute-done.28 = bf16[256,2048]{1,0:T(8,128)(2,1)S(1)} collective-permute-done((bf16[256,2048]{1,0:T(8,128)(2,1)S(1)}, bf16[256,2048]{1,0:T(8,128)(2,1)S(1)}, u32[]{:S(2)}, u32[]{:S(2)}) %collective-permute-start.28) | collective-permute-done | bytes 1048608 | tf_op jit(solution)/shard_map/ppermute | solution.py:563
  926.8 21.7 %collective-permute-done.19 = bf16[256,2048]{1,0:T(8,128)(2,1)S(1)} collective-permute-done((bf16[256,2048]{1,0:T(8,128)(2,1)S(1)}, bf16[256,2048]{1,0:T(8,128)(2,1)S(1)}, u32[]{:S(2)}, u32[]{:S(2)}) %collective-permute-start.19) | collective-permute-done | bytes 1048608 | tf_op jit(solution)/shard_map/ppermute | solution.py:563
  949.3 21.7 %collective-permute-done.16 = bf16[256,2048]{1,0:T(8,128)(2,1)S(1)} collective-permute-done((bf16[256,2048]{1,0:T(8,128)(2,1)S(1)}, bf16[256,2048]{1,0:T(8,128)(2,1)S(1)}, u32[]{:S(2)}, u32[]{:S(2)}) %collective-permute-start.16) | collective-permute-done | bytes 1048608 | tf_op jit(solution)/shard_map/ppermute | solution.py:563
  971.7 21.7 %collective-permute-done.32 = bf16[256,2048]{1,0:T(8,128)(2,1)S(1)} collective-permute-done((bf16[256,2048]{1,0:T(8,128)(2,1)S(1)}, bf16[256,2048]{1,0:T(8,128)(2,1)S(1)}, u32[]{:S(2)}, u32[]{:S(2)}) %collective-permute-start.32) | collective-permute-done | bytes 1048608 | tf_op jit(solution)/shard_map/ppermute | solution.py:563
  993.8 22.1 %collective-permute-done.29 = bf16[256,2048]{1,0:T(8,128)(2,1)S(1)} collective-permute-done((bf16[256,2048]{1,0:T(8,128)(2,1)S(1)}, bf16[256,2048]{1,0:T(8,128)(2,1)S(1)}, u32[]{:S(2)}, u32[]{:S(2)}) %collective-permute-start.29) | collective-permute-done | bytes 1048608 | tf_op jit(solution)/shard_map/ppermute | solution.py:563
  1068.9 40.8 %all-to-all-done.2.do_i = bf16[4,2,256,512]{3,2,1,0:T(8,128)(2,1)S(1)} async-done(((bf16[4,2,256,512]{3,2,1,0:T(8,128)(2,1)}), bf16[4,2,256,512]{3,2,1,0:T(8,128)(2,1)S(1)}, u32[]{:S(2)}, u32[]{:S(2)}) %all-to-all-start.2) | async-done | bytes 2097184 | tf_op jit(solution)/shard_map/all_to_all | solution.py:675
  1111.1 51.1 %attention_back.1 = (f32[4,2,256,512]{3,2,1,0:T(8,128)}, f32[4,2,256,512]{3,2,1,0:T(8,128)}, bf16[4,2,256,512]{3,2,1,0:T(8,128)(2,1)}, f32[2,2,4,4,256,1]{5,4,3,2,1,0:T(8,128)}, f32[2,2,1,512]{3,2,1,0:T(1,128)}) custom-call(s32[1]{0:T(128)} %bitcast.3.place_ref, s32[2]{0:T(128)} %bitcast.243, bf16[2,1024,512]{2,1,0:T(8,128)(2,1)} %get-tuple-element.73.q_i, ...), custom_call_target="tpu_custom_call" | custom-call | flops 7516192768 | bytes 23068672 | tf_op jit(solution)/shard_map/attention_back/pallas_call | solution.py:247
  1223.2 61.5 %expert_weight_grad.1 = bf16[2,4,2048,1024]{3,2,1,0:T(8,128)(2,1)} custom-call(bf16[4,1280,2048]{2,1,0:T(8,128)(2,1)} %get-tuple-element.83.x_i, bf16[4,1280,1024]{2,1,0:T(8,128)(2,1)} %get-tuple-element.63.dg_i, bf16[4,1280,1024]{2,1,0:T(8,128)(2,1)} %get-tuple-element.64.du_i), custom_call_target="tpu_custom_call" | custom-call | flops 42949672960 | bytes 75497472 | tf_op jit(solution)/shard_map/expert_weight_grad/pallas_call | solution.py:506
  1304.6 25.7 %collective-permute-done.36 = bf16[256,2048]{1,0:T(8,128)(2,1)S(1)} collective-permute-done((bf16[256,2048]{1,0:T(8,128)(2,1)S(1)}, bf16[256,2048]{1,0:T(8,128)(2,1)S(1)}, u32[]{:S(2)}, u32[]{:S(2)}) %collective-permute-start.36) | collective-permute-done | bytes 1048608 | tf_op jit(solution)/shard_map/ppermute | solution.py:563
  1350.3 26.8 %collective-permute-done.37 = bf16[256,2048]{1,0:T(8,128)(2,1)S(1)} collective-permute-done((bf16[256,2048]{1,0:T(8,128)(2,1)S(1)}, bf16[256,2048]{1,0:T(8,128)(2,1)S(1)}, u32[]{:S(2)}, u32[]{:S(2)}) %collective-permute-start.37) | collective-permute-done | bytes 1048608 | tf_op jit(solution)/shard_map/ppermute | solution.py:563
  1424.8 22.4 %collective-permute-done.41 = bf16[256,2048]{1,0:T(8,128)(2,1)} collective-permute-done((bf16[256,2048]{1,0:T(8,128)(2,1)}, bf16[256,2048]{1,0:T(8,128)(2,1)}, u32[]{:S(2)}, u32[]{:S(2)}) %collective-permute-start.41) | collective-permute-done | bytes 1048608 | tf_op jit(solution)/shard_map/ppermute | solution.py:563
  1497.4 174.5 %reduce-scatter.9.cloned.1.call-done = bf16[8,256,1024]{2,1,0:T(8,128)(2,1)} async-done(((bf16[8,2048,1024]{2,1,0:T(8,128)(2,1)}), bf16[8,256,1024]{2,1,0:T(8,128)(2,1)}) %reduce-scatter.9.cloned.1.call-update) | async-done | bytes 4194320 | tf_op jit(solution)/shard_map/reduce_scatter | solution.py:665
  (349 shorter events, 389.1 us)
Async XLA Ops:
  7.2 203.4 %all-gather.6.cloned.1.call-start = ((), (), s32[]{:S(2)}) async-start(), calls=%async_computation.9 | async-start | bytes 7077888 | tf_op jit(solution)/shard_map/all_gather | solution.py:582
  35.8 303.8 %all-gather.8.cloned.1.call-start = ((), (), s32[]{:S(2)}) async-start(), calls=%async_computation.10 | async-start | bytes 8650752 | tf_op jit(solution)/shard_map/all_gather | solution.py:587
  36.6 555.7 %all-gather.10.cloned.1.call-start = ((), (), s32[]{:S(2)}) async-start(), calls=%async_computation.11 | async-start | bytes 37748736 | tf_op jit(solution)/shard_map/all_gather | solution.py:588
  40.7 615.7 %all-gather.12.cloned.1.call-start = ((), (), s32[]{:S(2)}) async-start(), calls=%async_computation.12 | async-start | bytes 18874368 | tf_op jit(solution)/shard_map/all_gather | solution.py:591
  70.6 50.7 %collective-permute-start.2 = (bf16[256,2048]{1,0:T(8,128)(2,1)S(1)}, bf16[256,2048]{1,0:T(8,128)(2,1)}, u32[]{:S(2)}, u32[]{:S(2)}) collective-permute-start(bf16[256,2048]{1,0:T(8,128)(2,1)S(1)} %collective-permute-done.refs_2_), channel_id=1, source_target_pairs={{0,1},{1,2},{2,3},{3,0},{4,5},{5,6},{6,7},{7,4},{8,9},{9,10},{10,1... | collective-permute-start | bytes 3145736 | tf_op jit(solution)/shard_map/ppermute | solution.py:557
  93.0 50.6 %collective-permute-start.3 = (bf16[256,2048]{1,0:T(8,128)(2,1)S(1)}, bf16[256,2048]{1,0:T(8,128)(2,1)}, u32[]{:S(2)}, u32[]{:S(2)}) collective-permute-start(bf16[256,2048]{1,0:T(8,128)(2,1)S(1)} %collective-permute-done.1.refs_3_), channel_id=1, source_target_pairs={{0,1},{1,2},{2,3},{3,0},{4,5},{5,6},{6,7},{7,4},{8,9},{9,10},{10,1... | collective-permute-start | bytes 3145736 | tf_op jit(solution)/shard_map/ppermute | solution.py:557
  121.2 89.4 %collective-permute-start.4 = (bf16[256,2048]{1,0:T(8,128)(2,1)}, bf16[256,2048]{1,0:T(8,128)(2,1)}, u32[]{:S(2)}, u32[]{:S(2)}) collective-permute-start(bf16[256,2048]{1,0:T(8,128)(2,1)} %collective-permute-done.2.refs_4_), channel_id=1, source_target_pairs={{0,1},{1,2},{2,3},{3,0},{4,5},{5,6},{6,7},{7,4},{8,9},{9,10},{10,1... | collective-permute-start | bytes 3145736 | tf_op jit(solution)/shard_map/ppermute | solution.py:557
  143.7 66.9 %collective-permute-start.5 = (bf16[256,2048]{1,0:T(8,128)(2,1)}, bf16[256,2048]{1,0:T(8,128)(2,1)}, u32[]{:S(2)}, u32[]{:S(2)}) collective-permute-start(bf16[256,2048]{1,0:T(8,128)(2,1)} %collective-permute-done.3.refs_5_), channel_id=1, source_target_pairs={{0,1},{1,2},{2,3},{3,0},{4,5},{5,6},{6,7},{7,4},{8,9},{9,10},{10,1... | collective-permute-start | bytes 3145736 | tf_op jit(solution)/shard_map/ppermute | solution.py:557
  286.9 52.8 %all-to-all-start.1 = ((bf16[4,2,256,512]{3,2,1,0:T(8,128)(2,1)}), bf16[4,2,256,512]{3,2,1,0:T(8,128)(2,1)}, u32[]{:S(2)}, u32[]{:S(2)}) async-start(bf16[4,2,256,512]{3,2,1,0:T(8,128)(2,1)} %get-tuple-element.51), calls=%async_computation.1 | async-start | bytes 4194304 | tf_op jit(solution)/shard_map/all_to_all | solution.py:640
  351.1 145.4 %collective-permute-start.21 = (bf16[256,2048]{1,0:T(8,128)(2,1)S(1)}, bf16[256,2048]{1,0:T(8,128)(2,1)}, u32[]{:S(2)}, u32[]{:S(2)}) collective-permute-start(bf16[256,2048]{1,0:T(8,128)(2,1)S(1)} %get-tuple-element.188.refs_0_), channel_id=1, source_target_pairs={{0,1},{1,2},{2,3},{3,0},{4,5},{5,6},{6,7},{7,4},{8,9},{9,10},{10,1... | collective-permute-start | bytes 3145736 | tf_op jit(solution)/shard_map/ppermute | solution.py:557
  352.5 144.1 %collective-permute-start.22 = (bf16[256,2048]{1,0:T(8,128)(2,1)S(1)}, bf16[256,2048]{1,0:T(8,128)(2,1)}, u32[]{:S(2)}, u32[]{:S(2)}) collective-permute-start(bf16[256,2048]{1,0:T(8,128)(2,1)S(1)} %get-tuple-element.187.refs_1_), channel_id=1, source_target_pairs={{0,1},{1,2},{2,3},{3,0},{4,5},{5,6},{6,7},{7,4},{8,9},{9,10},{10,1... | collective-permute-start | bytes 3145736 | tf_op jit(solution)/shard_map/ppermute | solution.py:557
  377.4 120.4 %collective-permute-start.11 = (bf16[256,2048]{1,0:T(8,128)(2,1)}, bf16[256,2048]{1,0:T(8,128)(2,1)}, u32[]{:S(2)}, u32[]{:S(2)}) collective-permute-start(bf16[256,2048]{1,0:T(8,128)(2,1)} %collective-permute-done.9.refs_2_), channel_id=1, source_target_pairs={{0,1},{1,2},{2,3},{3,0},{4,5},{5,6},{6,7},{7,4},{8,9},{9,10},{10,1... | collective-permute-start | bytes 3145736 | tf_op jit(solution)/shard_map/ppermute | solution.py:557
  399.9 98.0 %collective-permute-start.12 = (bf16[256,2048]{1,0:T(8,128)(2,1)}, bf16[256,2048]{1,0:T(8,128)(2,1)S(1)}, u32[]{:S(2)}, u32[]{:S(2)}) collective-permute-start(bf16[256,2048]{1,0:T(8,128)(2,1)} %collective-permute-done.10.refs_3_), channel_id=1, source_target_pairs={{0,1},{1,2},{2,3},{3,0},{4,5},{5,6},{6,7},{7,4},{8,9},{9,10},{10,1... | collective-permute-start | bytes 3145736 | tf_op jit(solution)/shard_map/ppermute | solution.py:557
  496.7 50.7 %collective-permute-start.24 = (bf16[256,2048]{1,0:T(8,128)(2,1)}, bf16[256,2048]{1,0:T(8,128)(2,1)}, u32[]{:S(2)}, u32[]{:S(2)}) collective-permute-start(bf16[256,2048]{1,0:T(8,128)(2,1)} %collective-permute-done.22.refs_3_), channel_id=1, source_target_pairs={{0,1},{1,2},{2,3},{3,0},{4,5},{5,6},{6,7},{7,4},{8,9},{9,10},{10,1... | collective-permute-start | bytes 3145736 | tf_op jit(solution)/shard_map/ppermute | solution.py:557
  497.8 72.0 %collective-permute-start.13 = (bf16[256,2048]{1,0:T(8,128)(2,1)}, bf16[256,2048]{1,0:T(8,128)(2,1)}, u32[]{:S(2)}, u32[]{:S(2)}) collective-permute-start(bf16[256,2048]{1,0:T(8,128)(2,1)} %collective-permute-done.11.refs_4_), channel_id=1, source_target_pairs={{0,1},{1,2},{2,3},{3,0},{4,5},{5,6},{6,7},{7,4},{8,9},{9,10},{10,1... | collective-permute-start | bytes 3145736 | tf_op jit(solution)/shard_map/ppermute | solution.py:557
  497.9 94.4 %collective-permute-start.14 = (bf16[256,2048]{1,0:T(8,128)(2,1)S(1)}, bf16[256,2048]{1,0:T(8,128)(2,1)}, u32[]{:S(2)}, u32[]{:S(2)}) collective-permute-start(bf16[256,2048]{1,0:T(8,128)(2,1)S(1)} %collective-permute-done.12.refs_5_), channel_id=1, source_target_pairs={{0,1},{1,2},{2,3},{3,0},{4,5},{5,6},{6,7},{7,4},{8,9},{9,10},{10,1... | collective-permute-start | bytes 3145736 | tf_op jit(solution)/shard_map/ppermute | solution.py:557
  524.9 131.5 %collective-permute-start.25 = (bf16[256,2048]{1,0:T(8,128)(2,1)}, bf16[256,2048]{1,0:T(8,128)(2,1)}, u32[]{:S(2)}, u32[]{:S(2)}) collective-permute-start(bf16[256,2048]{1,0:T(8,128)(2,1)} %collective-permute-done.23.refs_4_), channel_id=1, source_target_pairs={{0,1},{1,2},{2,3},{3,0},{4,5},{5,6},{6,7},{7,4},{8,9},{9,10},{10,1... | collective-permute-start | bytes 3145736 | tf_op jit(solution)/shard_map/ppermute | solution.py:557
  547.3 109.0 %collective-permute-start.26 = (bf16[256,2048]{1,0:T(8,128)(2,1)}, bf16[256,2048]{1,0:T(8,128)(2,1)}, u32[]{:S(2)}, u32[]{:S(2)}) collective-permute-start(bf16[256,2048]{1,0:T(8,128)(2,1)} %collective-permute-done.24.refs_5_), channel_id=1, source_target_pairs={{0,1},{1,2},{2,3},{3,0},{4,5},{5,6},{6,7},{7,4},{8,9},{9,10},{10,1... | collective-permute-start | bytes 3145736 | tf_op jit(solution)/shard_map/ppermute | solution.py:557
  835.5 68.0 %collective-permute-start.31 = (bf16[256,2048]{1,0:T(8,128)(2,1)S(1)}, bf16[256,2048]{1,0:T(8,128)(2,1)S(1)}, u32[]{:S(2)}, u32[]{:S(2)}) collective-permute-start(bf16[256,2048]{1,0:T(8,128)(2,1)S(1)} %add_convert_fusion.1), channel_id=1, source_target_pairs={{0,1},{1,2},{2,3},{3,0},{4,5},{5,6},{6,7},{7,4},{8,9},{9,10},{10,1... | collective-permute-start | bytes 3145736 | tf_op jit(solution)/shard_map/ppermute | solution.py:563
  836.3 89.7 %collective-permute-start.28 = (bf16[256,2048]{1,0:T(8,128)(2,1)S(1)}, bf16[256,2048]{1,0:T(8,128)(2,1)S(1)}, u32[]{:S(2)}, u32[]{:S(2)}) collective-permute-start(bf16[256,2048]{1,0:T(8,128)(2,1)S(1)} %add_convert_fusion.3), channel_id=1, source_target_pairs={{0,1},{1,2},{2,3},{3,0},{4,5},{5,6},{6,7},{7,4},{8,9},{9,10},{10,1... | collective-permute-start | bytes 3145736 | tf_op jit(solution)/shard_map/ppermute | solution.py:563
  859.0 89.5 %collective-permute-start.19 = (bf16[256,2048]{1,0:T(8,128)(2,1)S(1)}, bf16[256,2048]{1,0:T(8,128)(2,1)S(1)}, u32[]{:S(2)}, u32[]{:S(2)}) collective-permute-start(bf16[256,2048]{1,0:T(8,128)(2,1)S(1)} %add_convert_fusion.5), channel_id=1, source_target_pairs={{0,1},{1,2},{2,3},{3,0},{4,5},{5,6},{6,7},{7,4},{8,9},{9,10},{10,1... | collective-permute-start | bytes 3145736 | tf_op jit(solution)/shard_map/ppermute | solution.py:563
  881.5 89.5 %collective-permute-start.16 = (bf16[256,2048]{1,0:T(8,128)(2,1)S(1)}, bf16[256,2048]{1,0:T(8,128)(2,1)S(1)}, u32[]{:S(2)}, u32[]{:S(2)}) collective-permute-start(bf16[256,2048]{1,0:T(8,128)(2,1)S(1)} %add_convert_fusion.7), channel_id=1, source_target_pairs={{0,1},{1,2},{2,3},{3,0},{4,5},{5,6},{6,7},{7,4},{8,9},{9,10},{10,1... | collective-permute-start | bytes 3145736 | tf_op jit(solution)/shard_map/ppermute | solution.py:563
  904.0 89.5 %collective-permute-start.32 = (bf16[256,2048]{1,0:T(8,128)(2,1)S(1)}, bf16[256,2048]{1,0:T(8,128)(2,1)S(1)}, u32[]{:S(2)}, u32[]{:S(2)}) collective-permute-start(bf16[256,2048]{1,0:T(8,128)(2,1)S(1)} %add_convert_fusion), channel_id=1, source_target_pairs={{0,1},{1,2},{2,3},{3,0},{4,5},{5,6},{6,7},{7,4},{8,9},{9,10},{10,1... | collective-permute-start | bytes 3145736 | tf_op jit(solution)/shard_map/ppermute | solution.py:563
  926.4 89.5 %collective-permute-start.29 = (bf16[256,2048]{1,0:T(8,128)(2,1)S(1)}, bf16[256,2048]{1,0:T(8,128)(2,1)S(1)}, u32[]{:S(2)}, u32[]{:S(2)}) collective-permute-start(bf16[256,2048]{1,0:T(8,128)(2,1)S(1)} %add_convert_fusion.2), channel_id=1, source_target_pairs={{0,1},{1,2},{2,3},{3,0},{4,5},{5,6},{6,7},{7,4},{8,9},{9,10},{10,1... | collective-permute-start | bytes 3145736 | tf_op jit(solution)/shard_map/ppermute | solution.py:563
  948.9 89.5 %collective-permute-start.20 = (bf16[256,2048]{1,0:T(8,128)(2,1)S(1)}, bf16[256,2048]{1,0:T(8,128)(2,1)S(1)}, u32[]{:S(2)}, u32[]{:S(2)}) collective-permute-start(bf16[256,2048]{1,0:T(8,128)(2,1)S(1)} %add_convert_fusion.4), channel_id=1, source_target_pairs={{0,1},{1,2},{2,3},{3,0},{4,5},{5,6},{6,7},{7,4},{8,9},{9,10},{10,1... | collective-permute-start | bytes 3145736 | tf_op jit(solution)/shard_map/ppermute | solution.py:563
  971.4 81.9 %collective-permute-start.17 = (bf16[256,2048]{1,0:T(8,128)(2,1)S(1)}, bf16[256,2048]{1,0:T(8,128)(2,1)S(1)}, u32[]{:S(2)}, u32[]{:S(2)}) collective-permute-start(bf16[256,2048]{1,0:T(8,128)(2,1)S(1)} %add_convert_fusion.6), channel_id=1, source_target_pairs={{0,1},{1,2},{2,3},{3,0},{4,5},{5,6},{6,7},{7,4},{8,9},{9,10},{10,1... | collective-permute-start | bytes 3145736 | tf_op jit(solution)/shard_map/ppermute | solution.py:563
  1068.6 327.9 %reduce-scatter.5.cloned.1.call-start = ((), (), s32[]{:S(2)}) async-start(), calls=%async_computation.13 | async-start | bytes 7667712 | tf_op jit(solution)/shard_map/reduce_scatter | solution.py:708
  1201.5 251.3 %reduce-scatter.7.cloned.1.call-start = ((), (), s32[]{:S(2)}) async-start(), calls=%async_computation.14 | async-start | bytes 10027008 | tf_op jit(solution)/shard_map/reduce_scatter | solution.py:679
  1222.4 270.3 %reduce-scatter.11.cloned.1.call-start = ((), (), s32[]{:S(2)}) async-start(), calls=%async_computation.16 | async-start | bytes 18874368 | tf_op jit(solution)/shard_map/reduce_scatter | solution.py:662
  1223.2 448.7 %reduce-scatter.9.cloned.1.call-start = ((), (), s32[]{:S(2)}) async-start(), calls=%async_computation.15 | async-start | bytes 37748736 | tf_op jit(solution)/shard_map/reduce_scatter | solution.py:665
  1396.5 50.8 %collective-permute-start.41 = (bf16[256,2048]{1,0:T(8,128)(2,1)}, bf16[256,2048]{1,0:T(8,128)(2,1)}, u32[]{:S(2)}, u32[]{:S(2)}) collective-permute-start(bf16[256,2048]{1,0:T(8,128)(2,1)} %get-tuple-element.178), channel_id=1, source_target_pairs={{0,1},{1,2},{2,3},{3,0},{4,5},{5,6},{6,7},{7,4},{8,9},{9,10},{10,1... | collective-permute-start | bytes 3145736 | tf_op jit(solution)/shard_map/ppermute | solution.py:563
  1398.7 60.4 %all-to-all-start.3 = ((bf16[4,64,1664]{2,1,0:T(8,128)(2,1)}), bf16[4,64,1664]{2,1,0:T(8,128)(2,1)S(1)}, u32[]{:S(2)}, u32[]{:S(2)}) async-start(bf16[4,64,1664]{2,1,0:T(8,128)(2,1)} %bitcast.70), calls=%async_computation.4 | async-start | bytes 1703936 | tf_op jit(solution)/shard_map/all_to_all | solution.py:576
  (88 other events, 3389.5 us)
Sparse Core Ops, SparseCore 0:
  36.0 44.6 all-gather.5
  83.6 157.9 all-gather.7
  244.0 159.3 all-gather.9
  405.2 93.1 all-gather.11
  1201.6 63.2 reduce-scatter.4
  1268.8 73.8 reduce-scatter.6
  1346.6 115.9 reduce-scatter.10
  1466.6 205.2 reduce-scatter.8

commit v2 on v1

--- a/solution.py
+++ b/solution.py
@@ -11,6 +11,7 @@
 MASKED = -1e30
 LANES = 128
 ROOM = 58 << 20
+SLIM = 1
 
 f32 = jnp.float32
 bf16 = jnp.bfloat16
@@ -34,7 +35,9 @@
 
 def cost(flops, *arrays):
     moved = sum(a.size * a.dtype.itemsize for a in arrays)
-    return pl.CostEstimate(flops=int(flops), bytes_accessed=int(moved), transcendentals=0)
+    return pl.CostEstimate(
+        flops=int(flops) // SLIM, bytes_accessed=int(moved) // SLIM, transcendentals=0
+    )
 
 
 def whole(array):
@@ -55,9 +58,8 @@
     return parts
 
 
-def project(pieces, gain, weight):
+def project(pieces, gain, weight, third, first):
     count, (rows, width) = len(pieces), pieces[0].shape
-    third = weight.shape[1] // 3
     total = count * rows
     step = 32
     part = min(total, 512)
@@ -97,7 +99,7 @@
         kernel,
         grid=(3,),
         in_specs=[whole(x) for x in pieces]
-        + [whole(gain), pl.BlockSpec((width, third), lambda t: (0, t))],
+        + [whole(gain), pl.BlockSpec((width, third), lambda t: (0, first + t))],
         out_specs=(
             pl.BlockSpec((total, width), lambda t: (0, 0)),
             pl.BlockSpec((total, third), lambda t: (0, t)),
@@ -105,7 +107,7 @@
         ),
         out_shape=outs,
         compiler_params=params(1),
-        cost_estimate=cost(2 * total * width * 3 * third, *pieces, weight, *outs[:2]),
+        cost_estimate=cost(2 * total * width * 3 * third, *pieces, *outs[:2]),
         name="project",
     )(*pieces, gain, weight)
 
@@ -278,6 +280,168 @@
     )(place, lengths, q, k, v, grad, lse, qkv, qkv, inverse, gains, cosines, sines)
 
 
+def back_project(dzq, dzk, dv, qkv, inverse, stats, gains, weight, first, pieces):
+    total, third = dv.shape
+    width = weight.shape[0]
+    rows = total // pieces
+    tile = min(512, width)
+
+    def kernel(dzq_i, dzk_i, dv_i, q_i, k_i, inv, st, gain_ref, wq, wk, wv, *rest):
+        outs, low = rest[:pieces], rest[pieces]
+
+        @pl.when(pl.program_id(0) == 0)
+        def _():
+            for which, (dz, raw) in enumerate(((dzq_i, q_i), (dzk_i, k_i))):
+                r = inv[which]
+                low[:, which * third : (which + 1) * third] = (
+                    r * (gain_ref[which] * dz[...]) - raw[...] * (r * r * r * st[which])
+                ).astype(bf16)
+            low[:, 2 * third :] = dv_i[...]
+
+        for i in range(pieces):
+            at = slice(i * rows, (i + 1) * rows)
+            outs[i][...] = (
+                dot_nt(low[at, :third], wq[...])
+                + dot_nt(low[at, third : 2 * third], wk[...])
+                + dot_nt(low[at, 2 * third :], wv[...])
+            ).astype(bf16)
+
+    def raw(k):
+        return pl.BlockSpec((total, third), lambda d: (0, k))
+
+    def taken(k):
+        return pl.BlockSpec((tile, third), lambda d: (d, first + k))
+
+    outs = (struct((rows, width), bf16),) * pieces + (struct((total, 3 * third), bf16),)
+    return pl.pallas_call(
+        kernel,
+        grid=(width // tile,),
+        in_specs=[whole(dzq), whole(dzk), whole(dv), raw(0), raw(1)]
+        + [whole(inverse), whole(stats), whole(gains), taken(0), taken(1), taken(2)],
+        out_specs=(pl.BlockSpec((rows, tile), lambda d: (0, d)),) * pieces
+        + (pl.BlockSpec((total, 3 * third), lambda d: (0, 0)),),
+        out_shape=outs,
+        compiler_params=params(1),
+        cost_estimate=cost(6 * total * width * third, dzq, dzk, dv, *outs),
+        name="back_project",
+    )(dzq, dzk, dv, qkv, qkv, inverse, stats, gains, weight, weight, weight)
+
+
+def out_project(att, rows_in, weight, gain):
+    n, rows, cols = att.shape
+    width = n * cols
+
+    def kernel(a_i, x_i, w_i, gain_ref, h_o, n_o, acc):
+        p = pl.program_id(0)
+
+        @pl.when(p == 0)
+        def _():
+            acc[...] = x_i[...].astype(f32)
+
+        acc[...] += dot(a_i[0], w_i[...])
+
+        @pl.when(p == n - 1)
+        def _():
+            h = acc[...]
+            h_o[...] = h
+            r = lax.rsqrt(jnp.mean(h * h, axis=-1, keepdims=True) + EPS)
+            n_o[...] = (h * r * gain_ref[...]).astype(bf16)
+
+    outs = (struct((rows, width), f32), struct((rows, width), bf16))
+    return pl.pallas_call(
+        kernel,
+        grid=(n,),
+        in_specs=[
+            pl.BlockSpec((1, rows, cols), lambda p: (p, 0, 0)),
+            whole(rows_in),
+            pl.BlockSpec((cols, width), lambda p: (p, 0)),
+            whole(gain),
+        ],
+        out_specs=(pl.BlockSpec((rows, width), lambda p: (0, 0)),) * 2,
+        out_shape=outs,
+        scratch_shapes=[pltpu.VMEM((rows, width), f32)],
+        compiler_params=params(1),
+        cost_estimate=cost(2 * rows * width * width, att, rows_in, *outs),
+        name="out_project",
+    )(att, rows_in, weight, gain)
+
+
+def out_back(moved, part, low, hidden, gain, weight, n):
+    rows, width = hidden.shape
+    cols = width // n
+
+    def kernel(m_i, p_i, l_i, h_i, gain_ref, w_i, gh_o, da_o, do_o, fg_o):
+        @pl.when(pl.program_id(0) == 0)
+        def _():
+            dz = m_i[...].astype(f32) + p_i[...].astype(f32)
+            v = h_i[...]
+            r = lax.rsqrt(jnp.mean(v * v, axis=-1, keepdims=True) + EPS)
+            fg_o[...] = jnp.sum(dz * v * r, axis=0, keepdims=True)
+            scaled = dz * gain_ref[...]
+            inner = jnp.mean(v * scaled, axis=-1, keepdims=True)
+            total = l_i[...].astype(f32) + r * scaled - v * (r * r * r * inner)
+            gh_o[...] = total
+            da_o[...] = total.astype(bf16)
+
+        do_o[0] = dot_nt(da_o[...], w_i[...]).astype(bf16)
+
+    outs = (
+        struct((rows, width), f32),
+        struct((rows, width), bf16),
+        struct((n, rows, cols), bf16),
+        struct((1, width), f32),
+    )
+    full = pl.BlockSpec((rows, width), lambda p: (0, 0))
+    return pl.pallas_call(
+        kernel,
+        grid=(n,),
+        in_specs=[whole(moved), whole(part), whole(low), whole(hidden), whole(gain)]
+        + [pl.BlockSpec((cols, width), lambda p: (p, 0))],
+        out_specs=(
+            full,
+            full,
+            pl.BlockSpec((1, rows, cols), lambda p: (p, 0, 0)),
+            pl.BlockSpec((1, width), lambda p: (0, 0)),
+        ),
+        out_shape=outs,
+        compiler_params=params(1),
+        cost_estimate=cost(2 * rows * width * width, hidden, *outs),
+        name="out_back",
+    )(moved, part, low, hidden, gain, weight)
+
+
+def attention_weight_grads(atts, datts, normeds, lows, columns):
+    count = len(atts)
+    n, rows, cols = atts[0].shape
+    width = n * cols
+    total, wide = lows[0].shape
+
+    def kernel(*refs):
+        at, da, nm, lw = (refs[i * count : (i + 1) * count] for i in range(4))
+        column_ref, o = refs[4 * count :]
+        o[:, :width] = sum(dot_tn(at[g][0], da[g][...]) for g in range(count)).astype(bf16)
+        o[:, width : width + wide] = sum(
+            dot_tn(nm[g][...], lw[g][...]) for g in range(count)
+        ).astype(bf16)
+        o[:, width + wide :] = column_ref[...]
+
+    out = struct((width, width + wide + LANES), bf16)
+    return pl.pallas_call(
+        kernel,
+        grid=(n,),
+        in_specs=[pl.BlockSpec((1, rows, cols), lambda p: (p, 0, 0)) for _ in atts]
+        + [whole(x) for x in datts]
+        + [pl.BlockSpec((total, cols), lambda p: (0, p)) for _ in normeds]
+        + [whole(x) for x in lows]
+        + [pl.BlockSpec((cols, LANES), lambda p: (p, 0))],
+        out_specs=pl.BlockSpec((cols, width + wide + LANES), lambda p: (p, 0)),
+        out_shape=out,
+        compiler_params=params(1),
+        cost_estimate=cost(2 * count * width * (rows * width + total * wide), *normeds, *lows, out),
+        name="attention_weight_grads",
+    )(*atts, *datts, *normeds, *lows, columns)
+
+
 def picks(rank_ref, nb, cap):
     row = rank_ref[0, nb : nb + 1, :]
     return lax.broadcasted_iota(jnp.int32, (cap, row.shape[1]), 0) == row
@@ -287,19 +451,30 @@
     return jnp.sum(jnp.where(hot, coef_ref[0, nb : nb + 1, :], 0.0), axis=-1, keepdims=True)
 
 
-def expert_forward(pieces, rank, gate_up, cap):
+def in_place(arrays, given):
+    if arrays is None:
+        return (), [], {}
+    return (
+        tuple(arrays),
+        [pl.BlockSpec(memory_space=pl.ANY)] * len(arrays),
+        {given + i: i for i in range(len(arrays))},
+    )
+
+
+def expert_forward(pieces, rank, gate_up, cap, start, stop, begun=None):
     experts, blocks, rows = rank.shape
     width, hidden = gate_up.shape[1:]
     slots = blocks * cap
     tile = min(256, hidden)
     parts = chunks_of(blocks, cap)
     part = slots // parts
+    more, more_specs, aliases = in_place(begun, blocks + 3)
 
     def kernel(*refs):
         xs, (rank_ref, wg, wu), (x_o, g_o, u_o, a_o) = (
             refs[:blocks],
             refs[blocks : blocks + 3],
-            refs[blocks + 3 :],
+            refs[-4:],
         )
 
         @pl.when(pl.program_id(1) == 0)
@@ -318,23 +493,30 @@
             u_o[0, at, :] = upper.astype(bf16)
             a_o[0, at, :] = (gate * jax.nn.sigmoid(gate) * upper).astype(bf16)
 
-    tiled = pl.BlockSpec((1, slots, tile), lambda e, f: (e, 0, f))
+    tiled = pl.BlockSpec((1, slots, tile), lambda e, f: (start + e, 0, f))
     outs = (struct((experts, slots, width), bf16),) + (struct((experts, slots, hidden), bf16),) * 3
     return pl.pallas_call(
         kernel,
-        grid=(experts, hidden // tile),
+        grid=(stop - start, hidden // tile),
         in_specs=[whole(x) for x in pieces]
         + [
-            pl.BlockSpec((1, blocks, rows), lambda e, f: (e, 0, 0)),
-            pl.BlockSpec((1, width, tile), lambda e, f: (e, 0, f)),
-            pl.BlockSpec((1, width, tile), lambda e, f: (experts + e, 0, f)),
-        ],
-        out_specs=(pl.BlockSpec((1, slots, width), lambda e, f: (e, 0, 0)), tiled, tiled, tiled),
+            pl.BlockSpec((1, blocks, rows), lambda e, f: (start + e, 0, 0)),
+            pl.BlockSpec((1, width, tile), lambda e, f: (start + e, 0, f)),
+            pl.BlockSpec((1, width, tile), lambda e, f: (experts + start + e, 0, f)),
+        ]
+        + more_specs,
+        out_specs=(
+            pl.BlockSpec((1, slots, width), lambda e, f: (start + e, 0, 0)),
+            tiled,
+            tiled,
+            tiled,
+        ),
         out_shape=outs,
+        input_output_aliases=aliases,
         compiler_params=params(2),
-        cost_estimate=cost(4 * experts * slots * width * hidden, *pieces, gate_up, *outs),
+        cost_estimate=cost(4 * (stop - start) * slots * width * hidden, *pieces),
         name="expert_forward",
-    )(*pieces, rank, gate_up, gate_up)
+    )(*pieces, rank, gate_up, gate_up, *more)
 
 
 def expert_output(active, rank, coef, down, cap):
@@ -492,27 +674,30 @@
     )(dgate, dupper, rank, gate_up, gate_up)
 
 
-def expert_weight_grad(x, dgate, dupper):
+def expert_weight_grad(x, dgate, dupper, start, stop, begun=None):
     experts, slots, width = x.shape
     hidden = dgate.shape[2]
     tile = min(256, width)
-
-    def kernel(x_i, dg_i, du_i, o):
+    more, more_specs, aliases = in_place(begun, 3)
+
+    def kernel(x_i, dg_i, du_i, *rest):
+        o = rest[-1]
         o[0, 0] = dot_tn(x_i[0], dg_i[0]).astype(bf16)
         o[1, 0] = dot_tn(x_i[0], du_i[0]).astype(bf16)
 
-    line = pl.BlockSpec((1, slots, hidden), lambda e, d: (e, 0, 0))
-    out = struct((2, experts, width, hidden), bf16)
-    return pl.pallas_call(
-        kernel,
-        grid=(experts, width // tile),
-        in_specs=[pl.BlockSpec((1, slots, tile), lambda e, d: (e, 0, d)), line, line],
-        out_specs=pl.BlockSpec((2, 1, tile, hidden), lambda e, d: (0, e, d, 0)),
-        out_shape=out,
+    line = pl.BlockSpec((1, slots, hidden), lambda e, d: (start + e, 0, 0))
+    return pl.pallas_call(
+        kernel,
+        grid=(stop - start, width // tile),
+        in_specs=[pl.BlockSpec((1, slots, tile), lambda e, d: (start + e, 0, d)), line, line]
+        + more_specs,
+        out_specs=(pl.BlockSpec((2, 1, tile, hidden), lambda e, d: (0, start + e, d, 0)),),
+        out_shape=(struct((2, experts, width, hidden), bf16),),
+        input_output_aliases=aliases,
         compiler_params=params(2),
-        cost_estimate=cost(4 * experts * slots * width * hidden, x, dgate, dupper, out),
+        cost_estimate=cost(4 * (stop - start) * slots * width * hidden, x),
         name="expert_weight_grad",
-    )(x, dgate, dupper).reshape(2 * experts, width, hidden)
+    )(x, dgate, dupper, *more)
 
 
 def tables(positions):
@@ -540,7 +725,6 @@
     top = expert_ids.shape[-1]
     experts = w_gate.shape[0]
     n = lax.axis_size("ctx")
-    groups = lax.axis_size("batch")
     here = lax.axis_index("ctx")
     seqs = batches * sequences
     cols = width // n
@@ -551,65 +735,82 @@
     up = [(i, (i + 1) % n) for i in range(n)]
     place = here.reshape(1).astype(jnp.int32)
 
-    def gather_ring(piece):
-        held = [piece]
-        for _ in range(n - 1):
-            held.append(lax.ppermute(held[-1], "ctx", up))
-        return held
-
-    def reduce_ring(parts):
-        total = parts[1 % n]
-        for j in range(2, n + 1):
-            moved = lax.ppermute(total, "ctx", up).astype(f32) + parts[j % n].astype(f32)
-            total = moved.astype(bf16) if j < n else moved
-        return total
+    def after(value, *others):
+        return lax.optimization_barrier((value, others))[0]
+
+    class Ring:
+        def __init__(self, piece):
+            self.held = [piece]
+
+        def hop(self, prev):
+            if len(self.held) == n:
+                return ()
+            self.held.append(lax.ppermute(after(self.held[-1], prev), "ctx", up))
+            return (self.held[-1],)
+
+    class Sum:
+        def __init__(self, parts):
+            self.parts = parts
+            self.moved = None
+            self.at = 1
+
+        def hop(self, prev):
+            if self.at == n:
+                return ()
+            part = after(self.parts[self.at], prev)
+            if self.moved is not None:
+                part = (after(self.moved, prev).astype(f32) + part.astype(f32)).astype(bf16)
+            self.moved = lax.ppermute(part, "ctx", up)
+            self.at += 1
+            return (self.moved,)
+
+    def finish(ring, prev):
+        while got := ring.hop(prev):
+            prev = (prev, got)
+        return prev
+
+    def direct(x):
+        return [x] + [
+            lax.ppermute(x, "ctx", [(i, (i + k) % n) for i in range(n)]) for k in range(1, n)
+        ]
 
     def ctx_sum(x):
-        total = x
-        for k in range(1, n):
-            got = lax.ppermute(x, "ctx", [(i, (i + k) % n) for i in range(n)])
-            total = total + jnp.roll(got, k, axis=0)
-        return total
-
-    def to_owner(summed):
-        pieces = summed.reshape(n, own, summed.shape[-1])
-        return lax.all_to_all(pieces, "ctx", split_axis=0, concat_axis=0, tiled=True)
-
+        held = direct(x)
+        return sum((jnp.roll(held[k], k, axis=0) for k in range(1, n)), held[0])
+
+    def exchange(x):
+        return lax.all_to_all(x, "ctx", split_axis=0, concat_axis=0, tiled=True)
+
+    gains = jnp.stack([attn_gain, query_gain, key_gain, ffn_gain], axis=1)
+    gains = jnp.pad(gains, ((0, 0), (0, LANES - 4)))
     mine = jnp.concatenate(
-        [jnp.swapaxes(w.reshape(own, n, cols), 0, 1) for w in (w_query, w_key, w_value)], axis=2
-    )
-    mine = lax.all_to_all(mine, "ctx", split_axis=0, concat_axis=0, tiled=True)
-    qkv_w = lax.all_gather(mine.reshape(n * own, 3 * cols), "batch", axis=0, tiled=True)
-    gain_attn, gain_query, gain_key, gain_ffn = (
-        lax.all_gather(g, ("batch", "ctx"), axis=0, tiled=True).astype(f32)
-        for g in (attn_gain, query_gain, key_gain, ffn_gain)
-    )
-    out_w = lax.all_gather(w_out, ("batch", "ctx"), axis=0, tiled=True).reshape(n, cols, width)
+        [jnp.broadcast_to(w_out[None], (n, own, width))]
+        + [jnp.swapaxes(w.reshape(own, n, cols), 0, 1) for w in (w_query, w_key, w_value)]
+        + [jnp.broadcast_to(gains[None], (n, own, LANES))],
+        axis=2,
+    )
+    mine = exchange(mine).reshape(n * own, -1)
+    att_w = lax.all_gather(mine, "batch", axis=0, tiled=True)
+    all_gains = att_w[:, width + 3 * cols : width + 3 * cols + 4].astype(f32).T
+    gain_attn, gain_ffn = all_gains[0], all_gains[3]
     gate_up = lax.all_gather(
-        jnp.concatenate([w_gate, w_up], axis=0), "batch", axis=1, tiled=True
-    )
-    down = lax.all_gather(w_down, "batch", axis=2, tiled=True)
-    qk_gains = lax.dynamic_slice_in_dim(
-        jnp.stack([gain_query, gain_key]), here * cols, cols, 1
-    ).reshape(2, 1, cols)
+        after(jnp.concatenate([w_gate, w_up], axis=0), mine), "batch", axis=1, tiled=True
+    )
+    down = lax.all_gather(after(w_down, mine), "batch", axis=2, tiled=True)
+    qk_gains = lax.dynamic_slice_in_dim(all_gains[1:3], here * cols, cols, 1).reshape(2, 1, cols)
 
     xs = tokens.reshape(seqs, rows, width)
     span_len = lengths.reshape(seqs)
     local_pos = here * rows + jnp.arange(rows, dtype=jnp.int32)
     live = (local_pos[None, :] < span_len[:, None])[:, :, None]
-    x_rings = [gather_ring(xs[g]) for g in range(seqs)]
-    x_pieces = [x_rings[g][j] for j in range(n) for g in range(seqs)]
     grad_low = jnp.where(live, cotangent.reshape(seqs, rows, width), jnp.zeros((), bf16))
-
     sent = jnp.stack(
         [
             jnp.swapaxes(expert_ids.reshape(seqs, rows, top), 1, 2),
             jnp.swapaxes(route_levels.reshape(seqs, rows, top), 1, 2),
         ]
     )
-    routes = lax.all_gather(sent, "ctx", axis=0, tiled=False)
-    order = lax.rem(here - jnp.arange(n, dtype=jnp.int32) + n, n)
-    routes = jnp.take(routes, order, axis=0)
+    routes = jnp.stack(direct(sent))
     chosen = routes[:, 0].reshape(blocks, top, rows)
     levels = routes[:, 1].reshape(blocks, top, rows).astype(f32)
     share = levels / jnp.sum(levels, axis=1, keepdims=True)
@@ -628,92 +829,212 @@
     cosines, sines = tables(jnp.arange(n * rows, dtype=jnp.int32))
     cosines = cosines.reshape(n, rows, HEAD_DIM)
     sines = sines.reshape(n, rows, HEAD_DIM)
-    normed, qkv, squares = project(x_pieces, gain_attn[None, :], qkv_w)
-    squares = squares[:2].reshape(2, n, seqs, rows)
-    squares = ctx_sum(jnp.swapaxes(squares, 0, 1))
-    inverse = lax.rsqrt(squares / width + EPS)
-    inverse = jnp.swapaxes(inverse, 0, 1)[..., None]
-    qkv = qkv.reshape(n, seqs, rows, 3 * cols)
-    q, k, v, att, lse = attention_forward(
-        place, span_len, qkv, inverse, qk_gains, cosines, sines
-    )
-    att = lax.all_to_all(att, "ctx", split_axis=0, concat_axis=0, tiled=True)
-    hidden = xs.astype(f32) + jnp.einsum(
-        "ngrd,nde->gre", att, out_w, preferred_element_type=f32
-    )
-    n2 = (
-        hidden * lax.rsqrt(jnp.mean(hidden * hidden, axis=-1, keepdims=True) + EPS) * gain_ffn
-    ).astype(bf16)
-
-    g_rings = [gather_ring(grad_low[g]) for g in range(seqs)]
-    grad_pieces = [g_rings[g][j] for j in range(n) for g in range(seqs)]
-    n_rings = [gather_ring(n2[g]) for g in range(seqs)]
-    n_pieces = [n_rings[g][j] for j in range(n) for g in range(seqs)]
-    slots_x, gate, upper, active = expert_forward(n_pieces, rank, gate_up, cap)
-    y_parts = expert_output(active, rank, coef, down, cap)
-    mixture = jnp.stack(
-        [reduce_ring([y_parts[j * seqs + g] for j in range(n)]) for g in range(seqs)]
-    )
-    out = jnp.where(live, hidden + mixture, 0.0).astype(bf16)
-
+    kept, atts, hiddens = [None] * seqs, [None] * seqs, [None] * seqs
+    xr = [Ring(xs[g]) for g in range(seqs)]
+    nr = [None] * seqs
+
+    def projected(g, prev):
+        normed, qkv, squares = project(
+            [after(xr[g].held[0], prev)] + xr[g].held[1:], gain_attn[None, :], att_w, cols, n
+        )
+        return normed, qkv.reshape(n, 1, rows, 3 * cols), squares
+
+    def scales(squares, prev):
+        squares = jnp.swapaxes(squares[:2].reshape(2, n, rows), 0, 1)
+        inverse = lax.rsqrt(ctx_sum(after(squares, prev)) / width + EPS)
+        return jnp.swapaxes(inverse, 0, 1).reshape(2, n, 1, rows, 1)
+
+    def attended(g, normed, qkv, inverse, prev):
+        q, k, v, att, lse = attention_forward(
+            place, span_len[g : g + 1], qkv, after(inverse, prev), qk_gains, cosines, sines
+        )
+        kept[g] = (q, k, v, lse, qkv, inverse, normed)
+        return att.reshape(n, rows, cols)
+
+    def out_projected(g, prev):
+        hiddens[g], n2 = out_project(
+            after(atts[g], prev), xs[g], att_w, gain_ffn[None, :]
+        )
+        nr[g] = Ring(n2)
+        return (n2,)
+
+    stage = xr[0].hop(routes)
+    stage = finish(xr[0], stage)
+    first = None
+    for g in range(seqs):
+        last = g + 1 == seqs
+        if not last:
+            stage = xr[g + 1].hop(stage)
+            moving = xr[g + 1].hop(stage)
+        else:
+            moving = ()
+        if first is not None:
+            moving = (exchange(after(first, stage)),)
+        normed, qkv, squares = projected(g, stage)
+        stage = (squares, moving)
+        inverse = scales(squares, stage)
+        if first is not None:
+            atts[g - 1] = moving[0]
+            stage = (inverse, out_projected(g - 1, stage))
+        else:
+            stage = (inverse,)
+        moving = () if last else xr[g + 1].hop(stage)
+        if first is not None:
+            moving += nr[g - 1].hop(stage)
+        att = attended(g, normed, qkv, inverse, stage)
+        stage = (att, moving)
+        if not last:
+            stage = finish(xr[g + 1], stage)
+        first = att
+    g = seqs - 1
+    moving = nr[g - 1].hop(stage) if g else ()
+    atts[g] = exchange(after(first, stage))
+    stage = (atts[g], moving)
+    moving = nr[g - 1].hop(stage) if g else ()
+    stage = (out_projected(g, stage), moving)
+    for one in nr:
+        stage = finish(one, stage)
+
+    dr = [Ring(grad_low[g]) for g in range(seqs)]
+    n_pieces = [nr[g].held[j] for j in range(n) for g in range(seqs)]
+    held = None
+    for start, stop in ((0, experts // 2), (experts // 2, experts)):
+        moving = [one.hop(stage) for one in dr]
+        held = expert_forward(
+            n_pieces, after(rank, stage), gate_up, cap, start, stop, held
+        )
+        stage = (held, moving)
+    slots_x, gate, upper, active = held
+    moving = [one.hop(stage) for one in dr]
+    y_parts = expert_output(after(active, stage), rank, coef, down, cap)
+    stage = (y_parts, moving)
+    stage = [finish(one, stage) for one in dr] or stage
+    grad_pieces = [dr[g].held[j] for j in range(n) for g in range(seqs)]
+    yr = [Sum([y_parts[j * seqs + g] for j in range(n)]) for g in range(seqs)]
+    moving = [one.hop(stage) for one in yr]
     dgate, dupper, grad_down = expert_backward(
-        grad_pieces, rank, coef, down, gate, upper, active, cap
-    )
-    grad_down = lax.psum_scatter(grad_down, "batch", scatter_dimension=2, tiled=True)
-    dx_parts = expert_input_grad(dgate, dupper, rank, gate_up, cap)
-    grad_gu = expert_weight_grad(slots_x, dgate, dupper)
-    grad_gu = lax.psum_scatter(grad_gu, "batch", scatter_dimension=1, tiled=True)
-    grad_mid = jnp.stack(
-        [reduce_ring([dx_parts[j * seqs + g] for j in range(n)]) for g in range(seqs)]
-    )
-    back, ffn_terms = norm_back(hidden, gain_ffn, grad_mid)
-    grad_hidden = grad_low.astype(f32) + back
-    ffn_part = jnp.sum(ffn_terms, axis=(0, 1))
-    datt = grad_hidden.astype(bf16)
-
-    do = jnp.einsum("gre,nde->ngrd", datt, out_w, preferred_element_type=f32).astype(bf16)
-    do = lax.all_to_all(do, "ctx", split_axis=0, concat_axis=0, tiled=True)
-    grad_out = jnp.einsum("ngrd,gre->nde", att, datt, preferred_element_type=f32)
-    grad_out = grad_out.astype(bf16).reshape(width, width)
-    column = jnp.pad(ffn_part.astype(bf16)[:, None], ((0, 0), (0, LANES - 1)))
-    grad_out = lax.psum_scatter(
-        jnp.concatenate([grad_out, column], axis=1), "batch", scatter_dimension=0, tiled=True
-    )
-    grad_out = jnp.sum(to_owner(grad_out).astype(f32), axis=0)
-
-    dzq, dzk, dv, stats, qk_part = attention_backward(
-        place, span_len, q, k, v, do, lse, qkv, inverse, qk_gains, cosines, sines
-    )
-    stats = jnp.sum(stats[..., 0], axis=2)
-    stats = ctx_sum(jnp.transpose(stats, (2, 0, 1, 3)))
-    stats = jnp.swapaxes(stats, 0, 1)[..., None] / width
-
-    def through_norm(which, dz):
-        r = inverse[which]
-        raw = qkv[..., which * cols : (which + 1) * cols]
-        return (r * qk_gains[which] * dz - raw * (r * r * r) * stats[which]).astype(bf16)
-
-    dqkv = jnp.concatenate([through_norm(0, dzq), through_norm(1, dzk), dv], axis=-1)
-    dqkv = dqkv.reshape(blocks * rows, 3 * cols)
-    dn1 = dot_nt(dqkv, qkv_w).astype(bf16).reshape(n, seqs, rows, width)
-    grad_n1 = jnp.stack([reduce_ring([dn1[j, g] for j in range(n)]) for g in range(seqs)])
-    back, _ = norm_back(xs.astype(f32), gain_attn, grad_n1)
-    grad_tokens = grad_hidden + back
-
-    grad_qkv = dot_tn(normed, dqkv).astype(bf16)
+        grad_pieces, after(rank, stage), coef, down, gate, upper, active, cap
+    )
+    stage = (dgate, moving)
+    grad_down = lax.psum_scatter(
+        after(grad_down, stage), "batch", scatter_dimension=2, tiled=True
+    )
+    moving = [one.hop(stage) for one in yr]
+    dx_parts = expert_input_grad(after(dgate, stage), dupper, rank, gate_up, cap)
+    stage = (dx_parts, moving)
+    zr = [Sum([dx_parts[j * seqs + g] for j in range(n)]) for g in range(seqs)]
+    held = None
+    for i in range(3):
+        moving = zr[0].hop(stage)
+        held = expert_weight_grad(
+            slots_x, after(dgate, stage), dupper, experts * i // 3, experts * (i + 1) // 3, held
+        )
+        stage = (held, moving)
+    gu_local = held[0].reshape(2 * experts, width, -1)
+    grad_gu = lax.psum_scatter(
+        after(gu_local, stage, grad_down), "batch", scatter_dimension=1, tiled=True
+    )
+    stage = finish(zr[0], stage)
+
+    grad_hiddens, datts, dos = [None] * seqs, [None] * seqs, [None] * seqs
+    lows, dn = [None] * seqs, [None] * seqs
+    ffn_part = jnp.zeros((1, width), f32)
+    qk_part = jnp.zeros((2, cols), f32)
+
+    def out_backed(g, prev):
+        grad_hiddens[g], datts[g], do, one = out_back(
+            after(zr[g].moved, prev), dx_parts[g], grad_low[g], hiddens[g], gain_ffn[None, :],
+            att_w, n,
+        )
+        return do, one
+
+    def attention_backed(g, prev):
+        q, k, v, lse, qkv, inverse, _ = kept[g]
+        *grads, stats, qk_one = attention_backward(
+            place, span_len[g : g + 1], after(q, prev), k, v, dos[g].reshape(n, 1, rows, cols),
+            lse, qkv, inverse, qk_gains, cosines, sines,
+        )
+        stats = jnp.sum(stats.reshape(2, cols // HEAD_DIM, n, rows), axis=1)
+        return grads, jnp.swapaxes(stats, 0, 1), qk_one.reshape(2, cols)
+
+    def summed_stats(stats, prev):
+        return jnp.swapaxes(ctx_sum(after(stats, prev)), 0, 1) / width
+
+    def back_projected(g, grads, stats, prev):
+        qkv, inverse = kept[g][4:6]
+        *dn1, lows[g] = back_project(
+            *(one.reshape(n * rows, cols) for one in grads), qkv.reshape(n * rows, 3 * cols),
+            inverse.reshape(2, n * rows, 1), after(stats, prev).reshape(2, n * rows, 1), qk_gains,
+            att_w, n, n,
+        )
+        dn[g] = Sum(dn1)
+        return (lows[g],)
+
+    held = None
+    for g in range(seqs):
+        last = g + 1 == seqs
+        if g == 0:
+            moving = () if last else zr[1].hop(stage)
+            do, one = out_backed(0, stage)
+            ffn_part = ffn_part + one
+            stage = (do, moving)
+        moving = () if last else zr[g + 1].hop(stage)
+        dos[g] = exchange(after(do, stage))
+        if held is not None:
+            moving += back_projected(g - 1, *held, stage)
+        stage = (dos[g], moving)
+        moving = () if last else zr[g + 1].hop(stage)
+        if held is not None:
+            moving += dn[g - 1].hop(stage)
+        grads, stats, one = attention_backed(g, stage)
+        qk_part = qk_part + one
+        stage = (stats, moving)
+        if not last:
+            stage = finish(zr[g + 1], stage)
+        stats = summed_stats(stats, stage)
+        if not last:
+            do, one = out_backed(g + 1, stage)
+            ffn_part = ffn_part + one
+            stage = (stats, do)
+        else:
+            stage = (stats,)
+        held = (grads, stats)
+    g = seqs - 1
+    moving = dn[g - 1].hop(stage) if g else ()
+    stage = (back_projected(g, *held, stage), moving)
     qk_rows = lax.dynamic_update_slice_in_dim(
-        jnp.zeros((2, width), f32), jnp.sum(qk_part, axis=(1, 2)), here * cols, 1
-    )
-    qk_column = jnp.pad(qk_rows.T.astype(bf16), ((0, 0), (0, LANES - 2)))
-    grad_qkv = lax.psum_scatter(
-        jnp.concatenate([grad_qkv, qk_column], axis=1), "batch", scatter_dimension=0, tiled=True
-    )
-    grad_qkv = to_owner(grad_qkv).astype(f32)
+        jnp.zeros((2, width), f32), qk_part, here * cols, 1
+    )
+    columns = jnp.concatenate([qk_rows, ffn_part]).T.astype(bf16)
+    columns = jnp.pad(columns, ((0, 0), (0, LANES - 3)))
+    moving = dn[g - 1].hop(stage) if g else ()
+    att_grads = attention_weight_grads(
+        atts, datts, [one[-1] for one in kept], lows, after(columns, stage)
+    )
+    stage = (att_grads, moving)
+    summed = lax.psum_scatter(after(att_grads, grad_gu), "batch", scatter_dimension=0, tiled=True)
+    while len(left := [one.hop(stage) for one in dn + yr if one.at < n]):
+        stage = left
+    outs = [
+        jnp.where(
+            live[g], hiddens[g] + (yr[g].moved.astype(f32) + y_parts[g].astype(f32)), 0.0
+        ).astype(bf16)
+        for g in range(seqs)
+    ]
+    token_grads = []
+    for g in range(seqs):
+        grad_n1 = dn[g].moved.astype(f32) + dn[g].parts[0].astype(f32)
+        back, _ = norm_back(xs[g].astype(f32), gain_attn, grad_n1)
+        token_grads.append(grad_hiddens[g] + back)
+    summed = exchange(summed.reshape(n, own, -1)).astype(f32)
+    grad_out = jnp.sum(summed[:, :, :width], axis=0)
     grad_q, grad_k, grad_v = (
-        jnp.swapaxes(grad_qkv[:, :, i * cols : (i + 1) * cols], 0, 1).reshape(own, width)
+        jnp.swapaxes(summed[:, :, width + i * cols : width + (i + 1) * cols], 0, 1).reshape(
+            own, width
+        )
         for i in range(3)
     )
-    qk_sums = jnp.sum(grad_qkv[:, :, 3 * cols :], axis=0)
+    gain_sums = jnp.sum(summed[:, :, width + 3 * cols :], axis=0)
     grad_attn_gain = (
         jnp.sum(
             w_query.astype(f32) * grad_q
@@ -725,16 +1046,16 @@
     )
     shape = (batches, sequences, rows, width)
     return (
-        out.reshape(shape),
-        grad_tokens.reshape(shape),
+        jnp.stack(outs).reshape(shape),
+        jnp.stack(token_grads).reshape(shape),
         grad_q,
         grad_k,
         grad_v,
-        grad_out[:, :width],
+        grad_out,
         grad_attn_gain,
-        qk_sums[:, 0],
-        qk_sums[:, 1],
-        grad_out[:, width],
+        gain_sums[:, 0],
+        gain_sums[:, 1],
+        gain_sums[:, 2],
         grad_gu[:experts].astype(f32),
         grad_gu[experts:].astype(f32),
         grad_down.astype(f32),

time: 1690 us -> 1220 us (0.72)
  waiting for transfers between devices: 870 us -> 454 us
  blocking collectives: 184 us -> 50.2 us
  Pallas kernels: 415 us -> 532 us
  matrix products: 60.8 us -> 0.77 us
  starting transfers between devices: 47.8 us -> 68.3 us
  other arithmetic: 68.2 us -> 48.9 us
    reduce_scatter x4 -> x3, waiting for transfers between devices: 175 us -> 0.03 us  [the longest x1 0.02 us: body(): lax.psum_scatter(after(grad_down, stage), 'batch', scatter_dimension=2, t...]
    ppermute x42 -> x51, waiting for transfers between devices: 579 us -> 434 us  [the longest x18 230 us: hop(): self.held.append(lax.ppermute(after(self.held[-1], prev), 'ctx', up))]
    pallas_call x2 -> x12, Pallas kernels: 126 us -> 230 us  [the longest x2 71.4 us: expert_forward(): pl.pallas_call(kernel, grid=(stop - start, hidden // tile), in_specs=[who...]
    all_to_all x4 -> x5, waiting for transfers between devices: 115 us -> 18.6 us  [exchange(): return lax.all_to_all(x, 'ctx', split_axis=0, concat_axis=0, tiled=True)]
    all_gather x1 -> x0, blocking collectives: 95.9 us -> none  [body(): routes = lax.all_gather(sent, 'ctx', axis=0, tiled=False)]
    unnamed x1 -> x0, blocking collectives: 62 us -> none
    dot_general x5 -> x0, matrix products: 60.1 us -> none  [the longest x2 34.9 us: dot(): lax.dot_general(left, right, (contract, ((), ())), preferred_element_type...]
    all_to_all x1, blocking collectives: 26.3 us -> 50.2 us  [exchange(): return lax.all_to_all(x, 'ctx', split_axis=0, concat_axis=0, tiled=True)]
  transfers between devices with their start and end apart: 54 -> 62, of which waited for: 33 -> 31; matrix products, arithmetic and copies ran while one was open for 5% -> 6% of each run, Pallas kernels for 14% -> 44%
where the time goes in v2:
time: 1220 us; the launch traced here: 1210 us
  Pallas kernels  532 us (44%)
  waiting for transfers between devices  454 us (37%)
  starting transfers between devices  68.3 us (6%)
  blocking collectives  50.2 us (4%)
  other arithmetic  48.9 us (4%)
  local copies, waits for them, and re-layouts  39.1 us (3%)
  between operations  15.7 us (1%)
    ppermute x18, waiting for transfers between devices, hop(): self.held.append(lax.ppermute(after(self.held[-1], prev), 'ctx', up))  230 us
    ppermute x18, waiting for transfers between devices, hop(): self.moved = lax.ppermute(part, 'ctx', up)  193 us
    pallas_call x2, Pallas kernels, expert_forward(): pl.pallas_call(kernel, grid=(stop - start, hidden // tile), in_specs=[who...  71.4 us
    pallas_call x1, Pallas kernels, expert_backward(): pl.pallas_call(kernel, grid=(experts, hidden // tile), in_specs=[whole(x)...  69.7 us
    pallas_call x1, Pallas kernels, expert_input_grad(): pl.pallas_call(kernel, grid=(width // tile, experts), in_specs=[line, lin...  66.3 us
    pallas_call x3, Pallas kernels, expert_weight_grad(): pl.pallas_call(kernel, grid=(stop - start, width // tile), in_specs=[pl.B...  65.1 us
    pallas_call x2, Pallas kernels, attention_backward(): pl.pallas_call(kernel, grid_spec=pltpu.PrefetchScalarGridSpec(num_scalar_...  56.3 us
    all_to_all x1, blocking collectives, exchange(): return lax.all_to_all(x, 'ctx', split_axis=0, concat_axis=0, tiled=True)  50.2 us
  transfers between devices with their start and end apart: 62, of which 31 were waited for; matrix products, arithmetic and copies ran while one was open for 6% of the time, Pallas kernels for 44%

profile of v2, /device:TPU:0, one launch (start us, length us, event | category | flops | bytes accessed | tf_op | source)
XLA Modules:
  0.0 1208.5 jit_solution(11682117086833694209)
XLA Ops:
  11.2 50.2 %all_to_all.30 = bf16[4,64,3712]{2,1,0:T(8,128)(2,1)} all-to-all(bf16[4,64,3712]{2,1,0:T(8,128)(2,1)S(1)} %broadcast_dynamic-update-slice_fusion.1), channel_id=1, replica_groups=mesh['batch'=8,'ctx'=4] {'ctx'}, dimensions={0} | all-to-all | bytes 3801088 | tf_op jit(solution)/shard_map/all_to_all | solution.py:782
  74.5 24.2 %collective-permute-done.3.refs_1_ = bf16[256,2048]{1,0:T(8,128)(2,1)S(1)} collective-permute-done((bf16[256,2048]{1,0:T(8,128)(2,1)S(1)}, bf16[256,2048]{1,0:T(8,128)(2,1)S(1)}, u32[]{:S(2)}, u32[]{:S(2)}) %collective-permute-start.3) | collective-permute-done | bytes 1048608 | tf_op jit(solution)/shard_map/ppermute | solution.py:748
  98.7 23.3 %collective-permute-done.4.refs_2_ = bf16[256,2048]{1,0:T(8,128)(2,1)S(1)} collective-permute-done((bf16[256,2048]{1,0:T(8,128)(2,1)S(1)}, bf16[256,2048]{1,0:T(8,128)(2,1)S(1)}, u32[]{:S(2)}, u32[]{:S(2)}) %collective-permute-start.4) | collective-permute-done | bytes 1048608 | tf_op jit(solution)/shard_map/ppermute | solution.py:748
  122.0 23.3 %collective-permute-done.5.refs_3_ = bf16[256,2048]{1,0:T(8,128)(2,1)S(1)} collective-permute-done((bf16[256,2048]{1,0:T(8,128)(2,1)S(1)}, bf16[256,2048]{1,0:T(8,128)(2,1)S(1)}, u32[]{:S(2)}, u32[]{:S(2)}) %collective-permute-start.5) | collective-permute-done | bytes 1048608 | tf_op jit(solution)/shard_map/ppermute | solution.py:748
  145.4 23.0 %collective-permute-done.6.refs_1_ = bf16[256,2048]{1,0:T(8,128)(2,1)} collective-permute-done((bf16[256,2048]{1,0:T(8,128)(2,1)S(1)}, bf16[256,2048]{1,0:T(8,128)(2,1)}, u32[]{:S(2)}, u32[]{:S(2)}) %collective-permute-start.6) | collective-permute-done | bytes 1048608 | tf_op jit(solution)/shard_map/ppermute | solution.py:748
  171.8 17.9 %project.2 = (bf16[1024,2048]{1,0:T(8,128)(2,1)}, f32[1024,1536]{1,0:T(8,128)}, f32[3,1024,1]{2,1,0:T(8,128)}) custom-call(bf16[256,2048]{1,0:T(8,128)(2,1)} %copy-done.14, bf16[256,2048]{1,0:T(8,128)(2,1)} %copy-done.68, bf16[256,2048]{1,0:T(8,128)(2,1)} %copy-done.70, bf16[256,2048]{1,0:T(8,128)(2,1)} %copy-done.71, f32[1,2048]{1,0:T(1,128)} %copy.188.refs_4_, ...), custom_call_target="tpu_custom_call" | custom-call | flops 6442450944 | bytes 14680064 | tf_op jit(solution)/shard_map/project/pallas_call | solution.py:98
  207.9 16.4 %attention.2 = (bf16[1,1024,512]{2,1,0:T(8,128)(2,1)}, bf16[1,1024,512]{2,1,0:T(8,128)(2,1)}, bf16[1,1024,512]{2,1,0:T(8,128)(2,1)}, bf16[4,1,256,512]{3,2,1,0:T(8,128)(2,1)}, f32[1,4,1024,1]{3,2,1,0:T(8,128)}) custom-call(s32[1]{0:T(128)} %bitcast.1.place_ref, s32[1]{0:T(128)} %bitcast.2.len_ref, f32[4,1,256,1536]{3,2,1,0:T(8,128)} %bitcast.152, ...), custom_call_target="tpu_custom_call" | custom-call | flops 1610612736 | bytes 10485760 | tf_op jit(solution)/shard_map/attention/pallas_call | solution.py:165
  229.7 17.9 %project.3 = (bf16[1024,2048]{1,0:T(8,128)(2,1)}, f32[1024,1536]{1,0:T(8,128)}, f32[3,1024,1]{2,1,0:T(8,128)}) custom-call(bf16[256,2048]{1,0:T(8,128)(2,1)} %copy-done.13, bf16[256,2048]{1,0:T(8,128)(2,1)} %collective-permute-done.6.refs_1_, bf16[256,2048]{1,0:T(8,128)(2,1)} %collective-permute-done.7.refs_2_, ...), custom_call_target="tpu_custom_call" | custom-call | flops 6442450944 | bytes 14680064 | tf_op jit(solution)/shard_map/project/pallas_call | solution.py:98
  265.7 16.4 %attention.3 = (bf16[1,1024,512]{2,1,0:T(8,128)(2,1)}, bf16[1,1024,512]{2,1,0:T(8,128)(2,1)}, bf16[1,1024,512]{2,1,0:T(8,128)(2,1)}, bf16[4,1,256,512]{3,2,1,0:T(8,128)(2,1)}, f32[1,4,1024,1]{3,2,1,0:T(8,128)}) custom-call(s32[1]{0:T(128)} %bitcast.1.place_ref, s32[1]{0:T(128)} %bitcast.31.len_ref, f32[4,1,256,1536]{3,2,1,0:T(8,128)} %bitcast.147, ...), custom_call_target="tpu_custom_call" | custom-call | flops 1610612736 | bytes 10485760 | tf_op jit(solution)/shard_map/attention/pallas_call | solution.py:165
  290.3 30.4 %collective-permute-done.16.refs_4_ = bf16[256,2048]{1,0:T(8,128)(2,1)} collective-permute-done((bf16[256,2048]{1,0:T(8,128)(2,1)}, bf16[256,2048]{1,0:T(8,128)(2,1)}, u32[]{:S(2)}, u32[]{:S(2)}) %collective-permute-start.16) | collective-permute-done | bytes 1048608 | tf_op jit(solution)/shard_map/ppermute | solution.py:748
  350.2 23.2 %collective-permute-done.18.refs_3_ = bf16[256,2048]{1,0:T(8,128)(2,1)} collective-permute-done((bf16[256,2048]{1,0:T(8,128)(2,1)}, bf16[256,2048]{1,0:T(8,128)(2,1)}, u32[]{:S(2)}, u32[]{:S(2)}) %collective-permute-start.18) | collective-permute-done | bytes 1048608 | tf_op jit(solution)/shard_map/ppermute | solution.py:748
  373.9 22.8 %collective-permute-done.19.refs_5_ = bf16[256,2048]{1,0:T(8,128)(2,1)} collective-permute-done((bf16[256,2048]{1,0:T(8,128)(2,1)}, bf16[256,2048]{1,0:T(8,128)(2,1)}, u32[]{:S(2)}, u32[]{:S(2)}) %collective-permute-start.19) | collective-permute-done | bytes 1048608 | tf_op jit(solution)/shard_map/ppermute | solution.py:748
  398.5 21.7 %collective-permute-done.20.refs_7_ = bf16[256,2048]{1,0:T(8,128)(2,1)S(1)} collective-permute-done((bf16[256,2048]{1,0:T(8,128)(2,1)}, bf16[256,2048]{1,0:T(8,128)(2,1)S(1)}, u32[]{:S(2)}, u32[]{:S(2)}) %collective-permute-start.20) | collective-permute-done | bytes 1048608 | tf_op jit(solution)/shard_map/ppermute | solution.py:748
  421.3 35.6 %expert_forward.2 = (bf16[4,1280,2048]{2,1,0:T(8,128)(2,1)}, bf16[4,1280,1024]{2,1,0:T(8,128)(2,1)}, bf16[4,1280,1024]{2,1,0:T(8,128)(2,1)}, bf16[4,1280,1024]{2,1,0:T(8,128)(2,1)}) custom-call(bf16[256,2048]{1,0:T(8,128)(2,1)} %get-tuple-element.192.refs_0_, bf16[256,2048]{1,0:T(8,128)(2,1)} %get-tuple-element.198.refs_1_, bf16[256,2048]{1,0:T(8,128)(2,1)} %copy-done.22, ...), custom_call_target="tpu_custom_call" | custom-call | flops 21474836480 | bytes 8388608 | tf_op jit(solution)/shard_map/expert_forward/pallas_call | solution.py:498
  466.3 35.7 %expert_forward.3 = (bf16[4,1280,2048]{2,1,0:T(8,128)(2,1)}, bf16[4,1280,1024]{2,1,0:T(8,128)(2,1)}, bf16[4,1280,1024]{2,1,0:T(8,128)(2,1)}, bf16[4,1280,1024]{2,1,0:T(8,128)(2,1)}) custom-call(bf16[256,2048]{1,0:T(8,128)(2,1)} %get-tuple-element.192.refs_0_, ...), custom_call_target="tpu_custom_call", output_to_operand_aliasing={{0}: (11, {}), {1}: (12, {}), {2}: (13, {}), {3}: (14, {})} | custom-call | flops 21474836480 | bytes 8388608 | tf_op jit(solution)/shard_map/expert_forward/pallas_call | solution.py:498
  511.9 41.1 %expert_output.1 = (bf16[256,2048]{1,0:T(8,128)(2,1)}, bf16[256,2048]{1,0:T(8,128)(2,1)}, bf16[256,2048]{1,0:T(8,128)(2,1)}, bf16[256,2048]{1,0:T(8,128)(2,1)}, ...) custom-call(bf16[4,1280,1024]{2,1,0:T(8,128)(2,1)} %get-tuple-elemen, ...), custom_call_target="tpu_custom_call" | custom-call | flops 21474836480 | bytes 35651584 | tf_op jit(solution)/shard_map/expert_output/pallas_call | solution.py:553
  558.6 69.7 %expert_backward.1 = (bf16[4,1280,1024]{2,1,0:T(8,128)(2,1)}, bf16[4,1280,1024]{2,1,0:T(8,128)(2,1)}, bf16[4,1024,2048]{2,1,0:T(8,128)(2,1)}) custom-call(bf16[256,2048]{1,0:T(8,128)(2,1)} %copy-done.8, bf16[256,2048]{1,0:T(8,128)(2,1)} %copy-done.7, bf16[256,2048]{1,0:T(8,128)(2,1)} %collective-permute-done.21.refs_2_, ...), custom_call_target="tpu_custom_call" | custom-call | flops 42949672960 | bytes 94371840 | tf_op jit(solution)/shard_map/expert_backward/pallas_call | solution.py:612
  637.6 66.3 %expert_input_grad.1 = (bf16[256,2048]{1,0:T(8,128)(2,1)}, bf16[256,2048]{1,0:T(8,128)(2,1)}, bf16[256,2048]{1,0:T(8,128)(2,1)}, bf16[256,2048]{1,0:T(8,128)(2,1...) custom-call(bf16[4,1280,1024]{2,1,0:T(8,128)(2,1)} %get-tuple-elemen, ...), custom_call_target="tpu_custom_call" | custom-call | flops 42949672960 | bytes 62914560 | tf_op jit(solution)/shard_map/expert_input_grad/pallas_call | solution.py:658
  704.0 17.3 %expert_weight_grad.3.rest_0_ = bf16[2,4,2048,1024]{3,2,1,0:T(8,128)(2,1)} custom-call(bf16[4,1280,2048]{2,1,0:T(8,128)(2,1)} %get-tuple-element.211.x_i, bf16[4,1280,1024]{2,1,0:T(8,128)(2,1)} %get-tuple-element.253.dg_i, bf16[4,1280,1024]{2,1,0:T(8,128)(2,1)} %get-tuple-element.235.du_i), custom_call_target="tpu_custom_call" | custom-call | flops 10737418240 | bytes 20971520 | tf_op jit(solution)/shard_map/expert_weight_grad/pallas_call | solution.py:689
  731.3 16.7 %expert_weight_grad.4.rest_0_ = bf16[2,4,2048,1024]{3,2,1,0:T(8,128)(2,1)} custom-call(bf16[4,1280,2048]{2,1,0:T(8,128)(2,1)} %get-tuple-element.211.x_i, bf16[4,1280,1024]{2,1,0:T(8,128)(2,1)} %get-tuple-element.253.dg_i, bf16[4,1280,1024]{2,1,0:T(8,128)(2,1)} %get-tuple-element.235.du_i, ...), custom_call_target="tpu_custom_call", output_to_operand_aliasing={{}: (3, {})} | custom-call | flops 10737418240 | bytes 20971520 | tf_op jit(solution)/shard_map/expert_weight_grad/pallas_call | solution.py:689
  759.5 31.1 %expert_weight_grad.5 = bf16[2,4,2048,1024]{3,2,1,0:T(8,128)(2,1)} custom-call(bf16[4,1280,2048]{2,1,0:T(8,128)(2,1)} %get-tuple-element.211.x_i, bf16[4,1280,1024]{2,1,0:T(8,128)(2,1)} %get-tuple-element.253.dg_i, bf16[4,1280,1024]{2,1,0:T(8,128)(2,1)} %get-tuple-element.235.du_i, ...), custom_call_target="tpu_custom_call", output_to_operand_aliasing={{}: (3, {})} | custom-call | flops 21474836480 | bytes 20971520 | tf_op jit(solution)/shard_map/expert_weight_grad/pallas_call | solution.py:689
  802.2 17.5 %collective-permute-done.34 = bf16[256,2048]{1,0:T(8,128)(2,1)S(1)} collective-permute-done((bf16[256,2048]{1,0:T(8,128)(2,1)}, bf16[256,2048]{1,0:T(8,128)(2,1)S(1)}, u32[]{:S(2)}, u32[]{:S(2)}) %collective-permute-start.34) | collective-permute-done | bytes 1048608 | tf_op jit(solution)/shard_map/ppermute | solution.py:763
  833.6 32.7 %collective-permute-done.35 = bf16[256,2048]{1,0:T(8,128)(2,1)} collective-permute-done((bf16[256,2048]{1,0:T(8,128)(2,1)S(1)}, bf16[256,2048]{1,0:T(8,128)(2,1)}, u32[]{:S(2)}, u32[]{:S(2)}) %collective-permute-start.35) | collective-permute-done | bytes 1048608 | tf_op jit(solution)/shard_map/ppermute | solution.py:763
  871.9 27.8 %attention_back.2 = (f32[4,1,256,512]{3,2,1,0:T(8,128)}, f32[4,1,256,512]{3,2,1,0:T(8,128)}, bf16[4,1,256,512]{3,2,1,0:T(8,128)(2,1)}, f32[2,1,4,4,256,1]{5,4,3,2,1,0:T(8,128)}, f32[2,1,1,512]{3,2,1,0:T(1,128)}) custom-call(s32[1]{0:T(128)} %bitcast.1.place_ref, s32[1]{0:T(128)} %bitcast.2.len_ref, bf16[1,1024,512]{2,1,0:T(8,128)(2,1)} %get-tuple-element.264.q_i, ...), custom_call_target="tpu_custom_call" | custom-call | flops 3758096384 | bytes 11534336 | tf_op jit(solution)/shard_map/attention_back/pallas_call | solution.py:249
  945.9 28.4 %attention_back.3 = (f32[4,1,256,512]{3,2,1,0:T(8,128)}, f32[4,1,256,512]{3,2,1,0:T(8,128)}, bf16[4,1,256,512]{3,2,1,0:T(8,128)(2,1)}, f32[2,1,4,4,256,1]{5,4,3,2,1,0:T(8,128)}, f32[2,1,1,512]{3,2,1,0:T(1,128)}) custom-call(s32[1]{0:T(128)} %bitcast.1.place_ref, s32[1]{0:T(128)} %bitcast.31.len_ref, bf16[1,1024,512]{2,1,0:T(8,128)(2,1)} %get-tuple-element.283.q_i, ...), custom_call_target="tpu_custom_call" | custom-call | flops 3758096384 | bytes 11534336 | tf_op jit(solution)/shard_map/attention_back/pallas_call | solution.py:249
  1003.9 24.8 %attention_weight_grads.1 = bf16[2048,3712]{1,0:T(8,128)(2,1)} custom-call(bf16[4,256,512]{2,1,0:T(8,128)(2,1)} %copy-done.11, bf16[4,256,512]{2,1,0:T(8,128)(2,1)} %copy-done.12, bf16[256,2048]{1,0:T(8,128)(2,1)} %get-tuple-element.255.refs_2_, bf16[256,2048]{1,0:T(8,128)(2,1)} %get-tuple-element.271.refs_3_, ...), custom_call_target="tpu_custom_call" | custom-call | flops 17179869184 | bytes 29884416 | tf_op jit(solution)/shard_map/attention_weight_grads/pallas_call | solution.py:429
  1030.8 27.6 %collective-permute-done.45 = bf16[256,2048]{1,0:T(8,128)(2,1)} collective-permute-done((bf16[256,2048]{1,0:T(8,128)(2,1)S(1)}, bf16[256,2048]{1,0:T(8,128)(2,1)}, u32[]{:S(2)}, u32[]{:S(2)}) %collective-permute-start.45) | collective-permute-done | bytes 1048608 | tf_op jit(solution)/shard_map/ppermute | solution.py:763
  1061.2 22.5 %collective-permute-done.47 = bf16[256,2048]{1,0:T(8,128)(2,1)S(1)} collective-permute-done((bf16[256,2048]{1,0:T(8,128)(2,1)S(1)}, bf16[256,2048]{1,0:T(8,128)(2,1)S(1)}, u32[]{:S(2)}, u32[]{:S(2)}) %collective-permute-start.47) | collective-permute-done | bytes 1048608 | tf_op jit(solution)/shard_map/ppermute | solution.py:763
  1083.7 16.3 %collective-permute-done.46 = bf16[256,2048]{1,0:T(8,128)(2,1)S(1)} collective-permute-done((bf16[256,2048]{1,0:T(8,128)(2,1)S(1)}, bf16[256,2048]{1,0:T(8,128)(2,1)S(1)}, u32[]{:S(2)}, u32[]{:S(2)}) %collective-permute-start.46) | collective-permute-done | bytes 1048608 | tf_op jit(solution)/shard_map/ppermute | solution.py:763
  1100.0 20.4 %collective-permute-done.48 = bf16[256,2048]{1,0:T(8,128)(2,1)S(1)} collective-permute-done((bf16[256,2048]{1,0:T(8,128)(2,1)S(1)}, bf16[256,2048]{1,0:T(8,128)(2,1)S(1)}, u32[]{:S(2)}, u32[]{:S(2)}) %collective-permute-start.48) | collective-permute-done | bytes 1048608 | tf_op jit(solution)/shard_map/ppermute | solution.py:763
  1120.9 16.5 %collective-permute-done.49 = bf16[256,2048]{1,0:T(8,128)(2,1)S(1)} collective-permute-done((bf16[256,2048]{1,0:T(8,128)(2,1)S(1)}, bf16[256,2048]{1,0:T(8,128)(2,1)S(1)}, u32[]{:S(2)}, u32[]{:S(2)}) %collective-permute-start.49) | collective-permute-done | bytes 1048608 | tf_op jit(solution)/shard_map/ppermute | solution.py:763
  1148.3 18.8 %collective-permute-done.50 = bf16[256,2048]{1,0:T(8,128)(2,1)} collective-permute-done((bf16[256,2048]{1,0:T(8,128)(2,1)}, bf16[256,2048]{1,0:T(8,128)(2,1)}, u32[]{:S(2)}, u32[]{:S(2)}) %collective-permute-start.50) | collective-permute-done | bytes 1048608 | tf_op jit(solution)/shard_map/ppermute | solution.py:763
  (377 shorter events, 314.8 us)
Async XLA Ops:
  7.2 161.3 %all-gather.4.cloned.1.call-start = ((), (), s32[]{:S(2)}) async-start(), calls=%async_computation.9 | async-start | bytes 17104896 | tf_op jit(solution)/shard_map/all_gather | solution.py:793
  61.4 358.9 %all-gather.6.cloned.1.call-start = ((), (), s32[]{:S(2)}) async-start(), calls=%async_computation.10 | async-start | bytes 37748736 | tf_op jit(solution)/shard_map/all_gather | solution.py:796
  66.1 445.8 %all-gather.8.cloned.1.call-start = ((), (), s32[]{:S(2)}) async-start(), calls=%async_computation.11 | async-start | bytes 18874368 | tf_op jit(solution)/shard_map/all_gather | solution.py:799
  283.2 42.9 %all-to-all-start.2 = ((bf16[4,256,512]{2,1,0:T(8,128)(2,1)}), bf16[4,256,512]{2,1,0:T(8,128)(2,1)S(1)}, u32[]{:S(2)}, u32[]{:S(2)}) async-start(bf16[4,256,512]{2,1,0:T(8,128)(2,1)} %bitcast.178), calls=%async_computation.2 | async-start | bytes 2097152 | tf_op jit(solution)/shard_map/all_to_all | solution.py:782
  288.3 502.4 %reduce-scatter.4.cloned.1.call-start = ((), (), s32[]{:S(2)}) async-start(), calls=%async_computation.12 | async-start | bytes 18874368 | tf_op jit(solution)/shard_map/reduce_scatter | solution.py:919
  288.3 32.4 %collective-permute-start.16 = (bf16[256,2048]{1,0:T(8,128)(2,1)}, bf16[256,2048]{1,0:T(8,128)(2,1)}, u32[]{:S(2)}, u32[]{:S(2)}) collective-permute-start(bf16[256,2048]{1,0:T(8,128)(2,1)} %copy-done.22), channel_id=1, source_target_pairs={{0,1},{1,2},{2,3},{3,0},{4,5},{5,6},{6,7},{7,4},{8,9},{9,10},{10,1... | collective-permute-start | bytes 3145736 | tf_op jit(solution)/shard_map/ppermute | solution.py:748
  420.3 36.6 %collective-permute-start.22 = (bf16[256,2048]{1,0:T(8,128)(2,1)S(1)}, bf16[256,2048]{1,0:T(8,128)(2,1)}, u32[]{:S(2)}, u32[]{:S(2)}) collective-permute-start(bf16[256,2048]{1,0:T(8,128)(2,1)S(1)} %get-tuple-element.208.refs_1_.l_i), channel_id=1, source_target_pairs={{0,1},{1,2},{2,3},{3,0},{4,5},{5,6},{6,7},{7,4},{8,9},{9,10},{10,1... | collective-permute-start | bytes 3145736 | tf_op jit(solution)/shard_map/ppermute | solution.py:748
  420.3 45.6 %collective-permute-start.21 = (bf16[256,2048]{1,0:T(8,128)(2,1)S(1)}, bf16[256,2048]{1,0:T(8,128)(2,1)}, u32[]{:S(2)}, u32[]{:S(2)}) collective-permute-start(bf16[256,2048]{1,0:T(8,128)(2,1)S(1)} %get-tuple-element.207.refs_0_.l_i), channel_id=1, source_target_pairs={{0,1},{1,2},{2,3},{3,0},{4,5},{5,6},{6,7},{7,4},{8,9},{9,10},{10,1... | collective-permute-start | bytes 3145736 | tf_op jit(solution)/shard_map/ppermute | solution.py:748
  465.9 36.1 %collective-permute-start.23 = (bf16[256,2048]{1,0:T(8,128)(2,1)}, bf16[256,2048]{1,0:T(8,128)(2,1)S(1)}, u32[]{:S(2)}, u32[]{:S(2)}) collective-permute-start(bf16[256,2048]{1,0:T(8,128)(2,1)} %collective-permute-done.21.refs_2_), channel_id=1, source_target_pairs={{0,1},{1,2},{2,3},{3,0},{4,5},{5,6},{6,7},{7,4},{8,9},{9,10},{10,1... | collective-permute-start | bytes 3145736 | tf_op jit(solution)/shard_map/ppermute | solution.py:748
  465.9 46.0 %collective-permute-start.24 = (bf16[256,2048]{1,0:T(8,128)(2,1)}, bf16[256,2048]{1,0:T(8,128)(2,1)S(1)}, u32[]{:S(2)}, u32[]{:S(2)}) collective-permute-start(bf16[256,2048]{1,0:T(8,128)(2,1)} %collective-permute-done.22.refs_3_), channel_id=1, source_target_pairs={{0,1},{1,2},{2,3},{3,0},{4,5},{5,6},{6,7},{7,4},{8,9},{9,10},{10,1... | collective-permute-start | bytes 3145736 | tf_op jit(solution)/shard_map/ppermute | solution.py:748
  511.9 41.1 %collective-permute-start.25 = (bf16[256,2048]{1,0:T(8,128)(2,1)S(1)}, bf16[256,2048]{1,0:T(8,128)(2,1)S(1)}, u32[]{:S(2)}, u32[]{:S(2)}) collective-permute-start(bf16[256,2048]{1,0:T(8,128)(2,1)S(1)} %collective-permute-done.23.refs_4_), channel_id=1, source_target_pairs={{0,1},{1,2},{2,3},{3,0},{4,5},{5,6},{6,7},{7,4},{8,9},{9,10},{10,1... | collective-permute-start | bytes 3145736 | tf_op jit(solution)/shard_map/ppermute | solution.py:748
  511.9 45.6 %collective-permute-start.26 = (bf16[256,2048]{1,0:T(8,128)(2,1)S(1)}, bf16[256,2048]{1,0:T(8,128)(2,1)}, u32[]{:S(2)}, u32[]{:S(2)}) collective-permute-start(bf16[256,2048]{1,0:T(8,128)(2,1)S(1)} %collective-permute-done.24.refs_5_), channel_id=1, source_target_pairs={{0,1},{1,2},{2,3},{3,0},{4,5},{5,6},{6,7},{7,4},{8,9},{9,10},{10,1... | collective-permute-start | bytes 3145736 | tf_op jit(solution)/shard_map/ppermute | solution.py:748
  557.5 70.9 %collective-permute-start.27 = (bf16[256,2048]{1,0:T(8,128)(2,1)}, bf16[256,2048]{1,0:T(8,128)(2,1)S(1)}, u32[]{:S(2)}, u32[]{:S(2)}) collective-permute-start(bf16[256,2048]{1,0:T(8,128)(2,1)} %get-tuple-element.228), channel_id=1, source_target_pairs={{0,1},{1,2},{2,3},{3,0},{4,5},{5,6},{6,7},{7,4},{8,9},{9,10},{10,1... | collective-permute-start | bytes 3145736 | tf_op jit(solution)/shard_map/ppermute | solution.py:763
  557.5 70.9 %collective-permute-start.28 = (bf16[256,2048]{1,0:T(8,128)(2,1)}, bf16[256,2048]{1,0:T(8,128)(2,1)S(1)}, u32[]{:S(2)}, u32[]{:S(2)}) collective-permute-start(bf16[256,2048]{1,0:T(8,128)(2,1)} %get-tuple-element.231), channel_id=1, source_target_pairs={{0,1},{1,2},{2,3},{3,0},{4,5},{5,6},{6,7},{7,4},{8,9},{9,10},{10,1... | collective-permute-start | bytes 3145736 | tf_op jit(solution)/shard_map/ppermute | solution.py:763
  629.3 399.4 %reduce-scatter.6.cloned.1.call-start = ((), (), s32[]{:S(2)}) async-start(), calls=%async_computation.13 | async-start | bytes 37748736 | tf_op jit(solution)/shard_map/reduce_scatter | solution.py:934
  633.1 70.8 %collective-permute-start.29 = (bf16[256,2048]{1,0:T(8,128)(2,1)}, bf16[256,2048]{1,0:T(8,128)(2,1)S(1)}, u32[]{:S(2)}, u32[]{:S(2)}) collective-permute-start(bf16[256,2048]{1,0:T(8,128)(2,1)} %add_convert_fusion.11), channel_id=1, source_target_pairs={{0,1},{1,2},{2,3},{3,0},{4,5},{5,6},{6,7},{7,4},{8,9},{9,10},{10,1... | collective-permute-start | bytes 3145736 | tf_op jit(solution)/shard_map/ppermute | solution.py:763
  633.6 70.4 %collective-permute-start.30 = (bf16[256,2048]{1,0:T(8,128)(2,1)S(1)}, bf16[256,2048]{1,0:T(8,128)(2,1)S(1)}, u32[]{:S(2)}, u32[]{:S(2)}) collective-permute-start(bf16[256,2048]{1,0:T(8,128)(2,1)S(1)} %add_convert_fusion.10), channel_id=1, source_target_pairs={{0,1},{1,2},{2,3},{3,0},{4,5},{5,6},{6,7},{7,4},{8,9},{9,10},{10,1... | collective-permute-start | bytes 3145736 | tf_op jit(solution)/shard_map/ppermute | solution.py:763
  703.9 26.9 %collective-permute-start.31 = (bf16[256,2048]{1,0:T(8,128)(2,1)}, bf16[256,2048]{1,0:T(8,128)(2,1)S(1)}, u32[]{:S(2)}, u32[]{:S(2)}) collective-permute-start(bf16[256,2048]{1,0:T(8,128)(2,1)} %get-tuple-element.246), channel_id=1, source_target_pairs={{0,1},{1,2},{2,3},{3,0},{4,5},{5,6},{6,7},{7,4},{8,9},{9,10},{10,1... | collective-permute-start | bytes 3145736 | tf_op jit(solution)/shard_map/ppermute | solution.py:763
  731.2 27.8 %collective-permute-start.32 = (bf16[256,2048]{1,0:T(8,128)(2,1)S(1)}, bf16[256,2048]{1,0:T(8,128)(2,1)S(1)}, u32[]{:S(2)}, u32[]{:S(2)}) collective-permute-start(bf16[256,2048]{1,0:T(8,128)(2,1)S(1)} %add_convert_fusion.9), channel_id=1, source_target_pairs={{0,1},{1,2},{2,3},{3,0},{4,5},{5,6},{6,7},{7,4},{8,9},{9,10},{10,1... | collective-permute-start | bytes 3145736 | tf_op jit(solution)/shard_map/ppermute | solution.py:763
  759.4 31.2 %collective-permute-start.33 = (bf16[256,2048]{1,0:T(8,128)(2,1)S(1)}, bf16[256,2048]{1,0:T(8,128)(2,1)S(1)}, u32[]{:S(2)}, u32[]{:S(2)}) collective-permute-start(bf16[256,2048]{1,0:T(8,128)(2,1)S(1)} %add_convert_fusion.8), channel_id=1, source_target_pairs={{0,1},{1,2},{2,3},{3,0},{4,5},{5,6},{6,7},{7,4},{8,9},{9,10},{10,1... | collective-permute-start | bytes 3145736 | tf_op jit(solution)/shard_map/ppermute | solution.py:763
  791.6 28.1 %collective-permute-start.34 = (bf16[256,2048]{1,0:T(8,128)(2,1)}, bf16[256,2048]{1,0:T(8,128)(2,1)S(1)}, u32[]{:S(2)}, u32[]{:S(2)}) collective-permute-start(bf16[256,2048]{1,0:T(8,128)(2,1)} %get-tuple-element.256), channel_id=1, source_target_pairs={{0,1},{1,2},{2,3},{3,0},{4,5},{5,6},{6,7},{7,4},{8,9},{9,10},{10,1... | collective-permute-start | bytes 3145736 | tf_op jit(solution)/shard_map/ppermute | solution.py:763
  820.7 47.4 %all-to-all-start.3 = ((bf16[4,256,512]{2,1,0:T(8,128)(2,1)}), bf16[4,256,512]{2,1,0:T(8,128)(2,1)S(1)}, u32[]{:S(2)}, u32[]{:S(2)}) async-start(bf16[4,256,512]{2,1,0:T(8,128)(2,1)} %get-tuple-element.260), calls=%async_computation.3 | async-start | bytes 2097152 | tf_op jit(solution)/shard_map/all_to_all | solution.py:782
  831.6 34.8 %collective-permute-start.35 = (bf16[256,2048]{1,0:T(8,128)(2,1)S(1)}, bf16[256,2048]{1,0:T(8,128)(2,1)}, u32[]{:S(2)}, u32[]{:S(2)}) collective-permute-start(bf16[256,2048]{1,0:T(8,128)(2,1)S(1)} %add_convert_fusion.7), channel_id=1, source_target_pairs={{0,1},{1,2},{2,3},{3,0},{4,5},{5,6},{6,7},{7,4},{8,9},{9,10},{10,1... | collective-permute-start | bytes 3145736 | tf_op jit(solution)/shard_map/ppermute | solution.py:763
  870.1 32.5 %collective-permute-start.36 = (bf16[256,2048]{1,0:T(8,128)(2,1)S(1)}, bf16[256,2048]{1,0:T(8,128)(2,1)S(1)}, u32[]{:S(2)}, u32[]{:S(2)}) collective-permute-start(bf16[256,2048]{1,0:T(8,128)(2,1)S(1)} %add_convert_fusion.6), channel_id=1, source_target_pairs={{0,1},{1,2},{2,3},{3,0},{4,5},{5,6},{6,7},{7,4},{8,9},{9,10},{10,1... | collective-permute-start | bytes 3145736 | tf_op jit(solution)/shard_map/ppermute | solution.py:763
  921.1 221.7 %reduce-scatter.8.cloned.1.call-start = ((), (), s32[]{:S(2)}) async-start(), calls=%async_computation.14 | async-start | bytes 17104896 | tf_op jit(solution)/shard_map/reduce_scatter | solution.py:1015
  940.4 36.7 %collective-permute-start.40 = (bf16[256,2048]{1,0:T(8,128)(2,1)}, bf16[256,2048]{1,0:T(8,128)(2,1)S(1)}, u32[]{:S(2)}, u32[]{:S(2)}) collective-permute-start(bf16[256,2048]{1,0:T(8,128)(2,1)} %get-tuple-element.292), channel_id=1, source_target_pairs={{0,1},{1,2},{2,3},{3,0},{4,5},{5,6},{6,7},{7,4},{8,9},{9,10},{10,1... | collective-permute-start | bytes 3145736 | tf_op jit(solution)/shard_map/ppermute | solution.py:763
  1030.3 28.1 %collective-permute-start.45 = (bf16[256,2048]{1,0:T(8,128)(2,1)S(1)}, bf16[256,2048]{1,0:T(8,128)(2,1)}, u32[]{:S(2)}, u32[]{:S(2)}) collective-permute-start(bf16[256,2048]{1,0:T(8,128)(2,1)S(1)} %add_convert_fusion.4), channel_id=1, source_target_pairs={{0,1},{1,2},{2,3},{3,0},{4,5},{5,6},{6,7},{7,4},{8,9},{9,10},{10,1... | collective-permute-start | bytes 3145736 | tf_op jit(solution)/shard_map/ppermute | solution.py:763
  1058.8 24.9 %collective-permute-start.47 = (bf16[256,2048]{1,0:T(8,128)(2,1)S(1)}, bf16[256,2048]{1,0:T(8,128)(2,1)S(1)}, u32[]{:S(2)}, u32[]{:S(2)}) collective-permute-start(bf16[256,2048]{1,0:T(8,128)(2,1)S(1)} %add_convert_fusion.2), channel_id=1, source_target_pairs={{0,1},{1,2},{2,3},{3,0},{4,5},{5,6},{6,7},{7,4},{8,9},{9,10},{10,1... | collective-permute-start | bytes 3145736 | tf_op jit(solution)/shard_map/ppermute | solution.py:763
  1059.3 40.7 %collective-permute-start.46 = (bf16[256,2048]{1,0:T(8,128)(2,1)S(1)}, bf16[256,2048]{1,0:T(8,128)(2,1)S(1)}, u32[]{:S(2)}, u32[]{:S(2)}) collective-permute-start(bf16[256,2048]{1,0:T(8,128)(2,1)S(1)} %add_convert_fusion.3), channel_id=1, source_target_pairs={{0,1},{1,2},{2,3},{3,0},{4,5},{5,6},{6,7},{7,4},{8,9},{9,10},{10,1... | collective-permute-start | bytes 3145736 | tf_op jit(solution)/shard_map/ppermute | solution.py:763
  1061.1 59.3 %collective-permute-start.48 = (bf16[256,2048]{1,0:T(8,128)(2,1)S(1)}, bf16[256,2048]{1,0:T(8,128)(2,1)S(1)}, u32[]{:S(2)}, u32[]{:S(2)}) collective-permute-start(bf16[256,2048]{1,0:T(8,128)(2,1)S(1)} %copy-done.65), channel_id=1, source_target_pairs={{0,1},{1,2},{2,3},{3,0},{4,5},{5,6},{6,7},{7,4},{8,9},{9,10},{10,1... | collective-permute-start | bytes 3145736 | tf_op jit(solution)/shard_map/ppermute | solution.py:763
  1138.9 28.2 %collective-permute-start.50 = (bf16[256,2048]{1,0:T(8,128)(2,1)}, bf16[256,2048]{1,0:T(8,128)(2,1)}, u32[]{:S(2)}, u32[]{:S(2)}) collective-permute-start(bf16[256,2048]{1,0:T(8,128)(2,1)} %add_convert_fusion), channel_id=1, source_target_pairs={{0,1},{1,2},{2,3},{3,0},{4,5},{5,6},{6,7},{7,4},{8,9},{9,10},{10,1... | collective-permute-start | bytes 3145736 | tf_op jit(solution)/shard_map/ppermute | solution.py:763
  1142.7 52.7 %all-to-all-start.5 = ((bf16[4,64,3712]{2,1,0:T(8,128)(2,1)}), bf16[4,64,3712]{2,1,0:T(8,128)(2,1)}, u32[]{:S(2)}, u32[]{:S(2)}) async-start(bf16[4,64,3712]{2,1,0:T(8,128)(2,1)} %bitcast.171), calls=%async_computation.8 | async-start | bytes 3801088 | tf_op jit(solution)/shard_map/all_to_all | solution.py:782
  (102 other events, 1964.7 us)
Sparse Core Ops, SparseCore 0:
  61.5 82.3 all-gather.3
  146.4 160.7 all-gather.5
  309.1 93.1 all-gather.7
  629.5 116.6 reduce-scatter.3
  790.8 205.9 reduce-scatter.5
  1028.9 106.3 reduce-scatter.7

commit v3 on v2

--- a/solution.py
+++ b/solution.py
@@ -11,7 +11,7 @@
 MASKED = -1e30
 LANES = 128
 ROOM = 58 << 20
-SLIM = 1
+SLIM = 8
 
 f32 = jnp.float32
 bf16 = jnp.bfloat16
@@ -49,13 +49,6 @@
     return pltpu.CompilerParams(
         dimension_semantics=("arbitrary",) * axes, vmem_limit_bytes=ROOM
     )
-
-
-def chunks_of(blocks, cap):
-    parts = max(1, (blocks * cap) // 640)
-    while blocks % parts:
-        parts -= 1
-    return parts
 
 
 def project(pieces, gain, weight, third, first):
@@ -410,36 +403,37 @@
     )(moved, part, low, hidden, gain, weight)
 
 
-def attention_weight_grads(atts, datts, normeds, lows, columns):
-    count = len(atts)
-    n, rows, cols = atts[0].shape
-    width = n * cols
-    total, wide = lows[0].shape
+def weight_grads(lefts, rights, columns, name):
+    count = len(lefts)
+    total, wide = rights[0].shape
+    folded = len(lefts[0].shape) == 3
+    width = columns.shape[0]
+    tile = lefts[0].shape[2] if folded else min(512, width)
 
     def kernel(*refs):
-        at, da, nm, lw = (refs[i * count : (i + 1) * count] for i in range(4))
-        column_ref, o = refs[4 * count :]
-        o[:, :width] = sum(dot_tn(at[g][0], da[g][...]) for g in range(count)).astype(bf16)
-        o[:, width : width + wide] = sum(
-            dot_tn(nm[g][...], lw[g][...]) for g in range(count)
+        ls, rs, (column_ref, o) = refs[:count], refs[count : 2 * count], refs[2 * count :]
+        o[:, :wide] = sum(
+            dot_tn(ls[g][0] if folded else ls[g][...], rs[g][...]) for g in range(count)
         ).astype(bf16)
-        o[:, width + wide :] = column_ref[...]
-
-    out = struct((width, width + wide + LANES), bf16)
-    return pl.pallas_call(
-        kernel,
-        grid=(n,),
-        in_specs=[pl.BlockSpec((1, rows, cols), lambda p: (p, 0, 0)) for _ in atts]
-        + [whole(x) for x in datts]
-        + [pl.BlockSpec((total, cols), lambda p: (0, p)) for _ in normeds]
-        + [whole(x) for x in lows]
-        + [pl.BlockSpec((cols, LANES), lambda p: (p, 0))],
-        out_specs=pl.BlockSpec((cols, width + wide + LANES), lambda p: (p, 0)),
+        o[:, wide:] = column_ref[...]
+
+    if folded:
+        left = pl.BlockSpec((1, total, tile), lambda p: (p, 0, 0))
+    else:
+        left = pl.BlockSpec((total, tile), lambda p: (0, p))
+    out = struct((width, wide + LANES), bf16)
+    return pl.pallas_call(
+        kernel,
+        grid=(width // tile,),
+        in_specs=[left] * count
+        + [whole(x) for x in rights]
+        + [pl.BlockSpec((tile, LANES), lambda p: (p, 0))],
+        out_specs=pl.BlockSpec((tile, wide + LANES), lambda p: (p, 0)),
         out_shape=out,
         compiler_params=params(1),
-        cost_estimate=cost(2 * count * width * (rows * width + total * wide), *normeds, *lows, out),
-        name="attention_weight_grads",
-    )(*atts, *datts, *normeds, *lows, columns)
+        cost_estimate=cost(2 * count * total * width * wide, *lefts, *rights, out),
+        name=name,
+    )(*lefts, *rights, columns)
 
 
 def picks(rank_ref, nb, cap):
@@ -466,8 +460,6 @@
     width, hidden = gate_up.shape[1:]
     slots = blocks * cap
     tile = min(256, hidden)
-    parts = chunks_of(blocks, cap)
-    part = slots // parts
     more, more_specs, aliases = in_place(begun, blocks + 3)
 
     def kernel(*refs):
@@ -483,15 +475,12 @@
                 hot = picks(rank_ref, nb, cap).astype(bf16)
                 x_o[0, nb * cap : (nb + 1) * cap, :] = dot(hot, xs[nb][...]).astype(bf16)
 
-        @pl.loop(0, parts)
-        def _(i):
-            at = pl.ds(pl.multiple_of(i * part, part), part)
-            x = x_o[0, at, :]
-            gate = dot(x, wg[0])
-            upper = dot(x, wu[0])
-            g_o[0, at, :] = gate.astype(bf16)
-            u_o[0, at, :] = upper.astype(bf16)
-            a_o[0, at, :] = (gate * jax.nn.sigmoid(gate) * upper).astype(bf16)
+        x = x_o[0]
+        gate = dot(x, wg[0])
+        upper = dot(x, wu[0])
+        g_o[0] = gate.astype(bf16)
+        u_o[0] = upper.astype(bf16)
+        a_o[0] = (gate * jax.nn.sigmoid(gate) * upper).astype(bf16)
 
     tiled = pl.BlockSpec((1, slots, tile), lambda e, f: (start + e, 0, f))
     outs = (struct((experts, slots, width), bf16),) + (struct((experts, slots, hidden), bf16),) * 3
@@ -524,8 +513,6 @@
     hidden, width = down.shape[1:]
     slots = blocks * cap
     tile = min(512, width)
-    parts = chunks_of(blocks, cap)
-    per = blocks // parts
 
     def kernel(a_i, rank_ref, coef_ref, wd, *rest):
         outs, acc = rest[:blocks], rest[blocks]
@@ -535,13 +522,11 @@
         def _():
             acc[...] = jnp.zeros_like(acc)
 
-        for i in range(parts):
-            y = dot(a_i[0, i * per * cap : (i + 1) * per * cap, :], wd[0])
-            for m in range(per):
-                nb = i * per + m
-                hot = picks(rank_ref, nb, cap)
-                weighed = y[m * cap : (m + 1) * cap, :] * slot_weight(hot, coef_ref, nb)
-                acc[nb] += dot_tn(hot.astype(bf16), weighed.astype(bf16))
+        y = dot(a_i[0], wd[0])
+        for nb in range(blocks):
+            hot = picks(rank_ref, nb, cap)
+            weighed = y[nb * cap : (nb + 1) * cap, :] * slot_weight(hot, coef_ref, nb)
+            acc[nb] += dot_tn(hot.astype(bf16), weighed.astype(bf16))
 
         @pl.when(e == experts - 1)
         def _():
@@ -573,8 +558,6 @@
     hidden, width = down.shape[1:]
     slots = blocks * cap
     tile = min(256, hidden)
-    parts = chunks_of(blocks, cap)
-    part = slots // parts
 
     def kernel(*refs):
         ds, (rank_ref, coef_ref, wd, g_i, u_i, a_i), (dg_o, du_o, dw_o, dy) = (
@@ -592,16 +575,11 @@
                     picked * slot_weight(hot, coef_ref, nb)
                 ).astype(bf16)
 
-        @pl.loop(0, parts)
-        def _(i):
-            at = pl.ds(pl.multiple_of(i * part, part), part)
-            da = dot_nt(dy[at, :], wd[0])
-            g = g_i[0, at, :].astype(f32)
-            s = jax.nn.sigmoid(g)
-            du_o[0, at, :] = (da * g * s).astype(bf16)
-            dg_o[0, at, :] = (
-                da * u_i[0, at, :].astype(f32) * s * (1.0 + g * (1.0 - s))
-            ).astype(bf16)
+        da = dot_nt(dy[...], wd[0])
+        g = g_i[0].astype(f32)
+        s = jax.nn.sigmoid(g)
+        du_o[0] = (da * g * s).astype(bf16)
+        dg_o[0] = (da * u_i[0].astype(f32) * s * (1.0 + g * (1.0 - s))).astype(bf16)
 
         dw_o[0] = dot_tn(a_i[0], dy[...]).astype(bf16)
 
@@ -624,13 +602,12 @@
     )(*pieces, rank, coef, down, gate, upper, active)
 
 
-def expert_input_grad(dgate, dupper, rank, gate_up, cap):
-    experts, blocks, rows = rank.shape
+def expert_input_grad(dgate, dupper, rank, gate_up, cap, g, seqs):
+    blocks, rows = rank.shape[1:]
     width, hidden = gate_up.shape[1:]
+    experts = gate_up.shape[0] // 2
     slots = blocks * cap
-    tile = min(512, width)
-    parts = chunks_of(blocks, cap)
-    per = blocks // parts
+    tile = min(1024, width)
 
     def kernel(dg_i, du_i, rank_ref, wg, wu, *rest):
         outs, acc = rest[:blocks], rest[blocks]
@@ -640,20 +617,17 @@
         def _():
             acc[...] = jnp.zeros_like(acc)
 
-        for i in range(parts):
-            at = slice(i * per * cap, (i + 1) * per * cap)
-            dx = (dot_nt(dg_i[0, at, :], wg[0]) + dot_nt(du_i[0, at, :], wu[0])).astype(bf16)
-            for m in range(per):
-                nb = i * per + m
-                hot = picks(rank_ref, nb, cap).astype(bf16)
-                acc[nb] += dot_tn(hot, dx[m * cap : (m + 1) * cap, :])
+        dx = (dot_nt(dg_i[0], wg[0]) + dot_nt(du_i[0], wu[0])).astype(bf16)
+        for nb in range(blocks):
+            hot = picks(rank_ref, nb, cap).astype(bf16)
+            acc[nb] += dot_tn(hot, dx[nb * cap : (nb + 1) * cap, :])
 
         @pl.when(e == experts - 1)
         def _():
             for nb in range(blocks):
                 outs[nb][...] = acc[nb].astype(bf16)
 
-    line = pl.BlockSpec((1, slots, hidden), lambda d, e: (e, 0, 0))
+    line = pl.BlockSpec((1, slots, hidden), lambda d, e: (e, g, 0))
     outs = (struct((rows, width), bf16),) * blocks
     return pl.pallas_call(
         kernel,
@@ -661,7 +635,7 @@
         in_specs=[
             line,
             line,
-            pl.BlockSpec((1, blocks, rows), lambda d, e: (e, 0, 0)),
+            pl.BlockSpec((1, blocks, rows), lambda d, e: (e * seqs + g, 0, 0)),
             pl.BlockSpec((1, tile, hidden), lambda d, e: (e, d, 0)),
             pl.BlockSpec((1, tile, hidden), lambda d, e: (experts + e, d, 0)),
         ],
@@ -669,7 +643,7 @@
         out_shape=outs,
         scratch_shapes=[pltpu.VMEM((blocks, rows, tile), f32)],
         compiler_params=params(2),
-        cost_estimate=cost(4 * experts * slots * width * hidden, dgate, dupper, gate_up, *outs),
+        cost_estimate=cost(4 * experts * slots * width * hidden, gate_up, *outs),
         name="expert_input_grad",
     )(dgate, dupper, rank, gate_up, gate_up)
 
@@ -677,7 +651,7 @@
 def expert_weight_grad(x, dgate, dupper, start, stop, begun=None):
     experts, slots, width = x.shape
     hidden = dgate.shape[2]
-    tile = min(256, width)
+    tile = min(512, width)
     more, more_specs, aliases = in_place(begun, 3)
 
     def kernel(x_i, dg_i, du_i, *rest):
@@ -783,20 +757,28 @@
 
     gains = jnp.stack([attn_gain, query_gain, key_gain, ffn_gain], axis=1)
     gains = jnp.pad(gains, ((0, 0), (0, LANES - 4)))
+    sent = jnp.stack(
+        [
+            jnp.swapaxes(expert_ids.reshape(seqs, rows, top), 1, 2),
+            jnp.swapaxes(route_levels.reshape(seqs, rows, top), 1, 2),
+        ]
+    )
+    sent = sent.astype(bf16).reshape(own, -1)
+    extra = sent.shape[1]
     mine = jnp.concatenate(
         [jnp.broadcast_to(w_out[None], (n, own, width))]
         + [jnp.swapaxes(w.reshape(own, n, cols), 0, 1) for w in (w_query, w_key, w_value)]
-        + [jnp.broadcast_to(gains[None], (n, own, LANES))],
+        + [jnp.broadcast_to(one[None], (n, *one.shape)) for one in (gains, sent)],
         axis=2,
     )
-    mine = exchange(mine).reshape(n * own, -1)
+    mine = exchange(mine)
+    routes = mine[:, :, -extra:].reshape(n, 2, seqs, top, rows)
+    order = lax.rem(here + n - jnp.arange(n, dtype=jnp.int32), n)
+    routes = jnp.take(routes, order, axis=0)
+    mine = mine.reshape(n * own, -1)
     att_w = lax.all_gather(mine, "batch", axis=0, tiled=True)
     all_gains = att_w[:, width + 3 * cols : width + 3 * cols + 4].astype(f32).T
     gain_attn, gain_ffn = all_gains[0], all_gains[3]
-    gate_up = lax.all_gather(
-        after(jnp.concatenate([w_gate, w_up], axis=0), mine), "batch", axis=1, tiled=True
-    )
-    down = lax.all_gather(after(w_down, mine), "batch", axis=2, tiled=True)
     qk_gains = lax.dynamic_slice_in_dim(all_gains[1:3], here * cols, cols, 1).reshape(2, 1, cols)
 
     xs = tokens.reshape(seqs, rows, width)
@@ -804,27 +786,21 @@
     local_pos = here * rows + jnp.arange(rows, dtype=jnp.int32)
     live = (local_pos[None, :] < span_len[:, None])[:, :, None]
     grad_low = jnp.where(live, cotangent.reshape(seqs, rows, width), jnp.zeros((), bf16))
-    sent = jnp.stack(
-        [
-            jnp.swapaxes(expert_ids.reshape(seqs, rows, top), 1, 2),
-            jnp.swapaxes(route_levels.reshape(seqs, rows, top), 1, 2),
-        ]
-    )
-    routes = jnp.stack(direct(sent))
-    chosen = routes[:, 0].reshape(blocks, top, rows)
-    levels = routes[:, 1].reshape(blocks, top, rows).astype(f32)
-    share = levels / jnp.sum(levels, axis=1, keepdims=True)
-    owned = here * experts + jnp.arange(experts, dtype=jnp.int32)
-    hit = chosen[None] == owned[:, None, None, None]
-    named = jnp.any(hit, axis=2)
-    coef = jnp.sum(jnp.where(hit, share[None], 0.0), axis=2)
-    upto = (
-        jnp.arange(rows, dtype=jnp.int32)[:, None] <= jnp.arange(rows, dtype=jnp.int32)[None, :]
-    ).astype(bf16)
-    count = jnp.dot(
-        named.astype(bf16).reshape(experts * blocks, rows), upto, preferred_element_type=f32
-    )
-    rank = jnp.where(named, count.reshape(experts, blocks, rows).astype(jnp.int32) - 1, -1)
+    def slots_of(routes):
+        chosen = jnp.swapaxes(routes[:, 0], 0, 1).reshape(blocks, top, rows).astype(jnp.int32)
+        levels = jnp.swapaxes(routes[:, 1], 0, 1).reshape(blocks, top, rows).astype(f32)
+        share = levels / jnp.sum(levels, axis=1, keepdims=True)
+        owned = here * experts + jnp.arange(experts, dtype=jnp.int32)
+        hit = chosen[None] == owned[:, None, None, None]
+        named = jnp.any(hit, axis=2)
+        coef = jnp.sum(jnp.where(hit, share[None], 0.0), axis=2)
+        at = jnp.arange(rows, dtype=jnp.int32)
+        upto = (at[:, None] <= at[None, :]).astype(bf16)
+        count = jnp.dot(
+            named.astype(bf16).reshape(experts * blocks, rows), upto, preferred_element_type=f32
+        )
+        count = count.reshape(experts, blocks, rows).astype(jnp.int32)
+        return jnp.where(named, count - 1, -1), coef
 
     cosines, sines = tables(jnp.arange(n * rows, dtype=jnp.int32))
     cosines = cosines.reshape(n, rows, HEAD_DIM)
@@ -858,7 +834,13 @@
         nr[g] = Ring(n2)
         return (n2,)
 
-    stage = xr[0].hop(routes)
+    stage = (xr[0].hop(()), mine)
+    rank, coef = slots_of(after(routes, stage))
+    stage = xr[0].hop(stage)
+    gate_up = lax.all_gather(
+        jnp.concatenate([after(w_gate, stage), w_up], axis=0), "batch", axis=1, tiled=True
+    )
+    down = lax.all_gather(after(w_down, stage), "batch", axis=2, tiled=True)
     stage = finish(xr[0], stage)
     first = None
     for g in range(seqs):
@@ -895,8 +877,41 @@
     for one in nr:
         stage = finish(one, stage)
 
+    grad_hiddens, datts, dos = [None] * seqs, [None] * seqs, [None] * seqs
+    lows, dn = [None] * seqs, [None] * seqs
+    qk_part = jnp.zeros((2, cols), f32)
+
+    def out_backed(g, prev):
+        grad_hiddens[g], datts[g], do, one = out_back(
+            after(zr[g].moved, prev), dx_parts[g][0], grad_low[g], hiddens[g], gain_ffn[None, :],
+            att_w, n,
+        )
+        return do, one
+
+    def attention_backed(g, prev):
+        q, k, v, lse, qkv, inverse, _ = kept[g]
+        *grads, stats, qk_one = attention_backward(
+            place, span_len[g : g + 1], after(q, prev), k, v, dos[g].reshape(n, 1, rows, cols),
+            lse, qkv, inverse, qk_gains, cosines, sines,
+        )
+        stats = jnp.sum(stats.reshape(2, cols // HEAD_DIM, n, rows), axis=1)
+        return grads, jnp.swapaxes(stats, 0, 1), qk_one.reshape(2, cols)
+
+    def summed_stats(stats, prev):
+        return jnp.swapaxes(ctx_sum(after(stats, prev)), 0, 1) / width
+
+    def back_projected(g, grads, stats, prev):
+        qkv, inverse = kept[g][4:6]
+        *dn1, lows[g] = back_project(
+            *(one.reshape(n * rows, cols) for one in grads), qkv.reshape(n * rows, 3 * cols),
+            inverse.reshape(2, n * rows, 1), after(stats, prev).reshape(2, n * rows, 1), qk_gains,
+            att_w, n, n,
+        )
+        dn[g] = Sum(dn1)
+        return (lows[g],)
+
     dr = [Ring(grad_low[g]) for g in range(seqs)]
-    n_pieces = [nr[g].held[j] for j in range(n) for g in range(seqs)]
+    n_pieces = [nr[g].held[j] for g in range(seqs) for j in range(n)]
     held = None
     for start, stop in ((0, experts // 2), (experts // 2, experts)):
         moving = [one.hop(stage) for one in dr]
@@ -909,8 +924,8 @@
     y_parts = expert_output(after(active, stage), rank, coef, down, cap)
     stage = (y_parts, moving)
     stage = [finish(one, stage) for one in dr] or stage
-    grad_pieces = [dr[g].held[j] for j in range(n) for g in range(seqs)]
-    yr = [Sum([y_parts[j * seqs + g] for j in range(n)]) for g in range(seqs)]
+    grad_pieces = [dr[g].held[j] for g in range(seqs) for j in range(n)]
+    yr = [Sum(y_parts[g * n : (g + 1) * n]) for g in range(seqs)]
     moving = [one.hop(stage) for one in yr]
     dgate, dupper, grad_down = expert_backward(
         grad_pieces, after(rank, stage), coef, down, gate, upper, active, cap
@@ -919,70 +934,51 @@
     grad_down = lax.psum_scatter(
         after(grad_down, stage), "batch", scatter_dimension=2, tiled=True
     )
+    rank_rows = rank.reshape(experts * seqs, n, rows)
+
+    def input_grad(g, prev):
+        dx_parts.append(
+            expert_input_grad(after(dgate, prev), dupper, rank_rows, gate_up, cap, g, seqs)
+        )
+        zr.append(Sum(dx_parts[g]))
+        return dx_parts[g]
+
+    zr, dx_parts = [], []
     moving = [one.hop(stage) for one in yr]
-    dx_parts = expert_input_grad(after(dgate, stage), dupper, rank, gate_up, cap)
-    stage = (dx_parts, moving)
-    zr = [Sum([dx_parts[j * seqs + g] for j in range(n)]) for g in range(seqs)]
+    stage = (input_grad(0, stage), moving)
     held = None
-    for i in range(3):
+    for start, stop in ((0, experts // 2), (experts // 2, experts)):
         moving = zr[0].hop(stage)
-        held = expert_weight_grad(
-            slots_x, after(dgate, stage), dupper, experts * i // 3, experts * (i + 1) // 3, held
-        )
+        held = expert_weight_grad(slots_x, after(dgate, stage), dupper, start, stop, held)
         stage = (held, moving)
     gu_local = held[0].reshape(2 * experts, width, -1)
     grad_gu = lax.psum_scatter(
-        after(gu_local, stage, grad_down), "batch", scatter_dimension=1, tiled=True
-    )
-    stage = finish(zr[0], stage)
-
-    grad_hiddens, datts, dos = [None] * seqs, [None] * seqs, [None] * seqs
-    lows, dn = [None] * seqs, [None] * seqs
-    ffn_part = jnp.zeros((1, width), f32)
-    qk_part = jnp.zeros((2, cols), f32)
-
-    def out_backed(g, prev):
-        grad_hiddens[g], datts[g], do, one = out_back(
-            after(zr[g].moved, prev), dx_parts[g], grad_low[g], hiddens[g], gain_ffn[None, :],
-            att_w, n,
-        )
-        return do, one
-
-    def attention_backed(g, prev):
-        q, k, v, lse, qkv, inverse, _ = kept[g]
-        *grads, stats, qk_one = attention_backward(
-            place, span_len[g : g + 1], after(q, prev), k, v, dos[g].reshape(n, 1, rows, cols),
-            lse, qkv, inverse, qk_gains, cosines, sines,
-        )
-        stats = jnp.sum(stats.reshape(2, cols // HEAD_DIM, n, rows), axis=1)
-        return grads, jnp.swapaxes(stats, 0, 1), qk_one.reshape(2, cols)
-
-    def summed_stats(stats, prev):
-        return jnp.swapaxes(ctx_sum(after(stats, prev)), 0, 1) / width
-
-    def back_projected(g, grads, stats, prev):
-        qkv, inverse = kept[g][4:6]
-        *dn1, lows[g] = back_project(
-            *(one.reshape(n * rows, cols) for one in grads), qkv.reshape(n * rows, 3 * cols),
-            inverse.reshape(2, n * rows, 1), after(stats, prev).reshape(2, n * rows, 1), qk_gains,
-            att_w, n, n,
-        )
-        dn[g] = Sum(dn1)
-        return (lows[g],)
+        after(gu_local, stage), "batch", scatter_dimension=1, tiled=True
+    )
+    for g in range(1, seqs):
+        moving = (zr[0].hop(stage), yr[0].hop(stage))
+        stage = (input_grad(g, stage), moving)
+    stage = (finish(zr[0], stage), grad_down)
+    moving = zr[1].hop(stage) if seqs > 1 else ()
+    do, ffn_part = out_backed(0, stage)
+    stage = (do, moving)
 
     held = None
     for g in range(seqs):
         last = g + 1 == seqs
-        if g == 0:
-            moving = () if last else zr[1].hop(stage)
-            do, one = out_backed(0, stage)
-            ffn_part = ffn_part + one
-            stage = (do, moving)
         moving = () if last else zr[g + 1].hop(stage)
         dos[g] = exchange(after(do, stage))
         if held is not None:
             moving += back_projected(g - 1, *held, stage)
+        if last:
+            column = jnp.pad(ffn_part.T.astype(bf16), ((0, 0), (0, LANES - 1)))
+            grad_out = weight_grads(atts, datts, after(column, stage), "out_weight_grad")
+            moving += (grad_out,)
         stage = (dos[g], moving)
+        if last:
+            grad_out = lax.psum_scatter(
+                after(grad_out, stage), "batch", scatter_dimension=0, tiled=True
+            )
         moving = () if last else zr[g + 1].hop(stage)
         if held is not None:
             moving += dn[g - 1].hop(stage)
@@ -993,31 +989,34 @@
             stage = finish(zr[g + 1], stage)
         stats = summed_stats(stats, stage)
         if not last:
+            moving = yr[-1].hop(stage)
             do, one = out_backed(g + 1, stage)
             ffn_part = ffn_part + one
-            stage = (stats, do)
+            stage = (stats, do, moving)
         else:
             stage = (stats,)
         held = (grads, stats)
     g = seqs - 1
+    stage = (stage, grad_gu)
     moving = dn[g - 1].hop(stage) if g else ()
     stage = (back_projected(g, *held, stage), moving)
     qk_rows = lax.dynamic_update_slice_in_dim(
         jnp.zeros((2, width), f32), qk_part, here * cols, 1
     )
-    columns = jnp.concatenate([qk_rows, ffn_part]).T.astype(bf16)
-    columns = jnp.pad(columns, ((0, 0), (0, LANES - 3)))
+    columns = jnp.pad(qk_rows.T.astype(bf16), ((0, 0), (0, LANES - 2)))
     moving = dn[g - 1].hop(stage) if g else ()
-    att_grads = attention_weight_grads(
-        atts, datts, [one[-1] for one in kept], lows, after(columns, stage)
-    )
-    stage = (att_grads, moving)
-    summed = lax.psum_scatter(after(att_grads, grad_gu), "batch", scatter_dimension=0, tiled=True)
-    while len(left := [one.hop(stage) for one in dn + yr if one.at < n]):
-        stage = left
+    grad_qkv = weight_grads(
+        [one[-1] for one in kept], lows, after(columns, stage), "qkv_weight_grad"
+    )
+    stage = (grad_qkv, moving)
+    grad_qkv = lax.psum_scatter(
+        after(grad_qkv, stage), "batch", scatter_dimension=0, tiled=True
+    )
+    while len(left := [one for one in dn[::-1] + yr if one.at < n][:2]):
+        stage = ([one.hop(stage) for one in left], grad_out)
     outs = [
         jnp.where(
-            live[g], hiddens[g] + (yr[g].moved.astype(f32) + y_parts[g].astype(f32)), 0.0
+            live[g], hiddens[g] + (yr[g].moved.astype(f32) + yr[g].parts[0].astype(f32)), 0.0
         ).astype(bf16)
         for g in range(seqs)
     ]
@@ -1026,15 +1025,15 @@
         grad_n1 = dn[g].moved.astype(f32) + dn[g].parts[0].astype(f32)
         back, _ = norm_back(xs[g].astype(f32), gain_attn, grad_n1)
         token_grads.append(grad_hiddens[g] + back)
-    summed = exchange(summed.reshape(n, own, -1)).astype(f32)
+    summed = exchange(grad_out.reshape(n, own, -1)).astype(f32)
     grad_out = jnp.sum(summed[:, :, :width], axis=0)
+    grad_ffn_gain = jnp.sum(summed[:, :, width], axis=0)
+    summed = exchange(grad_qkv.reshape(n, own, -1)).astype(f32)
     grad_q, grad_k, grad_v = (
-        jnp.swapaxes(summed[:, :, width + i * cols : width + (i + 1) * cols], 0, 1).reshape(
-            own, width
-        )
+        jnp.swapaxes(summed[:, :, i * cols : (i + 1) * cols], 0, 1).reshape(own, width)
         for i in range(3)
     )
-    gain_sums = jnp.sum(summed[:, :, width + 3 * cols :], axis=0)
+    gain_sums = jnp.sum(summed[:, :, 3 * cols :], axis=0)
     grad_attn_gain = (
         jnp.sum(
             w_query.astype(f32) * grad_q
@@ -1055,7 +1054,7 @@
         grad_attn_gain,
         gain_sums[:, 0],
         gain_sums[:, 1],
-        gain_sums[:, 2],
+        grad_ffn_gain,
         grad_gu[:experts].astype(f32),
         grad_gu[experts:].astype(f32),
         grad_down.astype(f32),

time: 1220 us -> 1170 us (0.959)
  waiting for transfers between devices: 454 us -> 390 us
    ppermute x18, waiting for transfers between devices: 193 us -> 79.5 us  [hop(): self.moved = lax.ppermute(part, 'ctx', up)]
    all_to_all x5 -> x6, waiting for transfers between devices: 18.6 us -> 49.2 us  [exchange(): return lax.all_to_all(x, 'ctx', split_axis=0, concat_axis=0, tiled=True)]
    pallas_call x3 -> x2, Pallas kernels: 65.1 us -> 58.2 us  [expert_weight_grad(): pl.pallas_call(kernel, grid=(stop - start, width // tile), in_specs=[pl.B...]
    pallas_call x1 -> x2, Pallas kernels: 66.3 us -> 71.7 us  [expert_input_grad(): pl.pallas_call(kernel, grid=(width // tile, experts), in_specs=[line, lin...]
    pallas_call x1 -> x2, Pallas kernels: 24.8 us -> 27.8 us  [weight_grads(): pl.pallas_call(kernel, grid=(width // tile,), in_specs=[left] * count + [...]
    all_to_all x5 -> x6, starting transfers between devices: 27.6 us -> 26.8 us  [exchange(): return lax.all_to_all(x, 'ctx', split_axis=0, concat_axis=0, tiled=True)]
  transfers between devices with their start and end apart: 62 -> 61, of which waited for: 31 -> 29; matrix products, arithmetic and copies ran while one was open for 6% -> 7% of each run, Pallas kernels for 44% -> 45%
where the time goes in v3:
time: 1170 us; the launch traced here: 1160 us
  Pallas kernels  526 us (45%)
  waiting for transfers between devices  390 us (33%)
  starting transfers between devices  72.4 us (6%)
  other arithmetic  56.9 us (5%)
  blocking collectives  51.9 us (4%)
  local copies, waits for them, and re-layouts  46.9 us (4%)
  between operations  15.6 us (1%)
    ppermute x18, waiting for transfers between devices, hop(): self.held.append(lax.ppermute(after(self.held[-1], prev), 'ctx', up))  238 us
    ppermute x18, waiting for transfers between devices, hop(): self.moved = lax.ppermute(part, 'ctx', up)  79.5 us
    pallas_call x2, Pallas kernels, expert_input_grad(): pl.pallas_call(kernel, grid=(width // tile, experts), in_specs=[line, lin...  71.7 us
    pallas_call x2, Pallas kernels, expert_forward(): pl.pallas_call(kernel, grid=(stop - start, hidden // tile), in_specs=[who...  67.4 us
    pallas_call x1, Pallas kernels, expert_backward(): pl.pallas_call(kernel, grid=(experts, hidden // tile), in_specs=[whole(x)...  64.5 us
    pallas_call x2, Pallas kernels, expert_weight_grad(): pl.pallas_call(kernel, grid=(stop - start, width // tile), in_specs=[pl.B...  58.2 us
    pallas_call x2, Pallas kernels, attention_backward(): pl.pallas_call(kernel, grid_spec=pltpu.PrefetchScalarGridSpec(num_scalar_...  56 us
    all_to_all x1, blocking collectives, exchange(): return lax.all_to_all(x, 'ctx', split_axis=0, concat_axis=0, tiled=True)  51.9 us
  transfers between devices with their start and end apart: 61, of which 29 were waited for; matrix products, arithmetic and copies ran while one was open for 7% of the time, Pallas kernels for 45%

profile of v3, /device:TPU:0, one launch (start us, length us, event | category | flops | bytes accessed | tf_op | source)
XLA Modules:
  0.0 1160.7 jit_solution(6597917652524670889)
XLA Ops:
  15.3 51.9 %all_to_all.35 = bf16[4,64,3840]{2,1,0:T(8,128)(2,1)} all-to-all(bf16[4,64,3840]{2,1,0:T(8,128)(2,1)} %broadcast_dynamic-update-slice_fusion.1), channel_id=1, replica_groups=mesh['batch'=8,'ctx'=4] {'ctx'}, dimensions={0} | all-to-all | bytes 3932160 | tf_op jit(solution)/shard_map/all_to_all | solution.py:756
  68.8 25.4 %collective-permute-done.refs_1_ = bf16[256,2048]{1,0:T(8,128)(2,1)S(1)} collective-permute-done((bf16[256,2048]{1,0:T(8,128)(2,1)S(1)}, bf16[256,2048]{1,0:T(8,128)(2,1)S(1)}, u32[]{:S(2)}, u32[]{:S(2)}) %collective-permute-start) | collective-permute-done | bytes 1048608 | tf_op jit(solution)/shard_map/ppermute | solution.py:722
  95.1 24.6 %collective-permute-done.1.refs_2_ = bf16[256,2048]{1,0:T(8,128)(2,1)S(1)} collective-permute-done((bf16[256,2048]{1,0:T(8,128)(2,1)S(1)}, bf16[256,2048]{1,0:T(8,128)(2,1)S(1)}, u32[]{:S(2)}, u32[]{:S(2)}) %collective-permute-start.1) | collective-permute-done | bytes 1048608 | tf_op jit(solution)/shard_map/ppermute | solution.py:722
  123.0 23.7 %collective-permute-done.2.refs_3_ = bf16[256,2048]{1,0:T(8,128)(2,1)S(1)} collective-permute-done((bf16[256,2048]{1,0:T(8,128)(2,1)S(1)}, bf16[256,2048]{1,0:T(8,128)(2,1)S(1)}, u32[]{:S(2)}, u32[]{:S(2)}) %collective-permute-start.2) | collective-permute-done | bytes 1048608 | tf_op jit(solution)/shard_map/ppermute | solution.py:722
  146.7 23.1 %collective-permute-done.3.refs_1_ = bf16[256,2048]{1,0:T(8,128)(2,1)} collective-permute-done((bf16[256,2048]{1,0:T(8,128)(2,1)S(1)}, bf16[256,2048]{1,0:T(8,128)(2,1)}, u32[]{:S(2)}, u32[]{:S(2)}) %collective-permute-start.3) | collective-permute-done | bytes 1048608 | tf_op jit(solution)/shard_map/ppermute | solution.py:722
  173.2 17.9 %project.2 = (bf16[1024,2048]{1,0:T(8,128)(2,1)}, f32[1024,1536]{1,0:T(8,128)}, f32[3,1024,1]{2,1,0:T(8,128)}) custom-call(bf16[256,2048]{1,0:T(8,128)(2,1)} %copy-done.5, bf16[256,2048]{1,0:T(8,128)(2,1)} %copy-done.37, bf16[256,2048]{1,0:T(8,128)(2,1)} %copy-done.41, bf16[256,2048]{1,0:T(8,128)(2,1)} %copy-done.46, f32[1,2048]{1,0:T(1,128)} %copy.237.refs_4_, ...), custom_call_target="tpu_custom_call" | custom-call | flops 805306368 | bytes 1835008 | tf_op jit(solution)/shard_map/project/pallas_call | solution.py:91
  209.2 16.4 %attention.2 = (bf16[1,1024,512]{2,1,0:T(8,128)(2,1)}, bf16[1,1024,512]{2,1,0:T(8,128)(2,1)}, bf16[1,1024,512]{2,1,0:T(8,128)(2,1)}, bf16[4,1,256,512]{3,2,1,0:T(8,128)(2,1)}, f32[1,4,1024,1]{3,2,1,0:T(8,128)}) custom-call(s32[1]{0:T(128)} %bitcast.1.place_ref, s32[1]{0:T(128)} %bitcast.2.len_ref, f32[4,1,256,1536]{3,2,1,0:T(8,128)} %bitcast.166, ...), custom_call_target="tpu_custom_call" | custom-call | flops 201326592 | bytes 1310720 | tf_op jit(solution)/shard_map/attention/pallas_call | solution.py:158
  231.0 17.9 %project.3 = (bf16[1024,2048]{1,0:T(8,128)(2,1)}, f32[1024,1536]{1,0:T(8,128)}, f32[3,1024,1]{2,1,0:T(8,128)}) custom-call(bf16[256,2048]{1,0:T(8,128)(2,1)} %copy-done.3, bf16[256,2048]{1,0:T(8,128)(2,1)} %collective-permute-done.3.refs_1_, bf16[256,2048]{1,0:T(8,128)(2,1)} %collective-permute-done.4.refs_2_, bf16[256,2048]{1,0:T(8,128)(2,1)} %copy-done.36, ...), custom_call_target="tpu_custom_call" | custom-call | flops 805306368 | bytes 1835008 | tf_op jit(solution)/shard_map/project/pallas_call | solution.py:91
  267.1 16.7 %attention.3 = (bf16[1,1024,512]{2,1,0:T(8,128)(2,1)}, bf16[1,1024,512]{2,1,0:T(8,128)(2,1)}, bf16[1,1024,512]{2,1,0:T(8,128)(2,1)}, bf16[4,1,256,512]{3,2,1,0:T(8,128)(2,1)}, f32[1,4,1024,1]{3,2,1,0:T(8,128)}) custom-call(s32[1]{0:T(128)} %bitcast.1.place_ref, s32[1]{0:T(128)} %bitcast.31.len_ref, f32[4,1,256,1536]{3,2,1,0:T(8,128)} %bitcast.171, ...), custom_call_target="tpu_custom_call" | custom-call | flops 201326592 | bytes 1310720 | tf_op jit(solution)/shard_map/attention/pallas_call | solution.py:158
  289.9 33.9 %collective-permute-done.13.refs_2_ = bf16[256,2048]{1,0:T(8,128)(2,1)S(1)} collective-permute-done((bf16[256,2048]{1,0:T(8,128)(2,1)S(1)}, bf16[256,2048]{1,0:T(8,128)(2,1)S(1)}, u32[]{:S(2)}, u32[]{:S(2)}) %collective-permute-start.13) | collective-permute-done | bytes 1048608 | tf_op jit(solution)/shard_map/ppermute | solution.py:722
  338.6 14.2 %collective-permute-done.14.refs_3_ = bf16[256,2048]{1,0:T(8,128)(2,1)S(1)} collective-permute-done((bf16[256,2048]{1,0:T(8,128)(2,1)S(1)}, bf16[256,2048]{1,0:T(8,128)(2,1)S(1)}, u32[]{:S(2)}, u32[]{:S(2)}) %collective-permute-start.14) | collective-permute-done | bytes 1048608 | tf_op jit(solution)/shard_map/ppermute | solution.py:722
  353.8 23.5 %collective-permute-done.15.refs_5_ = bf16[256,2048]{1,0:T(8,128)(2,1)S(1)} collective-permute-done((bf16[256,2048]{1,0:T(8,128)(2,1)}, bf16[256,2048]{1,0:T(8,128)(2,1)S(1)}, u32[]{:S(2)}, u32[]{:S(2)}) %collective-permute-start.15) | collective-permute-done | bytes 1048608 | tf_op jit(solution)/shard_map/ppermute | solution.py:722
  377.5 23.0 %collective-permute-done.16.refs_6_ = bf16[256,2048]{1,0:T(8,128)(2,1)} collective-permute-done((bf16[256,2048]{1,0:T(8,128)(2,1)S(1)}, bf16[256,2048]{1,0:T(8,128)(2,1)}, u32[]{:S(2)}, u32[]{:S(2)}) %collective-permute-start.16) | collective-permute-done | bytes 1048608 | tf_op jit(solution)/shard_map/ppermute | solution.py:722
  404.1 19.9 %collective-permute-done.17.refs_7_ = bf16[256,2048]{1,0:T(8,128)(2,1)} collective-permute-done((bf16[256,2048]{1,0:T(8,128)(2,1)}, bf16[256,2048]{1,0:T(8,128)(2,1)}, u32[]{:S(2)}, u32[]{:S(2)}) %collective-permute-start.17) | collective-permute-done | bytes 1048608 | tf_op jit(solution)/shard_map/ppermute | solution.py:722
  425.0 33.7 %expert_forward.2 = (bf16[4,1280,2048]{2,1,0:T(8,128)(2,1)}, bf16[4,1280,1024]{2,1,0:T(8,128)(2,1)}, bf16[4,1280,1024]{2,1,0:T(8,128)(2,1)}, bf16[4,1280,1024]{2,1,0:T(8,128)(2,1)}) custom-call(bf16[256,2048]{1,0:T(8,128)(2,1)} %get-tuple-element.190.refs_0_, bf16[256,2048]{1,0:T(8,128)(2,1)} %copy-done.10, bf16[256,2048]{1,0:T(8,128)(2,1)} %copy-done.11, ...), custom_call_target="tpu_custom_call" | custom-call | flops 2684354560 | bytes 1048576 | tf_op jit(solution)/shard_map/expert_forward/pallas_call | solution.py:487
  470.0 33.7 %expert_forward.3 = (bf16[4,1280,2048]{2,1,0:T(8,128)(2,1)}, bf16[4,1280,1024]{2,1,0:T(8,128)(2,1)}, bf16[4,1280,1024]{2,1,0:T(8,128)(2,1)}, bf16[4,1280,1024]{2,1,0:T(8,128)(2,1)}) custom-call(bf16[256,2048]{1,0:T(8,128)(2,1)} %get-tuple-element.190.refs_0_, ...), custom_call_target="tpu_custom_call", output_to_operand_aliasing={{0}: (11, {}), {1}: (12, {}), {2}: (13, {}), {3}: (14, {})} | custom-call | flops 2684354560 | bytes 1048576 | tf_op jit(solution)/shard_map/expert_forward/pallas_call | solution.py:487
  516.6 41.2 %expert_output.1 = (bf16[256,2048]{1,0:T(8,128)(2,1)}, bf16[256,2048]{1,0:T(8,128)(2,1)}, bf16[256,2048]{1,0:T(8,128)(2,1)}, bf16[256,2048]{1,0:T(8,128)(2,1)}, ...) custom-call(bf16[4,1280,1024]{2,1,0:T(8,128)(2,1)} %get-tuple-elemen, ...), custom_call_target="tpu_custom_call" | custom-call | flops 2684354560 | bytes 4456448 | tf_op jit(solution)/shard_map/expert_output/pallas_call | solution.py:538
  562.7 64.5 %expert_backward.1 = (bf16[4,1280,1024]{2,1,0:T(8,128)(2,1)}, bf16[4,1280,1024]{2,1,0:T(8,128)(2,1)}, bf16[4,1024,2048]{2,1,0:T(8,128)(2,1)}) custom-call(bf16[256,2048]{1,0:T(8,128)(2,1)} %copy-done.4, bf16[256,2048]{1,0:T(8,128)(2,1)} %copy-done.29, bf16[256,2048]{1,0:T(8,128)(2,1)} %copy-done.33, bf16[256,2048]{1,0:T(8,128)(2,1)} %collective-permute-done.22.refs_3_, ...), custom_call_target="tpu_custom_call" | custom-call | flops 5368709120 | bytes 11796480 | tf_op jit(solution)/shard_map/expert_backward/pallas_call | solution.py:590
  638.2 35.9 %expert_input_grad.2 = (bf16[256,2048]{1,0:T(8,128)(2,1)}, bf16[256,2048]{1,0:T(8,128)(2,1)}, bf16[256,2048]{1,0:T(8,128)(2,1)}, bf16[256,2048]{1,0:T(8,128)(2,1)}) custom-call(bf16[4,1280,1024]{2,1,0:T(8,128)(2,1)} %get-tuple-element.255.dg_i, bf16[4,1280,1024]{2,1,0:T(8,128)(2,1)} %get-tuple-element.237.du_i, s32[8,4,256]{2,1,0:T(4,128)} %reshape.395.rank_ref, ...), custom_call_target="tpu_custom_call" | custom-call | flops 2684354560 | bytes 4718592 | tf_op jit(solution)/shard_map/expert_input_grad/pallas_call | solution.py:632
  674.2 29.0 %expert_weight_grad.2.rest_0_ = bf16[2,4,2048,1024]{3,2,1,0:T(8,128)(2,1)} custom-call(bf16[4,1280,2048]{2,1,0:T(8,128)(2,1)} %get-tuple-element.213.x_i, bf16[4,1280,1024]{2,1,0:T(8,128)(2,1)} %get-tuple-element.255.dg_i, bf16[4,1280,1024]{2,1,0:T(8,128)(2,1)} %get-tuple-element.237.du_i), custom_call_target="tpu_custom_call" | custom-call | flops 2684354560 | bytes 2621440 | tf_op jit(solution)/shard_map/expert_weight_grad/pallas_call | solution.py:663
  704.8 29.2 %expert_weight_grad.3 = bf16[2,4,2048,1024]{3,2,1,0:T(8,128)(2,1)} custom-call(bf16[4,1280,2048]{2,1,0:T(8,128)(2,1)} %get-tuple-element.213.x_i, bf16[4,1280,1024]{2,1,0:T(8,128)(2,1)} %get-tuple-element.255.dg_i, bf16[4,1280,1024]{2,1,0:T(8,128)(2,1)} %get-tuple-element.237.du_i, ...), custom_call_target="tpu_custom_call", output_to_operand_aliasing={{}: (3, {})} | custom-call | flops 2684354560 | bytes 2621440 | tf_op jit(solution)/shard_map/expert_weight_grad/pallas_call | solution.py:663
  740.8 35.8 %expert_input_grad.3 = (bf16[256,2048]{1,0:T(8,128)(2,1)}, bf16[256,2048]{1,0:T(8,128)(2,1)}, bf16[256,2048]{1,0:T(8,128)(2,1)}, bf16[256,2048]{1,0:T(8,128)(2,1)}) custom-call(bf16[4,1280,1024]{2,1,0:T(8,128)(2,1)} %get-tuple-element.255.dg_i, bf16[4,1280,1024]{2,1,0:T(8,128)(2,1)} %get-tuple-element.237.du_i, s32[8,4,256]{2,1,0:T(4,128)} %reshape.395.rank_ref, ...), custom_call_target="tpu_custom_call" | custom-call | flops 2684354560 | bytes 4718592 | tf_op jit(solution)/shard_map/expert_input_grad/pallas_call | solution.py:632
  809.1 24.1 %collective-permute-done.33 = bf16[256,2048]{1,0:T(8,128)(2,1)} collective-permute-done((bf16[256,2048]{1,0:T(8,128)(2,1)S(1)}, bf16[256,2048]{1,0:T(8,128)(2,1)}, u32[]{:S(2)}, u32[]{:S(2)}) %collective-permute-start.33) | collective-permute-done | bytes 1048608 | tf_op jit(solution)/shard_map/ppermute | solution.py:737
  843.1 28.0 %attention_back.2 = (f32[4,1,256,512]{3,2,1,0:T(8,128)}, f32[4,1,256,512]{3,2,1,0:T(8,128)}, bf16[4,1,256,512]{3,2,1,0:T(8,128)(2,1)}, f32[2,1,4,4,256,1]{5,4,3,2,1,0:T(8,128)}, f32[2,1,1,512]{3,2,1,0:T(1,128)}) custom-call(s32[1]{0:T(128)} %bitcast.1.place_ref, s32[1]{0:T(128)} %bitcast.2.len_ref, bf16[1,1024,512]{2,1,0:T(8,128)(2,1)} %get-tuple-element.268.q_i, ...), custom_call_target="tpu_custom_call" | custom-call | flops 469762048 | bytes 1441792 | tf_op jit(solution)/shard_map/attention_back/pallas_call | solution.py:242
  917.3 15.5 %back_project.2 = (bf16[256,2048]{1,0:T(8,128)(2,1)}, bf16[256,2048]{1,0:T(8,128)(2,1)}, bf16[256,2048]{1,0:T(8,128)(2,1)}, bf16[256,2048]{1,0:T(8,128)(2,1)}, bf16[1024,1536]{1,0:T(8,128)(2,1)}) custom-call(f32[1024,512]{1,0:T(8,128)} %bitcast.180, f32[1024,512]{1,0:T(8,128)} %bitcast.181, bf16[1024,512]{1,0:T(8,128)(2,1)} %bitcast.192, ...), custom_call_target="tpu_custom_call" | custom-call | flops 805306368 | bytes 1572864 | tf_op jit(solution)/shard_map/back_project/pallas_call | solution.py:309
  937.2 28.0 %attention_back.3 = (f32[4,1,256,512]{3,2,1,0:T(8,128)}, f32[4,1,256,512]{3,2,1,0:T(8,128)}, bf16[4,1,256,512]{3,2,1,0:T(8,128)(2,1)}, f32[2,1,4,4,256,1]{5,4,3,2,1,0:T(8,128)}, f32[2,1,1,512]{3,2,1,0:T(1,128)}) custom-call(s32[1]{0:T(128)} %bitcast.1.place_ref, s32[1]{0:T(128)} %bitcast.31.len_ref, bf16[1,1024,512]{2,1,0:T(8,128)(2,1)} %get-tuple-element.295.q_i, ...), custom_call_target="tpu_custom_call" | custom-call | flops 469762048 | bytes 1441792 | tf_op jit(solution)/shard_map/attention_back/pallas_call | solution.py:242
  981.3 15.5 %back_project.3 = (bf16[256,2048]{1,0:T(8,128)(2,1)}, bf16[256,2048]{1,0:T(8,128)(2,1)}, bf16[256,2048]{1,0:T(8,128)(2,1)}, bf16[256,2048]{1,0:T(8,128)(2,1)}, bf16[1024,1536]{1,0:T(8,128)(2,1)}) custom-call(f32[1024,512]{1,0:T(8,128)} %bitcast.182, f32[1024,512]{1,0:T(8,128)} %bitcast.183, bf16[1024,512]{1,0:T(8,128)(2,1)} %bitcast.193, ...), custom_call_target="tpu_custom_call" | custom-call | flops 805306368 | bytes 1572864 | tf_op jit(solution)/shard_map/back_project/pallas_call | solution.py:309
  1001.5 19.0 %qkv_weight_grad.1 = bf16[2048,1664]{1,0:T(8,128)(2,1)} custom-call(bf16[1024,2048]{1,0:T(8,128)(2,1)} %get-tuple-element.316.refs_0_, bf16[1024,2048]{1,0:T(8,128)(2,1)} %get-tuple-element.317.refs_1_, bf16[1024,1536]{1,0:T(8,128)(2,1)} %get-tuple-element.287.refs_2_, bf16[1024,1536]{1,0:T(8,128)(2,1)} %get-tuple-element.309.refs_3_, ...), custom_call_target="tpu_custom_call" | custom-call | flops 1610612736 | bytes 2686976 | tf_op jit(solution)/shard_map/qkv_weight_grad/pallas_call | solution.py:425
  1035.0 15.2 %collective-permute-done.45 = bf16[256,2048]{1,0:T(8,128)(2,1)S(1)} collective-permute-done((bf16[256,2048]{1,0:T(8,128)(2,1)}, bf16[256,2048]{1,0:T(8,128)(2,1)S(1)}, u32[]{:S(2)}, u32[]{:S(2)}) %collective-permute-start.45) | collective-permute-done | bytes 1048608 | tf_op jit(solution)/shard_map/ppermute | solution.py:737
  1056.8 28.3 %collective-permute-done.46 = bf16[256,2048]{1,0:T(8,128)(2,1)S(1)} collective-permute-done((bf16[256,2048]{1,0:T(8,128)(2,1)S(1)}, bf16[256,2048]{1,0:T(8,128)(2,1)S(1)}, u32[]{:S(2)}, u32[]{:S(2)}) %collective-permute-start.46) | collective-permute-done | bytes 1048608 | tf_op jit(solution)/shard_map/ppermute | solution.py:737
  1090.9 22.6 %all-to-all-done.6 = bf16[4,64,2176]{2,1,0:T(8,128)(2,1)S(1)} async-done(((bf16[4,64,2176]{2,1,0:T(8,128)(2,1)}), bf16[4,64,2176]{2,1,0:T(8,128)(2,1)S(1)}, u32[]{:S(2)}, u32[]{:S(2)}) %all-to-all-start.6) | async-done | bytes 1114144 | tf_op jit(solution)/shard_map/all_to_all | solution.py:756
  1133.5 15.8 %all-to-all-done.5 = bf16[4,64,1664]{2,1,0:T(8,128)(2,1)} async-done(((bf16[4,64,1664]{2,1,0:T(8,128)(2,1)}), bf16[4,64,1664]{2,1,0:T(8,128)(2,1)}, u32[]{:S(2)}, u32[]{:S(2)}) %all-to-all-start.5) | async-done | bytes 852000 | tf_op jit(solution)/shard_map/all_to_all | solution.py:756
  (395 shorter events, 298.1 us)
Async XLA Ops:
  7.2 162.6 %all-gather.4.cloned.1.call-start = ((), (), s32[]{:S(2)}) async-start(), calls=%async_computation.11 | async-start | bytes 17694720 | tf_op jit(solution)/shard_map/all_gather | solution.py:779
  67.3 357.7 %all-gather.6.cloned.1.call-start = ((), (), s32[]{:S(2)}) async-start(), calls=%async_computation.12 | async-start | bytes 37748736 | tf_op jit(solution)/shard_map/all_gather | solution.py:840
  122.2 394.4 %all-gather.8.cloned.1.call-start = ((), (), s32[]{:S(2)}) async-start(), calls=%async_computation.13 | async-start | bytes 18874368 | tf_op jit(solution)/shard_map/all_gather | solution.py:843
  284.4 44.8 %all-to-all-start.2 = ((bf16[4,256,512]{2,1,0:T(8,128)(2,1)}), bf16[4,256,512]{2,1,0:T(8,128)(2,1)S(1)}, u32[]{:S(2)}, u32[]{:S(2)}) async-start(bf16[4,256,512]{2,1,0:T(8,128)(2,1)} %bitcast.198), calls=%async_computation.2 | async-start | bytes 2097152 | tf_op jit(solution)/shard_map/all_to_all | solution.py:756
  287.9 488.8 %reduce-scatter.5.cloned.1.call-start = ((), (), s32[]{:S(2)}) async-start(), calls=%async_computation.14 | async-start | bytes 18874368 | tf_op jit(solution)/shard_map/reduce_scatter | solution.py:934
  287.9 35.8 %collective-permute-start.13 = (bf16[256,2048]{1,0:T(8,128)(2,1)S(1)}, bf16[256,2048]{1,0:T(8,128)(2,1)S(1)}, u32[]{:S(2)}, u32[]{:S(2)}) collective-permute-start(bf16[256,2048]{1,0:T(8,128)(2,1)S(1)} %collective-permute-done.12.refs_1_), channel_id=1, source_target_pairs={{0,1},{1,2},{2,3},{3,0},{4,5},{5,6},{6,7},{7,4},{8,9},{9,10},{10,1... | collective-permute-start | bytes 3145736 | tf_op jit(solution)/shard_map/ppermute | solution.py:722
  424.0 34.7 %collective-permute-start.18 = (bf16[256,2048]{1,0:T(8,128)(2,1)S(1)}, bf16[256,2048]{1,0:T(8,128)(2,1)S(1)}, u32[]{:S(2)}, u32[]{:S(2)}) collective-permute-start(bf16[256,2048]{1,0:T(8,128)(2,1)S(1)} %get-tuple-element.209.refs_0_.l_i), channel_id=1, source_target_pairs={{0,1},{1,2},{2,3},{3,0},{4,5},{5,6},{6,7},{7,4},{8,9},{9,10},{10,1... | collective-permute-start | bytes 3145736 | tf_op jit(solution)/shard_map/ppermute | solution.py:722
  424.0 45.8 %collective-permute-start.19 = (bf16[256,2048]{1,0:T(8,128)(2,1)S(1)}, bf16[256,2048]{1,0:T(8,128)(2,1)}, u32[]{:S(2)}, u32[]{:S(2)}) collective-permute-start(bf16[256,2048]{1,0:T(8,128)(2,1)S(1)} %get-tuple-element.210.refs_4_.l_i), channel_id=1, source_target_pairs={{0,1},{1,2},{2,3},{3,0},{4,5},{5,6},{6,7},{7,4},{8,9},{9,10},{10,1... | collective-permute-start | bytes 3145736 | tf_op jit(solution)/shard_map/ppermute | solution.py:722
  469.8 33.9 %collective-permute-start.20 = (bf16[256,2048]{1,0:T(8,128)(2,1)S(1)}, bf16[256,2048]{1,0:T(8,128)(2,1)S(1)}, u32[]{:S(2)}, u32[]{:S(2)}) collective-permute-start(bf16[256,2048]{1,0:T(8,128)(2,1)S(1)} %collective-permute-done.18.refs_1_), channel_id=1, source_target_pairs={{0,1},{1,2},{2,3},{3,0},{4,5},{5,6},{6,7},{7,4},{8,9},{9,10},{10,1... | collective-permute-start | bytes 3145736 | tf_op jit(solution)/shard_map/ppermute | solution.py:722
  469.8 45.8 %collective-permute-start.21 = (bf16[256,2048]{1,0:T(8,128)(2,1)}, bf16[256,2048]{1,0:T(8,128)(2,1)S(1)}, u32[]{:S(2)}, u32[]{:S(2)}) collective-permute-start(bf16[256,2048]{1,0:T(8,128)(2,1)} %collective-permute-done.19.refs_5_), channel_id=1, source_target_pairs={{0,1},{1,2},{2,3},{3,0},{4,5},{5,6},{6,7},{7,4},{8,9},{9,10},{10,1... | collective-permute-start | bytes 3145736 | tf_op jit(solution)/shard_map/ppermute | solution.py:722
  515.6 42.1 %collective-permute-start.23 = (bf16[256,2048]{1,0:T(8,128)(2,1)S(1)}, bf16[256,2048]{1,0:T(8,128)(2,1)S(1)}, u32[]{:S(2)}, u32[]{:S(2)}) collective-permute-start(bf16[256,2048]{1,0:T(8,128)(2,1)S(1)} %collective-permute-done.21.refs_6_), channel_id=1, source_target_pairs={{0,1},{1,2},{2,3},{3,0},{4,5},{5,6},{6,7},{7,4},{8,9},{9,10},{10,1... | collective-permute-start | bytes 3145736 | tf_op jit(solution)/shard_map/ppermute | solution.py:722
  515.6 45.6 %collective-permute-start.22 = (bf16[256,2048]{1,0:T(8,128)(2,1)S(1)}, bf16[256,2048]{1,0:T(8,128)(2,1)}, u32[]{:S(2)}, u32[]{:S(2)}) collective-permute-start(bf16[256,2048]{1,0:T(8,128)(2,1)S(1)} %collective-permute-done.20.refs_2_), channel_id=1, source_target_pairs={{0,1},{1,2},{2,3},{3,0},{4,5},{5,6},{6,7},{7,4},{8,9},{9,10},{10,1... | collective-permute-start | bytes 3145736 | tf_op jit(solution)/shard_map/ppermute | solution.py:722
  561.2 66.0 %collective-permute-start.25 = (bf16[256,2048]{1,0:T(8,128)(2,1)}, bf16[256,2048]{1,0:T(8,128)(2,1)}, u32[]{:S(2)}, u32[]{:S(2)}) collective-permute-start(bf16[256,2048]{1,0:T(8,128)(2,1)} %get-tuple-element.233), channel_id=1, source_target_pairs={{0,1},{1,2},{2,3},{3,0},{4,5},{5,6},{6,7},{7,4},{8,9},{9,10},{10,1... | collective-permute-start | bytes 3145736 | tf_op jit(solution)/shard_map/ppermute | solution.py:737
  561.2 66.0 %collective-permute-start.24 = (bf16[256,2048]{1,0:T(8,128)(2,1)}, bf16[256,2048]{1,0:T(8,128)(2,1)}, u32[]{:S(2)}, u32[]{:S(2)}) collective-permute-start(bf16[256,2048]{1,0:T(8,128)(2,1)} %get-tuple-element.230), channel_id=1, source_target_pairs={{0,1},{1,2},{2,3},{3,0},{4,5},{5,6},{6,7},{7,4},{8,9},{9,10},{10,1... | collective-permute-start | bytes 3145736 | tf_op jit(solution)/shard_map/ppermute | solution.py:737
  627.2 349.1 %reduce-scatter.7.cloned.1.call-start = ((), (), s32[]{:S(2)}) async-start(), calls=%async_computation.15 | async-start | bytes 37748736 | tf_op jit(solution)/shard_map/reduce_scatter | solution.py:955
  631.0 43.1 %collective-permute-start.27 = (bf16[256,2048]{1,0:T(8,128)(2,1)}, bf16[256,2048]{1,0:T(8,128)(2,1)S(1)}, u32[]{:S(2)}, u32[]{:S(2)}) collective-permute-start(bf16[256,2048]{1,0:T(8,128)(2,1)} %add_convert_fusion.10), channel_id=1, source_target_pairs={{0,1},{1,2},{2,3},{3,0},{4,5},{5,6},{6,7},{7,4},{8,9},{9,10},{10,1... | collective-permute-start | bytes 3145736 | tf_op jit(solution)/shard_map/ppermute | solution.py:737
  634.1 40.0 %collective-permute-start.26 = (bf16[256,2048]{1,0:T(8,128)(2,1)}, bf16[256,2048]{1,0:T(8,128)(2,1)S(1)}, u32[]{:S(2)}, u32[]{:S(2)}) collective-permute-start(bf16[256,2048]{1,0:T(8,128)(2,1)} %add_convert_fusion.11), channel_id=1, source_target_pairs={{0,1},{1,2},{2,3},{3,0},{4,5},{5,6},{6,7},{7,4},{8,9},{9,10},{10,1... | collective-permute-start | bytes 3145736 | tf_op jit(solution)/shard_map/ppermute | solution.py:737
  674.1 29.1 %collective-permute-start.28 = (bf16[256,2048]{1,0:T(8,128)(2,1)}, bf16[256,2048]{1,0:T(8,128)(2,1)S(1)}, u32[]{:S(2)}, u32[]{:S(2)}) collective-permute-start(bf16[256,2048]{1,0:T(8,128)(2,1)} %get-tuple-element.245), channel_id=1, source_target_pairs={{0,1},{1,2},{2,3},{3,0},{4,5},{5,6},{6,7},{7,4},{8,9},{9,10},{10,1... | collective-permute-start | bytes 3145736 | tf_op jit(solution)/shard_map/ppermute | solution.py:737
  703.6 30.4 %collective-permute-start.29 = (bf16[256,2048]{1,0:T(8,128)(2,1)S(1)}, bf16[256,2048]{1,0:T(8,128)(2,1)}, u32[]{:S(2)}, u32[]{:S(2)}) collective-permute-start(bf16[256,2048]{1,0:T(8,128)(2,1)S(1)} %add_convert_fusion.9), channel_id=1, source_target_pairs={{0,1},{1,2},{2,3},{3,0},{4,5},{5,6},{6,7},{7,4},{8,9},{9,10},{10,1... | collective-permute-start | bytes 3145736 | tf_op jit(solution)/shard_map/ppermute | solution.py:737
  735.6 41.0 %collective-permute-start.30 = (bf16[256,2048]{1,0:T(8,128)(2,1)S(1)}, bf16[256,2048]{1,0:T(8,128)(2,1)S(1)}, u32[]{:S(2)}, u32[]{:S(2)}) collective-permute-start(bf16[256,2048]{1,0:T(8,128)(2,1)S(1)} %add_convert_fusion.8), channel_id=1, source_target_pairs={{0,1},{1,2},{2,3},{3,0},{4,5},{5,6},{6,7},{7,4},{8,9},{9,10},{10,1... | collective-permute-start | bytes 3145736 | tf_op jit(solution)/shard_map/ppermute | solution.py:737
  738.7 37.9 %collective-permute-start.31 = (bf16[256,2048]{1,0:T(8,128)(2,1)S(1)}, bf16[256,2048]{1,0:T(8,128)(2,1)S(1)}, u32[]{:S(2)}, u32[]{:S(2)}) collective-permute-start(bf16[256,2048]{1,0:T(8,128)(2,1)S(1)} %add_convert_fusion.7), channel_id=1, source_target_pairs={{0,1},{1,2},{2,3},{3,0},{4,5},{5,6},{6,7},{7,4},{8,9},{9,10},{10,1... | collective-permute-start | bytes 3145736 | tf_op jit(solution)/shard_map/ppermute | solution.py:737
  798.2 40.3 %all-to-all-start.3 = ((bf16[4,256,512]{2,1,0:T(8,128)(2,1)}), bf16[4,256,512]{2,1,0:T(8,128)(2,1)S(1)}, u32[]{:S(2)}, u32[]{:S(2)}) async-start(bf16[4,256,512]{2,1,0:T(8,128)(2,1)} %get-tuple-element.265), calls=%async_computation.4 | async-start | bytes 2097152 | tf_op jit(solution)/shard_map/all_to_all | solution.py:756
  841.5 32.2 %collective-permute-start.34 = (bf16[256,2048]{1,0:T(8,128)(2,1)}, bf16[256,2048]{1,0:T(8,128)(2,1)S(1)}, u32[]{:S(2)}, u32[]{:S(2)}) collective-permute-start(bf16[256,2048]{1,0:T(8,128)(2,1)} %add_convert_fusion.5), channel_id=1, source_target_pairs={{0,1},{1,2},{2,3},{3,0},{4,5},{5,6},{6,7},{7,4},{8,9},{9,10},{10,1... | collective-permute-start | bytes 3145736 | tf_op jit(solution)/shard_map/ppermute | solution.py:737
  899.6 33.3 %all-to-all-start.4 = ((bf16[4,256,512]{2,1,0:T(8,128)(2,1)}), bf16[4,256,512]{2,1,0:T(8,128)(2,1)S(1)}, u32[]{:S(2)}, u32[]{:S(2)}) async-start(bf16[4,256,512]{2,1,0:T(8,128)(2,1)} %get-tuple-element.286), calls=%async_computation.5 | async-start | bytes 2097152 | tf_op jit(solution)/shard_map/all_to_all | solution.py:756
  903.1 127.2 %reduce-scatter.9.cloned.1.call-start = ((), (), s32[]{:S(2)}) async-start(), calls=%async_computation.16 | async-start | bytes 10027008 | tf_op jit(solution)/shard_map/reduce_scatter | solution.py:979
  933.9 189.2 %reduce-scatter.11.cloned.1.call-start = ((), (), s32[]{:S(2)}) async-start(), calls=%async_computation.17 | async-start | bytes 7667712 | tf_op jit(solution)/shard_map/reduce_scatter | solution.py:1012
  933.9 34.9 %collective-permute-start.39 = (bf16[256,2048]{1,0:T(8,128)(2,1)}, bf16[256,2048]{1,0:T(8,128)(2,1)S(1)}, u32[]{:S(2)}, u32[]{:S(2)}) collective-permute-start(bf16[256,2048]{1,0:T(8,128)(2,1)} %get-tuple-element.293), channel_id=1, source_target_pairs={{0,1},{1,2},{2,3},{3,0},{4,5},{5,6},{6,7},{7,4},{8,9},{9,10},{10,1... | collective-permute-start | bytes 3145736 | tf_op jit(solution)/shard_map/ppermute | solution.py:737
  1023.4 26.8 %collective-permute-start.45 = (bf16[256,2048]{1,0:T(8,128)(2,1)}, bf16[256,2048]{1,0:T(8,128)(2,1)S(1)}, u32[]{:S(2)}, u32[]{:S(2)}) collective-permute-start(bf16[256,2048]{1,0:T(8,128)(2,1)} %get-tuple-element.321), channel_id=1, source_target_pairs={{0,1},{1,2},{2,3},{3,0},{4,5},{5,6},{6,7},{7,4},{8,9},{9,10},{10,1... | collective-permute-start | bytes 3145736 | tf_op jit(solution)/shard_map/ppermute | solution.py:737
  1030.4 83.1 %all-to-all-start.6 = ((bf16[4,64,2176]{2,1,0:T(8,128)(2,1)}), bf16[4,64,2176]{2,1,0:T(8,128)(2,1)S(1)}, u32[]{:S(2)}, u32[]{:S(2)}) async-start(bf16[4,64,2176]{2,1,0:T(8,128)(2,1)} %bitcast.191), calls=%async_computation.10 | async-start | bytes 2228224 | tf_op jit(solution)/shard_map/all_to_all | solution.py:756
  1050.6 34.4 %collective-permute-start.46 = (bf16[256,2048]{1,0:T(8,128)(2,1)S(1)}, bf16[256,2048]{1,0:T(8,128)(2,1)S(1)}, u32[]{:S(2)}, u32[]{:S(2)}) collective-permute-start(bf16[256,2048]{1,0:T(8,128)(2,1)S(1)} %add_convert_fusion.1), channel_id=1, source_target_pairs={{0,1},{1,2},{2,3},{3,0},{4,5},{5,6},{6,7},{7,4},{8,9},{9,10},{10,1... | collective-permute-start | bytes 3145736 | tf_op jit(solution)/shard_map/ppermute | solution.py:737
  1086.5 33.9 %collective-permute-start.47 = (bf16[256,2048]{1,0:T(8,128)(2,1)}, bf16[256,2048]{1,0:T(8,128)(2,1)}, u32[]{:S(2)}, u32[]{:S(2)}) collective-permute-start(bf16[256,2048]{1,0:T(8,128)(2,1)} %add_convert_fusion), channel_id=1, source_target_pairs={{0,1},{1,2},{2,3},{3,0},{4,5},{5,6},{6,7},{7,4},{8,9},{9,10},{10,1... | collective-permute-start | bytes 3145736 | tf_op jit(solution)/shard_map/ppermute | solution.py:737
  1123.0 26.3 %all-to-all-start.5 = ((bf16[4,64,1664]{2,1,0:T(8,128)(2,1)}), bf16[4,64,1664]{2,1,0:T(8,128)(2,1)}, u32[]{:S(2)}, u32[]{:S(2)}) async-start(bf16[4,64,1664]{2,1,0:T(8,128)(2,1)} %bitcast.199), calls=%async_computation.9 | async-start | bytes 1703936 | tf_op jit(solution)/shard_map/all_to_all | solution.py:756
  (102 other events, 1601.3 us)
Sparse Core Ops, SparseCore 0:
  67.4 84.5 all-gather.3
  154.6 160.7 all-gather.5
  317.3 93.1 all-gather.7
  627.3 116.5 reduce-scatter.4
  747.4 205.2 reduce-scatter.6
  956.5 73.8 reduce-scatter.8
  1034.2 64.2 reduce-scatter.10

commit v4 on v3

--- a/solution.py
+++ b/solution.py
@@ -478,9 +478,11 @@
         x = x_o[0]
         gate = dot(x, wg[0])
         upper = dot(x, wu[0])
-        g_o[0] = gate.astype(bf16)
-        u_o[0] = upper.astype(bf16)
-        a_o[0] = (gate * jax.nn.sigmoid(gate) * upper).astype(bf16)
+        s = jax.nn.sigmoid(gate)
+        silu = gate * s
+        g_o[0] = (upper * (s + silu * (1.0 - s))).astype(bf16)
+        u_o[0] = silu.astype(bf16)
+        a_o[0] = (silu * upper).astype(bf16)
 
     tiled = pl.BlockSpec((1, slots, tile), lambda e, f: (start + e, 0, f))
     outs = (struct((experts, slots, width), bf16),) + (struct((experts, slots, hidden), bf16),) * 3
@@ -576,10 +578,8 @@
                 ).astype(bf16)
 
         da = dot_nt(dy[...], wd[0])
-        g = g_i[0].astype(f32)
-        s = jax.nn.sigmoid(g)
-        du_o[0] = (da * g * s).astype(bf16)
-        dg_o[0] = (da * u_i[0].astype(f32) * s * (1.0 + g * (1.0 - s))).astype(bf16)
+        du_o[0] = (da * u_i[0].astype(f32)).astype(bf16)
+        dg_o[0] = (da * g_i[0].astype(f32)).astype(bf16)
 
         dw_o[0] = dot_tn(a_i[0], dy[...]).astype(bf16)
 
@@ -919,7 +919,7 @@
             n_pieces, after(rank, stage), gate_up, cap, start, stop, held
         )
         stage = (held, moving)
-    slots_x, gate, upper, active = held
+    slots_x, by_gate, by_upper, active = held
     moving = [one.hop(stage) for one in dr]
     y_parts = expert_output(after(active, stage), rank, coef, down, cap)
     stage = (y_parts, moving)
@@ -928,7 +928,7 @@
     yr = [Sum(y_parts[g * n : (g + 1) * n]) for g in range(seqs)]
     moving = [one.hop(stage) for one in yr]
     dgate, dupper, grad_down = expert_backward(
-        grad_pieces, after(rank, stage), coef, down, gate, upper, active, cap
+        grad_pieces, after(rank, stage), coef, down, by_gate, by_upper, active, cap
     )
     stage = (dgate, moving)
     grad_down = lax.psum_scatter(
@@ -1025,10 +1025,12 @@
         grad_n1 = dn[g].moved.astype(f32) + dn[g].parts[0].astype(f32)
         back, _ = norm_back(xs[g].astype(f32), gain_attn, grad_n1)
         token_grads.append(grad_hiddens[g] + back)
-    summed = exchange(grad_out.reshape(n, own, -1)).astype(f32)
-    grad_out = jnp.sum(summed[:, :, :width], axis=0)
-    grad_ffn_gain = jnp.sum(summed[:, :, width], axis=0)
-    summed = exchange(grad_qkv.reshape(n, own, -1)).astype(f32)
+    grad_out, summed = lax.optimization_barrier(
+        (exchange(grad_out.reshape(n, own, -1)), exchange(grad_qkv.reshape(n, own, -1)))
+    )
+    grad_out, summed = grad_out.astype(f32), summed.astype(f32)
+    grad_ffn_gain = jnp.sum(grad_out[:, :, width], axis=0)
+    grad_out = jnp.sum(grad_out[:, :, :width], axis=0)
     grad_q, grad_k, grad_v = (
         jnp.swapaxes(summed[:, :, i * cols : (i + 1) * cols], 0, 1).reshape(own, width)
         for i in range(3)

time: 1170 us -> 1160 us (level)
  transfers between devices with their start and end apart: 61 -> 61, of which waited for: 29 -> 30; matrix products, arithmetic and copies ran while one was open for 7% -> 7% of each run, Pallas kernels for 45% -> 46%
where the time goes in v4:
time: 1160 us; the launch traced here: 1150 us
  Pallas kernels  525 us (45%)
  waiting for transfers between devices  383 us (33%)
  starting transfers between devices  67.1 us (6%)
  other arithmetic  60.6 us (5%)
  blocking collectives  51.9 us (4%)
  local copies, waits for them, and re-layouts  45.4 us (4%)
  between operations  15.6 us (1%)
    ppermute x18, waiting for transfers between devices, hop(): self.held.append(lax.ppermute(after(self.held[-1], prev), 'ctx', up))  236 us
    ppermute x18, waiting for transfers between devices, hop(): self.moved = lax.ppermute(part, 'ctx', up)  85.5 us
    pallas_call x2, Pallas kernels, expert_input_grad(): pl.pallas_call(kernel, grid=(width // tile, experts), in_specs=[line, lin...  71.7 us
    pallas_call x2, Pallas kernels, expert_forward(): pl.pallas_call(kernel, grid=(stop - start, hidden // tile), in_specs=[who...  69.9 us
    pallas_call x1, Pallas kernels, expert_backward(): pl.pallas_call(kernel, grid=(experts, hidden // tile), in_specs=[whole(x)...  60.5 us
    pallas_call x2, Pallas kernels, expert_weight_grad(): pl.pallas_call(kernel, grid=(stop - start, width // tile), in_specs=[pl.B...  58.2 us
    pallas_call x2, Pallas kernels, attention_backward(): pl.pallas_call(kernel, grid_spec=pltpu.PrefetchScalarGridSpec(num_scalar_...  56 us
    all_to_all x1, blocking collectives, exchange(): return lax.all_to_all(x, 'ctx', split_axis=0, concat_axis=0, tiled=True)  51.9 us
  transfers between devices with their start and end apart: 61, of which 30 were waited for; matrix products, arithmetic and copies ran while one was open for 7% of the time, Pallas kernels for 46%

profile of v4, /device:TPU:0, one launch (start us, length us, event | category | flops | bytes accessed | tf_op | source)
XLA Modules:
  0.0 1148.8 jit_solution(6524174850314885806)
XLA Ops:
  15.3 51.9 %all_to_all.35 = bf16[4,64,3840]{2,1,0:T(8,128)(2,1)} all-to-all(bf16[4,64,3840]{2,1,0:T(8,128)(2,1)} %broadcast_dynamic-update-slice_fusion.1), channel_id=1, replica_groups=mesh['batch'=8,'ctx'=4] {'ctx'}, dimensions={0} | all-to-all | bytes 3932160 | tf_op jit(solution)/shard_map/all_to_all | solution.py:756
  68.8 25.4 %collective-permute-done.refs_1_ = bf16[256,2048]{1,0:T(8,128)(2,1)S(1)} collective-permute-done((bf16[256,2048]{1,0:T(8,128)(2,1)S(1)}, bf16[256,2048]{1,0:T(8,128)(2,1)S(1)}, u32[]{:S(2)}, u32[]{:S(2)}) %collective-permute-start) | collective-permute-done | bytes 1048608 | tf_op jit(solution)/shard_map/ppermute | solution.py:722
  95.1 24.6 %collective-permute-done.1.refs_2_ = bf16[256,2048]{1,0:T(8,128)(2,1)S(1)} collective-permute-done((bf16[256,2048]{1,0:T(8,128)(2,1)S(1)}, bf16[256,2048]{1,0:T(8,128)(2,1)S(1)}, u32[]{:S(2)}, u32[]{:S(2)}) %collective-permute-start.1) | collective-permute-done | bytes 1048608 | tf_op jit(solution)/shard_map/ppermute | solution.py:722
  123.0 23.7 %collective-permute-done.2.refs_3_ = bf16[256,2048]{1,0:T(8,128)(2,1)S(1)} collective-permute-done((bf16[256,2048]{1,0:T(8,128)(2,1)S(1)}, bf16[256,2048]{1,0:T(8,128)(2,1)S(1)}, u32[]{:S(2)}, u32[]{:S(2)}) %collective-permute-start.2) | collective-permute-done | bytes 1048608 | tf_op jit(solution)/shard_map/ppermute | solution.py:722
  146.7 23.1 %collective-permute-done.3.refs_1_ = bf16[256,2048]{1,0:T(8,128)(2,1)} collective-permute-done((bf16[256,2048]{1,0:T(8,128)(2,1)S(1)}, bf16[256,2048]{1,0:T(8,128)(2,1)}, u32[]{:S(2)}, u32[]{:S(2)}) %collective-permute-start.3) | collective-permute-done | bytes 1048608 | tf_op jit(solution)/shard_map/ppermute | solution.py:722
  173.2 17.9 %project.2 = (bf16[1024,2048]{1,0:T(8,128)(2,1)}, f32[1024,1536]{1,0:T(8,128)}, f32[3,1024,1]{2,1,0:T(8,128)}) custom-call(bf16[256,2048]{1,0:T(8,128)(2,1)} %copy-done.5, bf16[256,2048]{1,0:T(8,128)(2,1)} %copy-done.37, bf16[256,2048]{1,0:T(8,128)(2,1)} %copy-done.41, bf16[256,2048]{1,0:T(8,128)(2,1)} %copy-done.46, f32[1,2048]{1,0:T(1,128)} %copy.237.refs_4_, ...), custom_call_target="tpu_custom_call" | custom-call | flops 805306368 | bytes 1835008 | tf_op jit(solution)/shard_map/project/pallas_call | solution.py:91
  209.2 16.4 %attention.2 = (bf16[1,1024,512]{2,1,0:T(8,128)(2,1)}, bf16[1,1024,512]{2,1,0:T(8,128)(2,1)}, bf16[1,1024,512]{2,1,0:T(8,128)(2,1)}, bf16[4,1,256,512]{3,2,1,0:T(8,128)(2,1)}, f32[1,4,1024,1]{3,2,1,0:T(8,128)}) custom-call(s32[1]{0:T(128)} %bitcast.1.place_ref, s32[1]{0:T(128)} %bitcast.2.len_ref, f32[4,1,256,1536]{3,2,1,0:T(8,128)} %bitcast.166, ...), custom_call_target="tpu_custom_call" | custom-call | flops 201326592 | bytes 1310720 | tf_op jit(solution)/shard_map/attention/pallas_call | solution.py:158
  231.0 17.9 %project.3 = (bf16[1024,2048]{1,0:T(8,128)(2,1)}, f32[1024,1536]{1,0:T(8,128)}, f32[3,1024,1]{2,1,0:T(8,128)}) custom-call(bf16[256,2048]{1,0:T(8,128)(2,1)} %copy-done.3, bf16[256,2048]{1,0:T(8,128)(2,1)} %collective-permute-done.3.refs_1_, bf16[256,2048]{1,0:T(8,128)(2,1)} %collective-permute-done.4.refs_2_, bf16[256,2048]{1,0:T(8,128)(2,1)} %copy-done.36, ...), custom_call_target="tpu_custom_call" | custom-call | flops 805306368 | bytes 1835008 | tf_op jit(solution)/shard_map/project/pallas_call | solution.py:91
  267.1 16.7 %attention.3 = (bf16[1,1024,512]{2,1,0:T(8,128)(2,1)}, bf16[1,1024,512]{2,1,0:T(8,128)(2,1)}, bf16[1,1024,512]{2,1,0:T(8,128)(2,1)}, bf16[4,1,256,512]{3,2,1,0:T(8,128)(2,1)}, f32[1,4,1024,1]{3,2,1,0:T(8,128)}) custom-call(s32[1]{0:T(128)} %bitcast.1.place_ref, s32[1]{0:T(128)} %bitcast.31.len_ref, f32[4,1,256,1536]{3,2,1,0:T(8,128)} %bitcast.171, ...), custom_call_target="tpu_custom_call" | custom-call | flops 201326592 | bytes 1310720 | tf_op jit(solution)/shard_map/attention/pallas_call | solution.py:158
  289.9 33.9 %collective-permute-done.13.refs_2_ = bf16[256,2048]{1,0:T(8,128)(2,1)S(1)} collective-permute-done((bf16[256,2048]{1,0:T(8,128)(2,1)S(1)}, bf16[256,2048]{1,0:T(8,128)(2,1)S(1)}, u32[]{:S(2)}, u32[]{:S(2)}) %collective-permute-start.13) | collective-permute-done | bytes 1048608 | tf_op jit(solution)/shard_map/ppermute | solution.py:722
  338.6 14.2 %collective-permute-done.14.refs_3_ = bf16[256,2048]{1,0:T(8,128)(2,1)S(1)} collective-permute-done((bf16[256,2048]{1,0:T(8,128)(2,1)S(1)}, bf16[256,2048]{1,0:T(8,128)(2,1)S(1)}, u32[]{:S(2)}, u32[]{:S(2)}) %collective-permute-start.14) | collective-permute-done | bytes 1048608 | tf_op jit(solution)/shard_map/ppermute | solution.py:722
  353.8 23.5 %collective-permute-done.15.refs_5_ = bf16[256,2048]{1,0:T(8,128)(2,1)S(1)} collective-permute-done((bf16[256,2048]{1,0:T(8,128)(2,1)}, bf16[256,2048]{1,0:T(8,128)(2,1)S(1)}, u32[]{:S(2)}, u32[]{:S(2)}) %collective-permute-start.15) | collective-permute-done | bytes 1048608 | tf_op jit(solution)/shard_map/ppermute | solution.py:722
  377.5 23.0 %collective-permute-done.16.refs_6_ = bf16[256,2048]{1,0:T(8,128)(2,1)} collective-permute-done((bf16[256,2048]{1,0:T(8,128)(2,1)S(1)}, bf16[256,2048]{1,0:T(8,128)(2,1)}, u32[]{:S(2)}, u32[]{:S(2)}) %collective-permute-start.16) | collective-permute-done | bytes 1048608 | tf_op jit(solution)/shard_map/ppermute | solution.py:722
  404.1 19.9 %collective-permute-done.17.refs_7_ = bf16[256,2048]{1,0:T(8,128)(2,1)} collective-permute-done((bf16[256,2048]{1,0:T(8,128)(2,1)}, bf16[256,2048]{1,0:T(8,128)(2,1)}, u32[]{:S(2)}, u32[]{:S(2)}) %collective-permute-start.17) | collective-permute-done | bytes 1048608 | tf_op jit(solution)/shard_map/ppermute | solution.py:722
  425.0 34.9 %expert_forward.2 = (bf16[4,1280,2048]{2,1,0:T(8,128)(2,1)}, bf16[4,1280,1024]{2,1,0:T(8,128)(2,1)}, bf16[4,1280,1024]{2,1,0:T(8,128)(2,1)}, bf16[4,1280,1024]{2,1,0:T(8,128)(2,1)}) custom-call(bf16[256,2048]{1,0:T(8,128)(2,1)} %get-tuple-element.192.refs_0_, bf16[256,2048]{1,0:T(8,128)(2,1)} %copy-done.10, bf16[256,2048]{1,0:T(8,128)(2,1)} %copy-done.11, ...), custom_call_target="tpu_custom_call" | custom-call | flops 2684354560 | bytes 1048576 | tf_op jit(solution)/shard_map/expert_forward/pallas_call | solution.py:489
  470.0 35.0 %expert_forward.3 = (bf16[4,1280,2048]{2,1,0:T(8,128)(2,1)}, bf16[4,1280,1024]{2,1,0:T(8,128)(2,1)}, bf16[4,1280,1024]{2,1,0:T(8,128)(2,1)}, bf16[4,1280,1024]{2,1,0:T(8,128)(2,1)}) custom-call(bf16[256,2048]{1,0:T(8,128)(2,1)} %get-tuple-element.192.refs_0_, ...), custom_call_target="tpu_custom_call", output_to_operand_aliasing={{0}: (11, {}), {1}: (12, {}), {2}: (13, {}), {3}: (14, {})} | custom-call | flops 2684354560 | bytes 1048576 | tf_op jit(solution)/shard_map/expert_forward/pallas_call | solution.py:489
  516.6 41.2 %expert_output.1 = (bf16[256,2048]{1,0:T(8,128)(2,1)}, bf16[256,2048]{1,0:T(8,128)(2,1)}, bf16[256,2048]{1,0:T(8,128)(2,1)}, bf16[256,2048]{1,0:T(8,128)(2,1)}, ...) custom-call(bf16[4,1280,1024]{2,1,0:T(8,128)(2,1)} %get-tuple-elemen, ...), custom_call_target="tpu_custom_call" | custom-call | flops 2684354560 | bytes 4456448 | tf_op jit(solution)/shard_map/expert_output/pallas_call | solution.py:540
  562.7 60.5 %expert_backward.1 = (bf16[4,1280,1024]{2,1,0:T(8,128)(2,1)}, bf16[4,1280,1024]{2,1,0:T(8,128)(2,1)}, bf16[4,1024,2048]{2,1,0:T(8,128)(2,1)}) custom-call(bf16[256,2048]{1,0:T(8,128)(2,1)} %copy-done.4, bf16[256,2048]{1,0:T(8,128)(2,1)} %copy-done.29, bf16[256,2048]{1,0:T(8,128)(2,1)} %copy-done.33, bf16[256,2048]{1,0:T(8,128)(2,1)} %collective-permute-done.22.refs_3_, ...), custom_call_target="tpu_custom_call" | custom-call | flops 5368709120 | bytes 11796480 | tf_op jit(solution)/shard_map/expert_backward/pallas_call | solution.py:590
  634.2 35.9 %expert_input_grad.2 = (bf16[256,2048]{1,0:T(8,128)(2,1)}, bf16[256,2048]{1,0:T(8,128)(2,1)}, bf16[256,2048]{1,0:T(8,128)(2,1)}, bf16[256,2048]{1,0:T(8,128)(2,1)}) custom-call(bf16[4,1280,1024]{2,1,0:T(8,128)(2,1)} %get-tuple-element.257.dg_i, bf16[4,1280,1024]{2,1,0:T(8,128)(2,1)} %get-tuple-element.239.du_i, s32[8,4,256]{2,1,0:T(4,128)} %reshape.395.rank_ref, ...), custom_call_target="tpu_custom_call" | custom-call | flops 2684354560 | bytes 4718592 | tf_op jit(solution)/shard_map/expert_input_grad/pallas_call | solution.py:632
  670.1 29.0 %expert_weight_grad.2.rest_0_ = bf16[2,4,2048,1024]{3,2,1,0:T(8,128)(2,1)} custom-call(bf16[4,1280,2048]{2,1,0:T(8,128)(2,1)} %get-tuple-element.215.x_i, bf16[4,1280,1024]{2,1,0:T(8,128)(2,1)} %get-tuple-element.257.dg_i, bf16[4,1280,1024]{2,1,0:T(8,128)(2,1)} %get-tuple-element.239.du_i), custom_call_target="tpu_custom_call" | custom-call | flops 2684354560 | bytes 2621440 | tf_op jit(solution)/shard_map/expert_weight_grad/pallas_call | solution.py:663
  700.8 29.2 %expert_weight_grad.3 = bf16[2,4,2048,1024]{3,2,1,0:T(8,128)(2,1)} custom-call(bf16[4,1280,2048]{2,1,0:T(8,128)(2,1)} %get-tuple-element.215.x_i, bf16[4,1280,1024]{2,1,0:T(8,128)(2,1)} %get-tuple-element.257.dg_i, bf16[4,1280,1024]{2,1,0:T(8,128)(2,1)} %get-tuple-element.239.du_i, ...), custom_call_target="tpu_custom_call", output_to_operand_aliasing={{}: (3, {})} | custom-call | flops 2684354560 | bytes 2621440 | tf_op jit(solution)/shard_map/expert_weight_grad/pallas_call | solution.py:663
  736.7 35.8 %expert_input_grad.3 = (bf16[256,2048]{1,0:T(8,128)(2,1)}, bf16[256,2048]{1,0:T(8,128)(2,1)}, bf16[256,2048]{1,0:T(8,128)(2,1)}, bf16[256,2048]{1,0:T(8,128)(2,1)}) custom-call(bf16[4,1280,1024]{2,1,0:T(8,128)(2,1)} %get-tuple-element.257.dg_i, bf16[4,1280,1024]{2,1,0:T(8,128)(2,1)} %get-tuple-element.239.du_i, s32[8,4,256]{2,1,0:T(4,128)} %reshape.395.rank_ref, ...), custom_call_target="tpu_custom_call" | custom-call | flops 2684354560 | bytes 4718592 | tf_op jit(solution)/shard_map/expert_input_grad/pallas_call | solution.py:632
  801.8 27.2 %collective-permute-done.33 = bf16[256,2048]{1,0:T(8,128)(2,1)} collective-permute-done((bf16[256,2048]{1,0:T(8,128)(2,1)S(1)}, bf16[256,2048]{1,0:T(8,128)(2,1)}, u32[]{:S(2)}, u32[]{:S(2)}) %collective-permute-start.33) | collective-permute-done | bytes 1048608 | tf_op jit(solution)/shard_map/ppermute | solution.py:737
  839.1 28.0 %attention_back.2 = (f32[4,1,256,512]{3,2,1,0:T(8,128)}, f32[4,1,256,512]{3,2,1,0:T(8,128)}, bf16[4,1,256,512]{3,2,1,0:T(8,128)(2,1)}, f32[2,1,4,4,256,1]{5,4,3,2,1,0:T(8,128)}, f32[2,1,1,512]{3,2,1,0:T(1,128)}) custom-call(s32[1]{0:T(128)} %bitcast.1.place_ref, s32[1]{0:T(128)} %bitcast.2.len_ref, bf16[1,1024,512]{2,1,0:T(8,128)(2,1)} %get-tuple-element.270.q_i, ...), custom_call_target="tpu_custom_call" | custom-call | flops 469762048 | bytes 1441792 | tf_op jit(solution)/shard_map/attention_back/pallas_call | solution.py:242
  913.3 15.5 %back_project.2 = (bf16[256,2048]{1,0:T(8,128)(2,1)}, bf16[256,2048]{1,0:T(8,128)(2,1)}, bf16[256,2048]{1,0:T(8,128)(2,1)}, bf16[256,2048]{1,0:T(8,128)(2,1)}, bf16[1024,1536]{1,0:T(8,128)(2,1)}) custom-call(f32[1024,512]{1,0:T(8,128)} %bitcast.180, f32[1024,512]{1,0:T(8,128)} %bitcast.181, bf16[1024,512]{1,0:T(8,128)(2,1)} %bitcast.192, ...), custom_call_target="tpu_custom_call" | custom-call | flops 805306368 | bytes 1572864 | tf_op jit(solution)/shard_map/back_project/pallas_call | solution.py:309
  933.2 28.0 %attention_back.3 = (f32[4,1,256,512]{3,2,1,0:T(8,128)}, f32[4,1,256,512]{3,2,1,0:T(8,128)}, bf16[4,1,256,512]{3,2,1,0:T(8,128)(2,1)}, f32[2,1,4,4,256,1]{5,4,3,2,1,0:T(8,128)}, f32[2,1,1,512]{3,2,1,0:T(1,128)}) custom-call(s32[1]{0:T(128)} %bitcast.1.place_ref, s32[1]{0:T(128)} %bitcast.31.len_ref, bf16[1,1024,512]{2,1,0:T(8,128)(2,1)} %get-tuple-element.297.q_i, ...), custom_call_target="tpu_custom_call" | custom-call | flops 469762048 | bytes 1441792 | tf_op jit(solution)/shard_map/attention_back/pallas_call | solution.py:242
  977.3 15.5 %back_project.3 = (bf16[256,2048]{1,0:T(8,128)(2,1)}, bf16[256,2048]{1,0:T(8,128)(2,1)}, bf16[256,2048]{1,0:T(8,128)(2,1)}, bf16[256,2048]{1,0:T(8,128)(2,1)}, bf16[1024,1536]{1,0:T(8,128)(2,1)}) custom-call(f32[1024,512]{1,0:T(8,128)} %bitcast.182, f32[1024,512]{1,0:T(8,128)} %bitcast.183, bf16[1024,512]{1,0:T(8,128)(2,1)} %bitcast.193, ...), custom_call_target="tpu_custom_call" | custom-call | flops 805306368 | bytes 1572864 | tf_op jit(solution)/shard_map/back_project/pallas_call | solution.py:309
  997.5 19.0 %qkv_weight_grad.1 = bf16[2048,1664]{1,0:T(8,128)(2,1)} custom-call(bf16[1024,2048]{1,0:T(8,128)(2,1)} %get-tuple-element.318.refs_0_, bf16[1024,2048]{1,0:T(8,128)(2,1)} %get-tuple-element.319.refs_1_, bf16[1024,1536]{1,0:T(8,128)(2,1)} %get-tuple-element.289.refs_2_, bf16[1024,1536]{1,0:T(8,128)(2,1)} %get-tuple-element.311.refs_3_, ...), custom_call_target="tpu_custom_call" | custom-call | flops 1610612736 | bytes 2686976 | tf_op jit(solution)/shard_map/qkv_weight_grad/pallas_call | solution.py:425
  1026.3 15.0 %collective-permute-done.45 = bf16[256,2048]{1,0:T(8,128)(2,1)} collective-permute-done((bf16[256,2048]{1,0:T(8,128)(2,1)}, bf16[256,2048]{1,0:T(8,128)(2,1)}, u32[]{:S(2)}, u32[]{:S(2)}) %collective-permute-start.45) | collective-permute-done | bytes 1048608 | tf_op jit(solution)/shard_map/ppermute | solution.py:737
  1047.9 16.9 %collective-permute-done.46 = bf16[256,2048]{1,0:T(8,128)(2,1)S(1)} collective-permute-done((bf16[256,2048]{1,0:T(8,128)(2,1)S(1)}, bf16[256,2048]{1,0:T(8,128)(2,1)S(1)}, u32[]{:S(2)}, u32[]{:S(2)}) %collective-permute-start.46) | collective-permute-done | bytes 1048608 | tf_op jit(solution)/shard_map/ppermute | solution.py:737
  1080.2 14.3 %collective-permute-done.47 = bf16[256,2048]{1,0:T(8,128)(2,1)} collective-permute-done((bf16[256,2048]{1,0:T(8,128)(2,1)}, bf16[256,2048]{1,0:T(8,128)(2,1)}, u32[]{:S(2)}, u32[]{:S(2)}) %collective-permute-start.47) | collective-permute-done | bytes 1048608 | tf_op jit(solution)/shard_map/ppermute | solution.py:737
  1120.2 15.5 %all-to-all-done.6 = bf16[4,64,1664]{2,1,0:T(8,128)(2,1)} async-done(((bf16[4,64,1664]{2,1,0:T(8,128)(2,1)}), bf16[4,64,1664]{2,1,0:T(8,128)(2,1)}, u32[]{:S(2)}, u32[]{:S(2)}) %all-to-all-start.6) | async-done | bytes 852000 | tf_op jit(solution)/shard_map/all_to_all | solution.py:756
  (395 shorter events, 304.6 us)
Async XLA Ops:
  7.2 162.6 %all-gather.4.cloned.1.call-start = ((), (), s32[]{:S(2)}) async-start(), calls=%async_computation.11 | async-start | bytes 17694720 | tf_op jit(solution)/shard_map/all_gather | solution.py:779
  67.3 357.7 %all-gather.6.cloned.1.call-start = ((), (), s32[]{:S(2)}) async-start(), calls=%async_computation.12 | async-start | bytes 37748736 | tf_op jit(solution)/shard_map/all_gather | solution.py:840
  68.6 25.6 %collective-permute-start = (bf16[256,2048]{1,0:T(8,128)(2,1)S(1)}, bf16[256,2048]{1,0:T(8,128)(2,1)S(1)}, u32[]{:S(2)}, u32[]{:S(2)}) collective-permute-start(bf16[256,2048]{1,0:T(8,128)(2,1)S(1)} %get-tuple-element.177.refs_0_.x_i), channel_id=1, source_target_pairs={{0,1},{1,2},{2,3},{3,0},{4,5},{5,6},{6,7},{7,4},{8,9},{9,10},{10,1... | collective-permute-start | bytes 3145736 | tf_op jit(solution)/shard_map/ppermute | solution.py:722
  122.2 394.4 %all-gather.8.cloned.1.call-start = ((), (), s32[]{:S(2)}) async-start(), calls=%async_computation.13 | async-start | bytes 18874368 | tf_op jit(solution)/shard_map/all_gather | solution.py:843
  284.4 44.8 %all-to-all-start.2 = ((bf16[4,256,512]{2,1,0:T(8,128)(2,1)}), bf16[4,256,512]{2,1,0:T(8,128)(2,1)S(1)}, u32[]{:S(2)}, u32[]{:S(2)}) async-start(bf16[4,256,512]{2,1,0:T(8,128)(2,1)} %bitcast.198), calls=%async_computation.2 | async-start | bytes 2097152 | tf_op jit(solution)/shard_map/all_to_all | solution.py:756
  287.9 484.7 %reduce-scatter.5.cloned.1.call-start = ((), (), s32[]{:S(2)}) async-start(), calls=%async_computation.14 | async-start | bytes 18874368 | tf_op jit(solution)/shard_map/reduce_scatter | solution.py:934
  287.9 35.8 %collective-permute-start.13 = (bf16[256,2048]{1,0:T(8,128)(2,1)S(1)}, bf16[256,2048]{1,0:T(8,128)(2,1)S(1)}, u32[]{:S(2)}, u32[]{:S(2)}) collective-permute-start(bf16[256,2048]{1,0:T(8,128)(2,1)S(1)} %collective-permute-done.12.refs_1_), channel_id=1, source_target_pairs={{0,1},{1,2},{2,3},{3,0},{4,5},{5,6},{6,7},{7,4},{8,9},{9,10},{10,1... | collective-permute-start | bytes 3145736 | tf_op jit(solution)/shard_map/ppermute | solution.py:722
  424.0 36.0 %collective-permute-start.18 = (bf16[256,2048]{1,0:T(8,128)(2,1)S(1)}, bf16[256,2048]{1,0:T(8,128)(2,1)S(1)}, u32[]{:S(2)}, u32[]{:S(2)}) collective-permute-start(bf16[256,2048]{1,0:T(8,128)(2,1)S(1)} %get-tuple-element.211.refs_0_.l_i), channel_id=1, source_target_pairs={{0,1},{1,2},{2,3},{3,0},{4,5},{5,6},{6,7},{7,4},{8,9},{9,10},{10,1... | collective-permute-start | bytes 3145736 | tf_op jit(solution)/shard_map/ppermute | solution.py:722
  424.0 45.8 %collective-permute-start.19 = (bf16[256,2048]{1,0:T(8,128)(2,1)S(1)}, bf16[256,2048]{1,0:T(8,128)(2,1)}, u32[]{:S(2)}, u32[]{:S(2)}) collective-permute-start(bf16[256,2048]{1,0:T(8,128)(2,1)S(1)} %get-tuple-element.212.refs_4_.l_i), channel_id=1, source_target_pairs={{0,1},{1,2},{2,3},{3,0},{4,5},{5,6},{6,7},{7,4},{8,9},{9,10},{10,1... | collective-permute-start | bytes 3145736 | tf_op jit(solution)/shard_map/ppermute | solution.py:722
  469.8 35.2 %collective-permute-start.20 = (bf16[256,2048]{1,0:T(8,128)(2,1)S(1)}, bf16[256,2048]{1,0:T(8,128)(2,1)S(1)}, u32[]{:S(2)}, u32[]{:S(2)}) collective-permute-start(bf16[256,2048]{1,0:T(8,128)(2,1)S(1)} %collective-permute-done.18.refs_1_), channel_id=1, source_target_pairs={{0,1},{1,2},{2,3},{3,0},{4,5},{5,6},{6,7},{7,4},{8,9},{9,10},{10,1... | collective-permute-start | bytes 3145736 | tf_op jit(solution)/shard_map/ppermute | solution.py:722
  469.8 45.8 %collective-permute-start.21 = (bf16[256,2048]{1,0:T(8,128)(2,1)}, bf16[256,2048]{1,0:T(8,128)(2,1)S(1)}, u32[]{:S(2)}, u32[]{:S(2)}) collective-permute-start(bf16[256,2048]{1,0:T(8,128)(2,1)} %collective-permute-done.19.refs_5_), channel_id=1, source_target_pairs={{0,1},{1,2},{2,3},{3,0},{4,5},{5,6},{6,7},{7,4},{8,9},{9,10},{10,1... | collective-permute-start | bytes 3145736 | tf_op jit(solution)/shard_map/ppermute | solution.py:722
  515.6 42.1 %collective-permute-start.23 = (bf16[256,2048]{1,0:T(8,128)(2,1)S(1)}, bf16[256,2048]{1,0:T(8,128)(2,1)S(1)}, u32[]{:S(2)}, u32[]{:S(2)}) collective-permute-start(bf16[256,2048]{1,0:T(8,128)(2,1)S(1)} %collective-permute-done.21.refs_6_), channel_id=1, source_target_pairs={{0,1},{1,2},{2,3},{3,0},{4,5},{5,6},{6,7},{7,4},{8,9},{9,10},{10,1... | collective-permute-start | bytes 3145736 | tf_op jit(solution)/shard_map/ppermute | solution.py:722
  515.6 45.6 %collective-permute-start.22 = (bf16[256,2048]{1,0:T(8,128)(2,1)S(1)}, bf16[256,2048]{1,0:T(8,128)(2,1)}, u32[]{:S(2)}, u32[]{:S(2)}) collective-permute-start(bf16[256,2048]{1,0:T(8,128)(2,1)S(1)} %collective-permute-done.20.refs_2_), channel_id=1, source_target_pairs={{0,1},{1,2},{2,3},{3,0},{4,5},{5,6},{6,7},{7,4},{8,9},{9,10},{10,1... | collective-permute-start | bytes 3145736 | tf_op jit(solution)/shard_map/ppermute | solution.py:722
  561.2 61.9 %collective-permute-start.25 = (bf16[256,2048]{1,0:T(8,128)(2,1)}, bf16[256,2048]{1,0:T(8,128)(2,1)}, u32[]{:S(2)}, u32[]{:S(2)}) collective-permute-start(bf16[256,2048]{1,0:T(8,128)(2,1)} %get-tuple-element.235), channel_id=1, source_target_pairs={{0,1},{1,2},{2,3},{3,0},{4,5},{5,6},{6,7},{7,4},{8,9},{9,10},{10,1... | collective-permute-start | bytes 3145736 | tf_op jit(solution)/shard_map/ppermute | solution.py:737
  561.2 61.9 %collective-permute-start.24 = (bf16[256,2048]{1,0:T(8,128)(2,1)}, bf16[256,2048]{1,0:T(8,128)(2,1)}, u32[]{:S(2)}, u32[]{:S(2)}) collective-permute-start(bf16[256,2048]{1,0:T(8,128)(2,1)} %get-tuple-element.232), channel_id=1, source_target_pairs={{0,1},{1,2},{2,3},{3,0},{4,5},{5,6},{6,7},{7,4},{8,9},{9,10},{10,1... | collective-permute-start | bytes 3145736 | tf_op jit(solution)/shard_map/ppermute | solution.py:737
  623.2 349.1 %reduce-scatter.7.cloned.1.call-start = ((), (), s32[]{:S(2)}) async-start(), calls=%async_computation.15 | async-start | bytes 37748736 | tf_op jit(solution)/shard_map/reduce_scatter | solution.py:955
  626.9 43.1 %collective-permute-start.27 = (bf16[256,2048]{1,0:T(8,128)(2,1)}, bf16[256,2048]{1,0:T(8,128)(2,1)S(1)}, u32[]{:S(2)}, u32[]{:S(2)}) collective-permute-start(bf16[256,2048]{1,0:T(8,128)(2,1)} %add_convert_fusion.10), channel_id=1, source_target_pairs={{0,1},{1,2},{2,3},{3,0},{4,5},{5,6},{6,7},{7,4},{8,9},{9,10},{10,1... | collective-permute-start | bytes 3145736 | tf_op jit(solution)/shard_map/ppermute | solution.py:737
  630.0 40.0 %collective-permute-start.26 = (bf16[256,2048]{1,0:T(8,128)(2,1)}, bf16[256,2048]{1,0:T(8,128)(2,1)S(1)}, u32[]{:S(2)}, u32[]{:S(2)}) collective-permute-start(bf16[256,2048]{1,0:T(8,128)(2,1)} %add_convert_fusion.11), channel_id=1, source_target_pairs={{0,1},{1,2},{2,3},{3,0},{4,5},{5,6},{6,7},{7,4},{8,9},{9,10},{10,1... | collective-permute-start | bytes 3145736 | tf_op jit(solution)/shard_map/ppermute | solution.py:737
  670.1 29.1 %collective-permute-start.28 = (bf16[256,2048]{1,0:T(8,128)(2,1)}, bf16[256,2048]{1,0:T(8,128)(2,1)S(1)}, u32[]{:S(2)}, u32[]{:S(2)}) collective-permute-start(bf16[256,2048]{1,0:T(8,128)(2,1)} %get-tuple-element.247), channel_id=1, source_target_pairs={{0,1},{1,2},{2,3},{3,0},{4,5},{5,6},{6,7},{7,4},{8,9},{9,10},{10,1... | collective-permute-start | bytes 3145736 | tf_op jit(solution)/shard_map/ppermute | solution.py:737
  699.5 30.4 %collective-permute-start.29 = (bf16[256,2048]{1,0:T(8,128)(2,1)S(1)}, bf16[256,2048]{1,0:T(8,128)(2,1)}, u32[]{:S(2)}, u32[]{:S(2)}) collective-permute-start(bf16[256,2048]{1,0:T(8,128)(2,1)S(1)} %add_convert_fusion.9), channel_id=1, source_target_pairs={{0,1},{1,2},{2,3},{3,0},{4,5},{5,6},{6,7},{7,4},{8,9},{9,10},{10,1... | collective-permute-start | bytes 3145736 | tf_op jit(solution)/shard_map/ppermute | solution.py:737
  731.6 41.0 %collective-permute-start.30 = (bf16[256,2048]{1,0:T(8,128)(2,1)S(1)}, bf16[256,2048]{1,0:T(8,128)(2,1)S(1)}, u32[]{:S(2)}, u32[]{:S(2)}) collective-permute-start(bf16[256,2048]{1,0:T(8,128)(2,1)S(1)} %add_convert_fusion.8), channel_id=1, source_target_pairs={{0,1},{1,2},{2,3},{3,0},{4,5},{5,6},{6,7},{7,4},{8,9},{9,10},{10,1... | collective-permute-start | bytes 3145736 | tf_op jit(solution)/shard_map/ppermute | solution.py:737
  734.7 37.9 %collective-permute-start.31 = (bf16[256,2048]{1,0:T(8,128)(2,1)S(1)}, bf16[256,2048]{1,0:T(8,128)(2,1)S(1)}, u32[]{:S(2)}, u32[]{:S(2)}) collective-permute-start(bf16[256,2048]{1,0:T(8,128)(2,1)S(1)} %add_convert_fusion.7), channel_id=1, source_target_pairs={{0,1},{1,2},{2,3},{3,0},{4,5},{5,6},{6,7},{7,4},{8,9},{9,10},{10,1... | collective-permute-start | bytes 3145736 | tf_op jit(solution)/shard_map/ppermute | solution.py:737
  794.2 40.3 %all-to-all-start.3 = ((bf16[4,256,512]{2,1,0:T(8,128)(2,1)}), bf16[4,256,512]{2,1,0:T(8,128)(2,1)S(1)}, u32[]{:S(2)}, u32[]{:S(2)}) async-start(bf16[4,256,512]{2,1,0:T(8,128)(2,1)} %get-tuple-element.267), calls=%async_computation.4 | async-start | bytes 2097152 | tf_op jit(solution)/shard_map/all_to_all | solution.py:756
  799.8 29.3 %collective-permute-start.33 = (bf16[256,2048]{1,0:T(8,128)(2,1)S(1)}, bf16[256,2048]{1,0:T(8,128)(2,1)}, u32[]{:S(2)}, u32[]{:S(2)}) collective-permute-start(bf16[256,2048]{1,0:T(8,128)(2,1)S(1)} %add_convert_fusion.6), channel_id=1, source_target_pairs={{0,1},{1,2},{2,3},{3,0},{4,5},{5,6},{6,7},{7,4},{8,9},{9,10},{10,1... | collective-permute-start | bytes 3145736 | tf_op jit(solution)/shard_map/ppermute | solution.py:737
  837.5 32.2 %collective-permute-start.34 = (bf16[256,2048]{1,0:T(8,128)(2,1)}, bf16[256,2048]{1,0:T(8,128)(2,1)S(1)}, u32[]{:S(2)}, u32[]{:S(2)}) collective-permute-start(bf16[256,2048]{1,0:T(8,128)(2,1)} %add_convert_fusion.5), channel_id=1, source_target_pairs={{0,1},{1,2},{2,3},{3,0},{4,5},{5,6},{6,7},{7,4},{8,9},{9,10},{10,1... | collective-permute-start | bytes 3145736 | tf_op jit(solution)/shard_map/ppermute | solution.py:737
  895.6 33.3 %all-to-all-start.4 = ((bf16[4,256,512]{2,1,0:T(8,128)(2,1)}), bf16[4,256,512]{2,1,0:T(8,128)(2,1)S(1)}, u32[]{:S(2)}, u32[]{:S(2)}) async-start(bf16[4,256,512]{2,1,0:T(8,128)(2,1)} %get-tuple-element.288), calls=%async_computation.5 | async-start | bytes 2097152 | tf_op jit(solution)/shard_map/all_to_all | solution.py:756
  899.1 127.2 %reduce-scatter.9.cloned.1.call-start = ((), (), s32[]{:S(2)}) async-start(), calls=%async_computation.16 | async-start | bytes 10027008 | tf_op jit(solution)/shard_map/reduce_scatter | solution.py:979
  929.9 179.6 %reduce-scatter.11.cloned.1.call-start = ((), (), s32[]{:S(2)}) async-start(), calls=%async_computation.17 | async-start | bytes 7667712 | tf_op jit(solution)/shard_map/reduce_scatter | solution.py:1012
  929.9 34.8 %collective-permute-start.39 = (bf16[256,2048]{1,0:T(8,128)(2,1)}, bf16[256,2048]{1,0:T(8,128)(2,1)S(1)}, u32[]{:S(2)}, u32[]{:S(2)}) collective-permute-start(bf16[256,2048]{1,0:T(8,128)(2,1)} %get-tuple-element.295), channel_id=1, source_target_pairs={{0,1},{1,2},{2,3},{3,0},{4,5},{5,6},{6,7},{7,4},{8,9},{9,10},{10,1... | collective-permute-start | bytes 3145736 | tf_op jit(solution)/shard_map/ppermute | solution.py:737
  1066.2 28.3 %collective-permute-start.47 = (bf16[256,2048]{1,0:T(8,128)(2,1)}, bf16[256,2048]{1,0:T(8,128)(2,1)}, u32[]{:S(2)}, u32[]{:S(2)}) collective-permute-start(bf16[256,2048]{1,0:T(8,128)(2,1)} %add_convert_fusion), channel_id=1, source_target_pairs={{0,1},{1,2},{2,3},{3,0},{4,5},{5,6},{6,7},{7,4},{8,9},{9,10},{10,1... | collective-permute-start | bytes 3145736 | tf_op jit(solution)/shard_map/ppermute | solution.py:737
  1067.7 41.7 %all-to-all-start.5 = ((bf16[4,64,2176]{2,1,0:T(8,128)(2,1)}), bf16[4,64,2176]{2,1,0:T(8,128)(2,1)S(1)}, u32[]{:S(2)}, u32[]{:S(2)}) async-start(bf16[4,64,2176]{2,1,0:T(8,128)(2,1)} %bitcast.191), calls=%async_computation.8 | async-start | bytes 2228224 | tf_op jit(solution)/shard_map/all_to_all | solution.py:756
  1109.5 26.2 %all-to-all-start.6 = ((bf16[4,64,1664]{2,1,0:T(8,128)(2,1)}), bf16[4,64,1664]{2,1,0:T(8,128)(2,1)}, u32[]{:S(2)}, u32[]{:S(2)}) async-start(bf16[4,64,1664]{2,1,0:T(8,128)(2,1)} %bitcast.199), calls=%async_computation.10 | async-start | bytes 1703936 | tf_op jit(solution)/shard_map/all_to_all | solution.py:756
  (102 other events, 1737.7 us)
Sparse Core Ops, SparseCore 0:
  67.4 84.5 all-gather.3
  154.6 160.7 all-gather.5
  317.3 93.1 all-gather.7
  623.3 116.5 reduce-scatter.4
  743.3 205.2 reduce-scatter.6
  952.4 73.7 reduce-scatter.8
  1030.1 64.2 reduce-scatter.10

commit v5 on v4

--- a/solution.py
+++ b/solution.py
@@ -203,15 +203,16 @@
             at = slice(p * rows, (p + 1) * rows)
             kv = (p + 1) * rows
             query, keys, values, do = q_i[0, at, :], k_i[0, :kv, :], v_i[0, :kv, :], do_i[p, 0]
-            s = dot_nt(query, keys) * scale
-            probs = jnp.where(
-                allowed_of(p * rows, rows, kv, length), jnp.exp(s - lse_i[0, 0, at, :]), 0.0
-            )
-            dp = dot_nt(do, values)
-            ds = (probs * (dp - jnp.sum(probs * dp, axis=-1, keepdims=True))).astype(bf16)
-            dq_s[at, :] = dot(ds, keys) * scale
-            dk_s[:kv, :] += dot_tn(ds, query)
-            dv_s[:kv, :] += dot_tn(probs.astype(bf16), do)
+            s = dot_nt(keys, query) * scale
+            col = lax.broadcasted_iota(jnp.int32, (kv, rows), 0)
+            row = p * rows + lax.broadcasted_iota(jnp.int32, (kv, rows), 1)
+            allowed = (col <= row) & (col < length)
+            probs = jnp.where(allowed, jnp.exp(s - lse_i[0, 0, :, at]), 0.0)
+            dp = dot_nt(values, do)
+            ds = (probs * (dp - jnp.sum(probs * dp, axis=0, keepdims=True))).astype(bf16)
+            dq_s[at, :] = dot_tn(ds, keys) * scale
+            dk_s[:kv, :] += dot(ds, query)
+            dv_s[:kv, :] += dot(probs.astype(bf16), do)
         dk_s[...] = dk_s[...] * scale
         sums = [jnp.zeros((1, HEAD_DIM), f32)] * 2
         for p in range(n):
@@ -249,7 +250,7 @@
                 line,
                 line,
                 block,
-                pl.BlockSpec((1, 1, span, 1), lambda g, h, *_: (g, h, 0, 0)),
+                pl.BlockSpec((1, 1, 1, span), lambda g, h, *_: (g, h, 0, 0)),
                 part(0),
                 part(1),
                 pl.BlockSpec((2, n, 1, rows, 1), lambda g, h, *_: (0, 0, g, 0, 0)),
@@ -270,7 +271,10 @@
         compiler_params=params(2),
         cost_estimate=cost(7 * seqs * heads * span * span * HEAD_DIM, qkv, *outs[:3]),
         name="attention_back",
-    )(place, lengths, q, k, v, grad, lse, qkv, qkv, inverse, gains, cosines, sines)
+    )(
+        place, lengths, q, k, v, grad, lse.reshape(seqs, heads, 1, span), qkv, qkv, inverse, gains,
+        cosines, sines,
+    )
 
 
 def back_project(dzq, dzk, dv, qkv, inverse, stats, gains, weight, first, pieces):

time: 1160 us -> 1160 us (level)
  transfers between devices with their start and end apart: 61 -> 61, of which waited for: 30 -> 31; matrix products, arithmetic and copies ran while one was open for 7% -> 7% of each run, Pallas kernels for 46% -> 45%
where the time goes in v5:
time: 1160 us; the launch traced here: 1140 us
  Pallas kernels  516 us (44%)
  waiting for transfers between devices  384 us (33%)
  starting transfers between devices  68.2 us (6%)
  other arithmetic  59.1 us (5%)
  blocking collectives  51.9 us (4%)
  local copies, waits for them, and re-layouts  48 us (4%)
  between operations  15.6 us (1%)
    ppermute x18, waiting for transfers between devices, hop(): self.held.append(lax.ppermute(after(self.held[-1], prev), 'ctx', up))  236 us
    ppermute x18, waiting for transfers between devices, hop(): self.moved = lax.ppermute(part, 'ctx', up)  81.6 us
    pallas_call x2, Pallas kernels, expert_input_grad(): pl.pallas_call(kernel, grid=(width // tile, experts), in_specs=[line, lin...  71.3 us
    pallas_call x2, Pallas kernels, expert_forward(): pl.pallas_call(kernel, grid=(stop - start, hidden // tile), in_specs=[who...  69.9 us
    pallas_call x1, Pallas kernels, expert_backward(): pl.pallas_call(kernel, grid=(experts, hidden // tile), in_specs=[whole(x)...  60.4 us
    pallas_call x2, Pallas kernels, expert_weight_grad(): pl.pallas_call(kernel, grid=(stop - start, width // tile), in_specs=[pl.B...  59.1 us
    all_to_all x1, blocking collectives, exchange(): return lax.all_to_all(x, 'ctx', split_axis=0, concat_axis=0, tiled=True)  51.9 us
    pallas_call x2, Pallas kernels, attention_backward(): pl.pallas_call(kernel, grid_spec=pltpu.PrefetchScalarGridSpec(num_scalar_...  47.7 us
  transfers between devices with their start and end apart: 61, of which 31 were waited for; matrix products, arithmetic and copies ran while one was open for 7% of the time, Pallas kernels for 45%

profile of v5, /device:TPU:0, one launch (start us, length us, event | category | flops | bytes accessed | tf_op | source)
XLA Modules:
  0.0 1144.3 jit_solution(14702132320322772822)
XLA Ops:
  15.3 51.9 %all_to_all.35 = bf16[4,64,3840]{2,1,0:T(8,128)(2,1)} all-to-all(bf16[4,64,3840]{2,1,0:T(8,128)(2,1)} %broadcast_dynamic-update-slice_fusion.1), channel_id=1, replica_groups=mesh['batch'=8,'ctx'=4] {'ctx'}, dimensions={0} | all-to-all | bytes 3932160 | tf_op jit(solution)/shard_map/all_to_all | solution.py:760
  68.8 25.3 %collective-permute-done.refs_1_ = bf16[256,2048]{1,0:T(8,128)(2,1)S(1)} collective-permute-done((bf16[256,2048]{1,0:T(8,128)(2,1)S(1)}, bf16[256,2048]{1,0:T(8,128)(2,1)S(1)}, u32[]{:S(2)}, u32[]{:S(2)}) %collective-permute-start) | collective-permute-done | bytes 1048608 | tf_op jit(solution)/shard_map/ppermute | solution.py:726
  95.1 24.6 %collective-permute-done.1.refs_2_ = bf16[256,2048]{1,0:T(8,128)(2,1)S(1)} collective-permute-done((bf16[256,2048]{1,0:T(8,128)(2,1)S(1)}, bf16[256,2048]{1,0:T(8,128)(2,1)S(1)}, u32[]{:S(2)}, u32[]{:S(2)}) %collective-permute-start.1) | collective-permute-done | bytes 1048608 | tf_op jit(solution)/shard_map/ppermute | solution.py:726
  123.0 23.7 %collective-permute-done.2.refs_3_ = bf16[256,2048]{1,0:T(8,128)(2,1)S(1)} collective-permute-done((bf16[256,2048]{1,0:T(8,128)(2,1)S(1)}, bf16[256,2048]{1,0:T(8,128)(2,1)S(1)}, u32[]{:S(2)}, u32[]{:S(2)}) %collective-permute-start.2) | collective-permute-done | bytes 1048608 | tf_op jit(solution)/shard_map/ppermute | solution.py:726
  146.7 23.1 %collective-permute-done.3.refs_1_ = bf16[256,2048]{1,0:T(8,128)(2,1)} collective-permute-done((bf16[256,2048]{1,0:T(8,128)(2,1)S(1)}, bf16[256,2048]{1,0:T(8,128)(2,1)}, u32[]{:S(2)}, u32[]{:S(2)}) %collective-permute-start.3) | collective-permute-done | bytes 1048608 | tf_op jit(solution)/shard_map/ppermute | solution.py:726
  173.2 17.9 %project.2 = (bf16[1024,2048]{1,0:T(8,128)(2,1)}, f32[1024,1536]{1,0:T(8,128)}, f32[3,1024,1]{2,1,0:T(8,128)}) custom-call(bf16[256,2048]{1,0:T(8,128)(2,1)} %copy-done.5, bf16[256,2048]{1,0:T(8,128)(2,1)} %copy-done.41, bf16[256,2048]{1,0:T(8,128)(2,1)} %copy-done.44, bf16[256,2048]{1,0:T(8,128)(2,1)} %copy-done.49, f32[1,2048]{1,0:T(1,128)} %copy.247.refs_4_, ...), custom_call_target="tpu_custom_call" | custom-call | flops 805306368 | bytes 1835008 | tf_op jit(solution)/shard_map/project/pallas_call | solution.py:91
  209.2 16.4 %attention.2 = (bf16[1,1024,512]{2,1,0:T(8,128)(2,1)}, bf16[1,1024,512]{2,1,0:T(8,128)(2,1)}, bf16[1,1024,512]{2,1,0:T(8,128)(2,1)}, bf16[4,1,256,512]{3,2,1,0:T(8,128)(2,1)}, f32[1,4,1024,1]{3,2,1,0:T(8,128)}) custom-call(s32[1]{0:T(128)} %bitcast.1.place_ref, s32[1]{0:T(128)} %bitcast.2.len_ref, f32[4,1,256,1536]{3,2,1,0:T(8,128)} %bitcast.166, ...), custom_call_target="tpu_custom_call" | custom-call | flops 201326592 | bytes 1310720 | tf_op jit(solution)/shard_map/attention/pallas_call | solution.py:158
  231.0 17.9 %project.3 = (bf16[1024,2048]{1,0:T(8,128)(2,1)}, f32[1024,1536]{1,0:T(8,128)}, f32[3,1024,1]{2,1,0:T(8,128)}) custom-call(bf16[256,2048]{1,0:T(8,128)(2,1)} %copy-done.3, bf16[256,2048]{1,0:T(8,128)(2,1)} %collective-permute-done.3.refs_1_, bf16[256,2048]{1,0:T(8,128)(2,1)} %collective-permute-done.4.refs_2_, bf16[256,2048]{1,0:T(8,128)(2,1)} %copy-done.40, ...), custom_call_target="tpu_custom_call" | custom-call | flops 805306368 | bytes 1835008 | tf_op jit(solution)/shard_map/project/pallas_call | solution.py:91
  267.1 16.7 %attention.3 = (bf16[1,1024,512]{2,1,0:T(8,128)(2,1)}, bf16[1,1024,512]{2,1,0:T(8,128)(2,1)}, bf16[1,1024,512]{2,1,0:T(8,128)(2,1)}, bf16[4,1,256,512]{3,2,1,0:T(8,128)(2,1)}, f32[1,4,1024,1]{3,2,1,0:T(8,128)}) custom-call(s32[1]{0:T(128)} %bitcast.1.place_ref, s32[1]{0:T(128)} %bitcast.31.len_ref, f32[4,1,256,1536]{3,2,1,0:T(8,128)} %bitcast.171, ...), custom_call_target="tpu_custom_call" | custom-call | flops 201326592 | bytes 1310720 | tf_op jit(solution)/shard_map/attention/pallas_call | solution.py:158
  289.8 33.9 %collective-permute-done.13.refs_2_ = bf16[256,2048]{1,0:T(8,128)(2,1)S(1)} collective-permute-done((bf16[256,2048]{1,0:T(8,128)(2,1)S(1)}, bf16[256,2048]{1,0:T(8,128)(2,1)S(1)}, u32[]{:S(2)}, u32[]{:S(2)}) %collective-permute-start.13) | collective-permute-done | bytes 1048608 | tf_op jit(solution)/shard_map/ppermute | solution.py:726
  338.5 14.2 %collective-permute-done.14.refs_3_ = bf16[256,2048]{1,0:T(8,128)(2,1)S(1)} collective-permute-done((bf16[256,2048]{1,0:T(8,128)(2,1)S(1)}, bf16[256,2048]{1,0:T(8,128)(2,1)S(1)}, u32[]{:S(2)}, u32[]{:S(2)}) %collective-permute-start.14) | collective-permute-done | bytes 1048608 | tf_op jit(solution)/shard_map/ppermute | solution.py:726
  353.7 23.5 %collective-permute-done.15.refs_5_ = bf16[256,2048]{1,0:T(8,128)(2,1)S(1)} collective-permute-done((bf16[256,2048]{1,0:T(8,128)(2,1)}, bf16[256,2048]{1,0:T(8,128)(2,1)S(1)}, u32[]{:S(2)}, u32[]{:S(2)}) %collective-permute-start.15) | collective-permute-done | bytes 1048608 | tf_op jit(solution)/shard_map/ppermute | solution.py:726
  377.4 23.0 %collective-permute-done.16.refs_6_ = bf16[256,2048]{1,0:T(8,128)(2,1)} collective-permute-done((bf16[256,2048]{1,0:T(8,128)(2,1)S(1)}, bf16[256,2048]{1,0:T(8,128)(2,1)}, u32[]{:S(2)}, u32[]{:S(2)}) %collective-permute-start.16) | collective-permute-done | bytes 1048608 | tf_op jit(solution)/shard_map/ppermute | solution.py:726
  404.0 19.9 %collective-permute-done.17.refs_7_ = bf16[256,2048]{1,0:T(8,128)(2,1)} collective-permute-done((bf16[256,2048]{1,0:T(8,128)(2,1)}, bf16[256,2048]{1,0:T(8,128)(2,1)}, u32[]{:S(2)}, u32[]{:S(2)}) %collective-permute-start.17) | collective-permute-done | bytes 1048608 | tf_op jit(solution)/shard_map/ppermute | solution.py:726
  425.0 34.9 %expert_forward.2 = (bf16[4,1280,2048]{2,1,0:T(8,128)(2,1)}, bf16[4,1280,1024]{2,1,0:T(8,128)(2,1)}, bf16[4,1280,1024]{2,1,0:T(8,128)(2,1)}, bf16[4,1280,1024]{2,1,0:T(8,128)(2,1)}) custom-call(bf16[256,2048]{1,0:T(8,128)(2,1)} %get-tuple-element.192.refs_0_, bf16[256,2048]{1,0:T(8,128)(2,1)} %copy-done.10, bf16[256,2048]{1,0:T(8,128)(2,1)} %copy-done.11, ...), custom_call_target="tpu_custom_call" | custom-call | flops 2684354560 | bytes 1048576 | tf_op jit(solution)/shard_map/expert_forward/pallas_call | solution.py:493
  469.9 35.0 %expert_forward.3 = (bf16[4,1280,2048]{2,1,0:T(8,128)(2,1)}, bf16[4,1280,1024]{2,1,0:T(8,128)(2,1)}, bf16[4,1280,1024]{2,1,0:T(8,128)(2,1)}, bf16[4,1280,1024]{2,1,0:T(8,128)(2,1)}) custom-call(bf16[256,2048]{1,0:T(8,128)(2,1)} %get-tuple-element.192.refs_0_, ...), custom_call_target="tpu_custom_call", output_to_operand_aliasing={{0}: (11, {}), {1}: (12, {}), {2}: (13, {}), {3}: (14, {})} | custom-call | flops 2684354560 | bytes 1048576 | tf_op jit(solution)/shard_map/expert_forward/pallas_call | solution.py:493
  516.5 41.2 %expert_output.1 = (bf16[256,2048]{1,0:T(8,128)(2,1)}, bf16[256,2048]{1,0:T(8,128)(2,1)}, bf16[256,2048]{1,0:T(8,128)(2,1)}, bf16[256,2048]{1,0:T(8,128)(2,1)}, ...) custom-call(bf16[4,1280,1024]{2,1,0:T(8,128)(2,1)} %get-tuple-elemen, ...), custom_call_target="tpu_custom_call" | custom-call | flops 2684354560 | bytes 4456448 | tf_op jit(solution)/shard_map/expert_output/pallas_call | solution.py:544
  562.6 60.4 %expert_backward.1 = (bf16[4,1280,1024]{2,1,0:T(8,128)(2,1)}, bf16[4,1280,1024]{2,1,0:T(8,128)(2,1)}, bf16[4,1024,2048]{2,1,0:T(8,128)(2,1)}) custom-call(bf16[256,2048]{1,0:T(8,128)(2,1)} %copy-done.4, bf16[256,2048]{1,0:T(8,128)(2,1)} %copy-done.33, bf16[256,2048]{1,0:T(8,128)(2,1)} %copy-done.37, bf16[256,2048]{1,0:T(8,128)(2,1)} %collective-permute-done.22.refs_3_, ...), custom_call_target="tpu_custom_call" | custom-call | flops 5368709120 | bytes 11796480 | tf_op jit(solution)/shard_map/expert_backward/pallas_call | solution.py:594
  633.1 35.6 %expert_input_grad.2 = (bf16[256,2048]{1,0:T(8,128)(2,1)}, bf16[256,2048]{1,0:T(8,128)(2,1)}, bf16[256,2048]{1,0:T(8,128)(2,1)}, bf16[256,2048]{1,0:T(8,128)(2,1)}) custom-call(bf16[4,1280,1024]{2,1,0:T(8,128)(2,1)} %get-tuple-element.257.dg_i, bf16[4,1280,1024]{2,1,0:T(8,128)(2,1)} %get-tuple-element.239.du_i, s32[8,4,256]{2,1,0:T(4,128)} %reshape.401.rank_ref, ...), custom_call_target="tpu_custom_call" | custom-call | flops 2684354560 | bytes 4718592 | tf_op jit(solution)/shard_map/expert_input_grad/pallas_call | solution.py:636
  669.2 29.2 %expert_weight_grad.2.rest_0_ = bf16[2,4,2048,1024]{3,2,1,0:T(8,128)(2,1)} custom-call(bf16[4,1280,2048]{2,1,0:T(8,128)(2,1)} %get-tuple-element.215.x_i, bf16[4,1280,1024]{2,1,0:T(8,128)(2,1)} %get-tuple-element.257.dg_i, bf16[4,1280,1024]{2,1,0:T(8,128)(2,1)} %get-tuple-element.239.du_i), custom_call_target="tpu_custom_call" | custom-call | flops 2684354560 | bytes 2621440 | tf_op jit(solution)/shard_map/expert_weight_grad/pallas_call | solution.py:667
  700.2 29.9 %expert_weight_grad.3 = bf16[2,4,2048,1024]{3,2,1,0:T(8,128)(2,1)} custom-call(bf16[4,1280,2048]{2,1,0:T(8,128)(2,1)} %get-tuple-element.215.x_i, bf16[4,1280,1024]{2,1,0:T(8,128)(2,1)} %get-tuple-element.257.dg_i, bf16[4,1280,1024]{2,1,0:T(8,128)(2,1)} %get-tuple-element.239.du_i, ...), custom_call_target="tpu_custom_call", output_to_operand_aliasing={{}: (3, {})} | custom-call | flops 2684354560 | bytes 2621440 | tf_op jit(solution)/shard_map/expert_weight_grad/pallas_call | solution.py:667
  735.4 35.7 %expert_input_grad.3 = (bf16[256,2048]{1,0:T(8,128)(2,1)}, bf16[256,2048]{1,0:T(8,128)(2,1)}, bf16[256,2048]{1,0:T(8,128)(2,1)}, bf16[256,2048]{1,0:T(8,128)(2,1)}) custom-call(bf16[4,1280,1024]{2,1,0:T(8,128)(2,1)} %get-tuple-element.257.dg_i, bf16[4,1280,1024]{2,1,0:T(8,128)(2,1)} %get-tuple-element.239.du_i, s32[8,4,256]{2,1,0:T(4,128)} %reshape.401.rank_ref, ...), custom_call_target="tpu_custom_call" | custom-call | flops 2684354560 | bytes 4718592 | tf_op jit(solution)/shard_map/expert_input_grad/pallas_call | solution.py:636
  802.5 26.2 %collective-permute-done.33 = bf16[256,2048]{1,0:T(8,128)(2,1)} collective-permute-done((bf16[256,2048]{1,0:T(8,128)(2,1)S(1)}, bf16[256,2048]{1,0:T(8,128)(2,1)}, u32[]{:S(2)}, u32[]{:S(2)}) %collective-permute-start.33) | collective-permute-done | bytes 1048608 | tf_op jit(solution)/shard_map/ppermute | solution.py:741
  840.1 24.0 %attention_back.2 = (f32[4,1,256,512]{3,2,1,0:T(8,128)}, f32[4,1,256,512]{3,2,1,0:T(8,128)}, bf16[4,1,256,512]{3,2,1,0:T(8,128)(2,1)}, f32[2,1,4,4,256,1]{5,4,3,2,1,0:T(8,128)}, f32[2,1,1,512]{3,2,1,0:T(1,128)}) custom-call(s32[1]{0:T(128)} %bitcast.1.place_ref, s32[1]{0:T(128)} %bitcast.2.len_ref, bf16[1,1024,512]{2,1,0:T(8,128)(2,1)} %get-tuple-element.270.q_i, ...), custom_call_target="tpu_custom_call" | custom-call | flops 469762048 | bytes 1441792 | tf_op jit(solution)/shard_map/attention_back/pallas_call | solution.py:243
  910.4 15.5 %back_project.2 = (bf16[256,2048]{1,0:T(8,128)(2,1)}, bf16[256,2048]{1,0:T(8,128)(2,1)}, bf16[256,2048]{1,0:T(8,128)(2,1)}, bf16[256,2048]{1,0:T(8,128)(2,1)}, bf16[1024,1536]{1,0:T(8,128)(2,1)}) custom-call(f32[1024,512]{1,0:T(8,128)} %bitcast.180, f32[1024,512]{1,0:T(8,128)} %bitcast.181, bf16[1024,512]{1,0:T(8,128)(2,1)} %bitcast.192, ...), custom_call_target="tpu_custom_call" | custom-call | flops 805306368 | bytes 1572864 | tf_op jit(solution)/shard_map/back_project/pallas_call | solution.py:313
  931.4 23.7 %attention_back.3 = (f32[4,1,256,512]{3,2,1,0:T(8,128)}, f32[4,1,256,512]{3,2,1,0:T(8,128)}, bf16[4,1,256,512]{3,2,1,0:T(8,128)(2,1)}, f32[2,1,4,4,256,1]{5,4,3,2,1,0:T(8,128)}, f32[2,1,1,512]{3,2,1,0:T(1,128)}) custom-call(s32[1]{0:T(128)} %bitcast.1.place_ref, s32[1]{0:T(128)} %bitcast.31.len_ref, bf16[1,1024,512]{2,1,0:T(8,128)(2,1)} %get-tuple-element.297.q_i, ...), custom_call_target="tpu_custom_call" | custom-call | flops 469762048 | bytes 1441792 | tf_op jit(solution)/shard_map/attention_back/pallas_call | solution.py:243
  971.9 15.0 %back_project.3 = (bf16[256,2048]{1,0:T(8,128)(2,1)}, bf16[256,2048]{1,0:T(8,128)(2,1)}, bf16[256,2048]{1,0:T(8,128)(2,1)}, bf16[256,2048]{1,0:T(8,128)(2,1)}, bf16[1024,1536]{1,0:T(8,128)(2,1)}) custom-call(f32[1024,512]{1,0:T(8,128)} %bitcast.182, f32[1024,512]{1,0:T(8,128)} %bitcast.183, bf16[1024,512]{1,0:T(8,128)(2,1)} %bitcast.193, ...), custom_call_target="tpu_custom_call" | custom-call | flops 805306368 | bytes 1572864 | tf_op jit(solution)/shard_map/back_project/pallas_call | solution.py:313
  992.5 19.2 %qkv_weight_grad.1 = bf16[2048,1664]{1,0:T(8,128)(2,1)} custom-call(bf16[1024,2048]{1,0:T(8,128)(2,1)} %get-tuple-element.318.refs_0_, bf16[1024,2048]{1,0:T(8,128)(2,1)} %get-tuple-element.319.refs_1_, bf16[1024,1536]{1,0:T(8,128)(2,1)} %get-tuple-element.289.refs_2_, bf16[1024,1536]{1,0:T(8,128)(2,1)} %get-tuple-element.311.refs_3_, ...), custom_call_target="tpu_custom_call" | custom-call | flops 1610612736 | bytes 2686976 | tf_op jit(solution)/shard_map/qkv_weight_grad/pallas_call | solution.py:429
  1043.3 16.5 %collective-permute-done.46 = bf16[256,2048]{1,0:T(8,128)(2,1)S(1)} collective-permute-done((bf16[256,2048]{1,0:T(8,128)(2,1)S(1)}, bf16[256,2048]{1,0:T(8,128)(2,1)S(1)}, u32[]{:S(2)}, u32[]{:S(2)}) %collective-permute-start.46) | collective-permute-done | bytes 1048608 | tf_op jit(solution)/shard_map/ppermute | solution.py:741
  1075.2 14.3 %collective-permute-done.47 = bf16[256,2048]{1,0:T(8,128)(2,1)} collective-permute-done((bf16[256,2048]{1,0:T(8,128)(2,1)}, bf16[256,2048]{1,0:T(8,128)(2,1)}, u32[]{:S(2)}, u32[]{:S(2)}) %collective-permute-start.47) | collective-permute-done | bytes 1048608 | tf_op jit(solution)/shard_map/ppermute | solution.py:741
  1092.2 12.7 %all-to-all-done.5 = bf16[4,64,2176]{2,1,0:T(8,128)(2,1)S(1)} async-done(((bf16[4,64,2176]{2,1,0:T(8,128)(2,1)}), bf16[4,64,2176]{2,1,0:T(8,128)(2,1)S(1)}, u32[]{:S(2)}, u32[]{:S(2)}) %all-to-all-start.5) | async-done | bytes 1114144 | tf_op jit(solution)/shard_map/all_to_all | solution.py:760
  1115.6 15.5 %all-to-all-done.6 = bf16[4,64,1664]{2,1,0:T(8,128)(2,1)} async-done(((bf16[4,64,1664]{2,1,0:T(8,128)(2,1)}), bf16[4,64,1664]{2,1,0:T(8,128)(2,1)}, u32[]{:S(2)}, u32[]{:S(2)}) %all-to-all-start.6) | async-done | bytes 852000 | tf_op jit(solution)/shard_map/all_to_all | solution.py:760
  (403 shorter events, 311.9 us)
Async XLA Ops:
  7.2 162.6 %all-gather.4.cloned.1.call-start = ((), (), s32[]{:S(2)}) async-start(), calls=%async_computation.11 | async-start | bytes 17694720 | tf_op jit(solution)/shard_map/all_gather | solution.py:783
  67.3 357.6 %all-gather.6.cloned.1.call-start = ((), (), s32[]{:S(2)}) async-start(), calls=%async_computation.12 | async-start | bytes 37748736 | tf_op jit(solution)/shard_map/all_gather | solution.py:844
  68.6 25.6 %collective-permute-start = (bf16[256,2048]{1,0:T(8,128)(2,1)S(1)}, bf16[256,2048]{1,0:T(8,128)(2,1)S(1)}, u32[]{:S(2)}, u32[]{:S(2)}) collective-permute-start(bf16[256,2048]{1,0:T(8,128)(2,1)S(1)} %get-tuple-element.177.refs_0_.x_i), channel_id=1, source_target_pairs={{0,1},{1,2},{2,3},{3,0},{4,5},{5,6},{6,7},{7,4},{8,9},{9,10},{10,1... | collective-permute-start | bytes 3145736 | tf_op jit(solution)/shard_map/ppermute | solution.py:726
  122.2 394.3 %all-gather.8.cloned.1.call-start = ((), (), s32[]{:S(2)}) async-start(), calls=%async_computation.13 | async-start | bytes 18874368 | tf_op jit(solution)/shard_map/all_gather | solution.py:847
  284.3 44.9 %all-to-all-start.2 = ((bf16[4,256,512]{2,1,0:T(8,128)(2,1)}), bf16[4,256,512]{2,1,0:T(8,128)(2,1)S(1)}, u32[]{:S(2)}, u32[]{:S(2)}) async-start(bf16[4,256,512]{2,1,0:T(8,128)(2,1)} %bitcast.198), calls=%async_computation.2 | async-start | bytes 2097152 | tf_op jit(solution)/shard_map/all_to_all | solution.py:760
  287.9 484.3 %reduce-scatter.5.cloned.1.call-start = ((), (), s32[]{:S(2)}) async-start(), calls=%async_computation.14 | async-start | bytes 18874368 | tf_op jit(solution)/shard_map/reduce_scatter | solution.py:938
  287.9 35.9 %collective-permute-start.13 = (bf16[256,2048]{1,0:T(8,128)(2,1)S(1)}, bf16[256,2048]{1,0:T(8,128)(2,1)S(1)}, u32[]{:S(2)}, u32[]{:S(2)}) collective-permute-start(bf16[256,2048]{1,0:T(8,128)(2,1)S(1)} %collective-permute-done.12.refs_1_), channel_id=1, source_target_pairs={{0,1},{1,2},{2,3},{3,0},{4,5},{5,6},{6,7},{7,4},{8,9},{9,10},{10,1... | collective-permute-start | bytes 3145736 | tf_op jit(solution)/shard_map/ppermute | solution.py:726
  423.9 36.0 %collective-permute-start.18 = (bf16[256,2048]{1,0:T(8,128)(2,1)S(1)}, bf16[256,2048]{1,0:T(8,128)(2,1)S(1)}, u32[]{:S(2)}, u32[]{:S(2)}) collective-permute-start(bf16[256,2048]{1,0:T(8,128)(2,1)S(1)} %get-tuple-element.211.refs_0_.l_i), channel_id=1, source_target_pairs={{0,1},{1,2},{2,3},{3,0},{4,5},{5,6},{6,7},{7,4},{8,9},{9,10},{10,1... | collective-permute-start | bytes 3145736 | tf_op jit(solution)/shard_map/ppermute | solution.py:726
  423.9 45.8 %collective-permute-start.19 = (bf16[256,2048]{1,0:T(8,128)(2,1)S(1)}, bf16[256,2048]{1,0:T(8,128)(2,1)}, u32[]{:S(2)}, u32[]{:S(2)}) collective-permute-start(bf16[256,2048]{1,0:T(8,128)(2,1)S(1)} %get-tuple-element.212.refs_4_.l_i), channel_id=1, source_target_pairs={{0,1},{1,2},{2,3},{3,0},{4,5},{5,6},{6,7},{7,4},{8,9},{9,10},{10,1... | collective-permute-start | bytes 3145736 | tf_op jit(solution)/shard_map/ppermute | solution.py:726
  469.7 35.2 %collective-permute-start.20 = (bf16[256,2048]{1,0:T(8,128)(2,1)S(1)}, bf16[256,2048]{1,0:T(8,128)(2,1)S(1)}, u32[]{:S(2)}, u32[]{:S(2)}) collective-permute-start(bf16[256,2048]{1,0:T(8,128)(2,1)S(1)} %collective-permute-done.18.refs_1_), channel_id=1, source_target_pairs={{0,1},{1,2},{2,3},{3,0},{4,5},{5,6},{6,7},{7,4},{8,9},{9,10},{10,1... | collective-permute-start | bytes 3145736 | tf_op jit(solution)/shard_map/ppermute | solution.py:726
  469.7 45.8 %collective-permute-start.21 = (bf16[256,2048]{1,0:T(8,128)(2,1)}, bf16[256,2048]{1,0:T(8,128)(2,1)S(1)}, u32[]{:S(2)}, u32[]{:S(2)}) collective-permute-start(bf16[256,2048]{1,0:T(8,128)(2,1)} %collective-permute-done.19.refs_5_), channel_id=1, source_target_pairs={{0,1},{1,2},{2,3},{3,0},{4,5},{5,6},{6,7},{7,4},{8,9},{9,10},{10,1... | collective-permute-start | bytes 3145736 | tf_op jit(solution)/shard_map/ppermute | solution.py:726
  515.5 42.1 %collective-permute-start.23 = (bf16[256,2048]{1,0:T(8,128)(2,1)S(1)}, bf16[256,2048]{1,0:T(8,128)(2,1)S(1)}, u32[]{:S(2)}, u32[]{:S(2)}) collective-permute-start(bf16[256,2048]{1,0:T(8,128)(2,1)S(1)} %collective-permute-done.21.refs_6_), channel_id=1, source_target_pairs={{0,1},{1,2},{2,3},{3,0},{4,5},{5,6},{6,7},{7,4},{8,9},{9,10},{10,1... | collective-permute-start | bytes 3145736 | tf_op jit(solution)/shard_map/ppermute | solution.py:726
  515.5 45.6 %collective-permute-start.22 = (bf16[256,2048]{1,0:T(8,128)(2,1)S(1)}, bf16[256,2048]{1,0:T(8,128)(2,1)}, u32[]{:S(2)}, u32[]{:S(2)}) collective-permute-start(bf16[256,2048]{1,0:T(8,128)(2,1)S(1)} %collective-permute-done.20.refs_2_), channel_id=1, source_target_pairs={{0,1},{1,2},{2,3},{3,0},{4,5},{5,6},{6,7},{7,4},{8,9},{9,10},{10,1... | collective-permute-start | bytes 3145736 | tf_op jit(solution)/shard_map/ppermute | solution.py:726
  561.1 61.9 %collective-permute-start.25 = (bf16[256,2048]{1,0:T(8,128)(2,1)}, bf16[256,2048]{1,0:T(8,128)(2,1)}, u32[]{:S(2)}, u32[]{:S(2)}) collective-permute-start(bf16[256,2048]{1,0:T(8,128)(2,1)} %get-tuple-element.235), channel_id=1, source_target_pairs={{0,1},{1,2},{2,3},{3,0},{4,5},{5,6},{6,7},{7,4},{8,9},{9,10},{10,1... | collective-permute-start | bytes 3145736 | tf_op jit(solution)/shard_map/ppermute | solution.py:741
  561.1 61.9 %collective-permute-start.24 = (bf16[256,2048]{1,0:T(8,128)(2,1)}, bf16[256,2048]{1,0:T(8,128)(2,1)}, u32[]{:S(2)}, u32[]{:S(2)}) collective-permute-start(bf16[256,2048]{1,0:T(8,128)(2,1)} %get-tuple-element.232), channel_id=1, source_target_pairs={{0,1},{1,2},{2,3},{3,0},{4,5},{5,6},{6,7},{7,4},{8,9},{9,10},{10,1... | collective-permute-start | bytes 3145736 | tf_op jit(solution)/shard_map/ppermute | solution.py:741
  623.1 342.5 %reduce-scatter.7.cloned.1.call-start = ((), (), s32[]{:S(2)}) async-start(), calls=%async_computation.15 | async-start | bytes 37748736 | tf_op jit(solution)/shard_map/reduce_scatter | solution.py:959
  625.9 42.8 %collective-permute-start.27 = (bf16[256,2048]{1,0:T(8,128)(2,1)S(1)}, bf16[256,2048]{1,0:T(8,128)(2,1)S(1)}, u32[]{:S(2)}, u32[]{:S(2)}) collective-permute-start(bf16[256,2048]{1,0:T(8,128)(2,1)S(1)} %add_convert_fusion.10), channel_id=1, source_target_pairs={{0,1},{1,2},{2,3},{3,0},{4,5},{5,6},{6,7},{7,4},{8,9},{9,10},{10,1... | collective-permute-start | bytes 3145736 | tf_op jit(solution)/shard_map/ppermute | solution.py:741
  629.0 39.7 %collective-permute-start.26 = (bf16[256,2048]{1,0:T(8,128)(2,1)}, bf16[256,2048]{1,0:T(8,128)(2,1)S(1)}, u32[]{:S(2)}, u32[]{:S(2)}) collective-permute-start(bf16[256,2048]{1,0:T(8,128)(2,1)} %add_convert_fusion.11), channel_id=1, source_target_pairs={{0,1},{1,2},{2,3},{3,0},{4,5},{5,6},{6,7},{7,4},{8,9},{9,10},{10,1... | collective-permute-start | bytes 3145736 | tf_op jit(solution)/shard_map/ppermute | solution.py:741
  668.7 29.8 %collective-permute-start.28 = (bf16[256,2048]{1,0:T(8,128)(2,1)}, bf16[256,2048]{1,0:T(8,128)(2,1)S(1)}, u32[]{:S(2)}, u32[]{:S(2)}) collective-permute-start(bf16[256,2048]{1,0:T(8,128)(2,1)} %get-tuple-element.247), channel_id=1, source_target_pairs={{0,1},{1,2},{2,3},{3,0},{4,5},{5,6},{6,7},{7,4},{8,9},{9,10},{10,1... | collective-permute-start | bytes 3145736 | tf_op jit(solution)/shard_map/ppermute | solution.py:741
  698.8 31.2 %collective-permute-start.29 = (bf16[256,2048]{1,0:T(8,128)(2,1)S(1)}, bf16[256,2048]{1,0:T(8,128)(2,1)S(1)}, u32[]{:S(2)}, u32[]{:S(2)}) collective-permute-start(bf16[256,2048]{1,0:T(8,128)(2,1)S(1)} %add_convert_fusion.9), channel_id=1, source_target_pairs={{0,1},{1,2},{2,3},{3,0},{4,5},{5,6},{6,7},{7,4},{8,9},{9,10},{10,1... | collective-permute-start | bytes 3145736 | tf_op jit(solution)/shard_map/ppermute | solution.py:741
  731.7 39.4 %collective-permute-start.30 = (bf16[256,2048]{1,0:T(8,128)(2,1)S(1)}, bf16[256,2048]{1,0:T(8,128)(2,1)S(1)}, u32[]{:S(2)}, u32[]{:S(2)}) collective-permute-start(bf16[256,2048]{1,0:T(8,128)(2,1)S(1)} %add_convert_fusion.8), channel_id=1, source_target_pairs={{0,1},{1,2},{2,3},{3,0},{4,5},{5,6},{6,7},{7,4},{8,9},{9,10},{10,1... | collective-permute-start | bytes 3145736 | tf_op jit(solution)/shard_map/ppermute | solution.py:741
  732.9 39.2 %collective-permute-start.31 = (bf16[256,2048]{1,0:T(8,128)(2,1)S(1)}, bf16[256,2048]{1,0:T(8,128)(2,1)S(1)}, u32[]{:S(2)}, u32[]{:S(2)}) collective-permute-start(bf16[256,2048]{1,0:T(8,128)(2,1)S(1)} %add_convert_fusion.7), channel_id=1, source_target_pairs={{0,1},{1,2},{2,3},{3,0},{4,5},{5,6},{6,7},{7,4},{8,9},{9,10},{10,1... | collective-permute-start | bytes 3145736 | tf_op jit(solution)/shard_map/ppermute | solution.py:741
  794.1 39.9 %all-to-all-start.3 = ((bf16[4,256,512]{2,1,0:T(8,128)(2,1)}), bf16[4,256,512]{2,1,0:T(8,128)(2,1)S(1)}, u32[]{:S(2)}, u32[]{:S(2)}) async-start(bf16[4,256,512]{2,1,0:T(8,128)(2,1)} %get-tuple-element.267), calls=%async_computation.4 | async-start | bytes 2097152 | tf_op jit(solution)/shard_map/all_to_all | solution.py:760
  800.4 28.3 %collective-permute-start.33 = (bf16[256,2048]{1,0:T(8,128)(2,1)S(1)}, bf16[256,2048]{1,0:T(8,128)(2,1)}, u32[]{:S(2)}, u32[]{:S(2)}) collective-permute-start(bf16[256,2048]{1,0:T(8,128)(2,1)S(1)} %add_convert_fusion.6), channel_id=1, source_target_pairs={{0,1},{1,2},{2,3},{3,0},{4,5},{5,6},{6,7},{7,4},{8,9},{9,10},{10,1... | collective-permute-start | bytes 3145736 | tf_op jit(solution)/shard_map/ppermute | solution.py:741
  837.3 29.5 %collective-permute-start.34 = (bf16[256,2048]{1,0:T(8,128)(2,1)}, bf16[256,2048]{1,0:T(8,128)(2,1)}, u32[]{:S(2)}, u32[]{:S(2)}) collective-permute-start(bf16[256,2048]{1,0:T(8,128)(2,1)} %add_convert_fusion.5), channel_id=1, source_target_pairs={{0,1},{1,2},{2,3},{3,0},{4,5},{5,6},{6,7},{7,4},{8,9},{9,10},{10,1... | collective-permute-start | bytes 3145736 | tf_op jit(solution)/shard_map/ppermute | solution.py:741
  892.7 33.2 %all-to-all-start.4 = ((bf16[4,256,512]{2,1,0:T(8,128)(2,1)}), bf16[4,256,512]{2,1,0:T(8,128)(2,1)S(1)}, u32[]{:S(2)}, u32[]{:S(2)}) async-start(bf16[4,256,512]{2,1,0:T(8,128)(2,1)} %get-tuple-element.288), calls=%async_computation.5 | async-start | bytes 2097152 | tf_op jit(solution)/shard_map/all_to_all | solution.py:760
  896.2 130.1 %reduce-scatter.9.cloned.1.call-start = ((), (), s32[]{:S(2)}) async-start(), calls=%async_computation.16 | async-start | bytes 10027008 | tf_op jit(solution)/shard_map/reduce_scatter | solution.py:983
  926.9 178.0 %reduce-scatter.11.cloned.1.call-start = ((), (), s32[]{:S(2)}) async-start(), calls=%async_computation.17 | async-start | bytes 7667712 | tf_op jit(solution)/shard_map/reduce_scatter | solution.py:1016
  926.9 31.0 %collective-permute-start.39 = (bf16[256,2048]{1,0:T(8,128)(2,1)}, bf16[256,2048]{1,0:T(8,128)(2,1)}, u32[]{:S(2)}, u32[]{:S(2)}) collective-permute-start(bf16[256,2048]{1,0:T(8,128)(2,1)} %get-tuple-element.295), channel_id=1, source_target_pairs={{0,1},{1,2},{2,3},{3,0},{4,5},{5,6},{6,7},{7,4},{8,9},{9,10},{10,1... | collective-permute-start | bytes 3145736 | tf_op jit(solution)/shard_map/ppermute | solution.py:741
  1061.2 28.3 %collective-permute-start.47 = (bf16[256,2048]{1,0:T(8,128)(2,1)}, bf16[256,2048]{1,0:T(8,128)(2,1)}, u32[]{:S(2)}, u32[]{:S(2)}) collective-permute-start(bf16[256,2048]{1,0:T(8,128)(2,1)} %add_convert_fusion), channel_id=1, source_target_pairs={{0,1},{1,2},{2,3},{3,0},{4,5},{5,6},{6,7},{7,4},{8,9},{9,10},{10,1... | collective-permute-start | bytes 3145736 | tf_op jit(solution)/shard_map/ppermute | solution.py:741
  1062.7 42.2 %all-to-all-start.5 = ((bf16[4,64,2176]{2,1,0:T(8,128)(2,1)}), bf16[4,64,2176]{2,1,0:T(8,128)(2,1)S(1)}, u32[]{:S(2)}, u32[]{:S(2)}) async-start(bf16[4,64,2176]{2,1,0:T(8,128)(2,1)} %bitcast.191), calls=%async_computation.8 | async-start | bytes 2228224 | tf_op jit(solution)/shard_map/all_to_all | solution.py:760
  1104.9 26.3 %all-to-all-start.6 = ((bf16[4,64,1664]{2,1,0:T(8,128)(2,1)}), bf16[4,64,1664]{2,1,0:T(8,128)(2,1)}, u32[]{:S(2)}, u32[]{:S(2)}) async-start(bf16[4,64,1664]{2,1,0:T(8,128)(2,1)} %bitcast.199), calls=%async_computation.10 | async-start | bytes 1703936 | tf_op jit(solution)/shard_map/all_to_all | solution.py:760
  (104 other events, 1762.4 us)
Sparse Core Ops, SparseCore 0:
  67.4 84.5 all-gather.3
  154.6 160.7 all-gather.5
  317.3 93.1 all-gather.7
  623.2 116.6 reduce-scatter.4
  743.3 205.2 reduce-scatter.6
  952.4 73.8 reduce-scatter.8
  1030.1 64.2 reduce-scatter.10
